TPU v7x, 256 devices: a whole 4x4x8 slice. The times are simulated.
256 devices in a mesh: seq: 32 (over z, y), head: 2 (over core), dp: 4 (over x).
Axes of the slice: x: 4, y: 4, z: 8, core: 2. Of those that a mesh axis runs over, the one named last changes fastest.
Arguments:
- queries: bfloat16 [90112, 2048], P(('dp', 'seq'), 'head'), parts along dimension 0, may hold values from -96 to 96
- out_grad: bfloat16 [90112, 2048], P(('dp', 'seq'), 'head'), parts along dimension 0, may hold values from -16 to 16
- encodings: bfloat16 [1280, 16, 2048], P(('dp', 'seq'), None, 'head'), parts along dimension 0, may hold values from -6 to 6
- key_weight: bfloat16 [2048, 2048], P(None, 'head'), may hold values from -0.125 to 0.125
- value_weight: bfloat16 [2048, 2048], P(None, 'head'), may hold values from -0.125 to 0.125
- neighbours: int32 [1408, 2], P(('dp', 'seq')), parts along dimension 0, may hold values from 0 to 319, as said below
Outputs:
- query_grad: bfloat16 [90112, 2048], P(('dp', 'seq'), 'head'), parts along dimension 0
- encoding_grad: bfloat16 [1280, 16, 2048], P(('dp', 'seq'), None, 'head'), parts along dimension 0
There are 4 independent parts, one for each index of `dp`. A program takes and returns all parts, laid end to end along the dimension named above; an argument that names none is the same for every part. Nothing has to cross between parts.
Inputs may be any that keep to these rules, and one draw needn't show every extreme that they name: `neighbours`: row r of encodings is held by index r // 10 of seq. In each aligned block of 11 spans, at most 2 of the 22 ids belong to one holder, and some holder has exactly 2. A span's two ids differ.
All inputs are finite; a program needn't handle non-finite values.
Results may differ from a plain program's by a relative error of at most 0.011.
Values may be sent and summed in bfloat16 or wider, within the bound.
No kernel may reach another device: no remote copies, remote signals or barrier semaphores. Data moves between devices by JAX's collectives and lax.ppermute only.
A program may use at most 64 MiB of HBM per device.

v0:
```python
import math

import jax
import jax.numpy as jnp
from jax import lax
from jax.sharding import PartitionSpec as P

D = 2048
HEADS = 16


def slot_ranks(owner_ids):
    count = owner_ids.shape[-1]
    same_owner = owner_ids[..., :, None] == owner_ids[..., None, :]
    positions = jnp.arange(count, dtype=jnp.int32)
    earlier = positions[None, :] < positions[:, None]
    return jnp.sum(same_owner & earlier, axis=-1)


def on_device(queries, out_grad, encodings, key_weight, value_weight, neighbours):
    seq_count = lax.axis_size("seq")
    seq_index = lax.axis_index("seq")
    spans_here = neighbours.shape[0]
    ref_count = 2 * spans_here
    rows_here, neighbour_len, half_width = encodings.shape
    full_width = key_weight.shape[0]
    tok_rows = queries.shape[0]
    span_len = tok_rows // spans_here
    head_size = D // HEADS
    heads_here = half_width // head_size
    scaling = 1.0 / math.sqrt(head_size)
    capacity = max(2, ref_count // seq_count)
    slot_count = seq_count * capacity
    all_lists = lax.all_gather(neighbours, "seq", axis=0, tiled=True).reshape(seq_count, ref_count)
    owner_table = all_lists // rows_here
    local_table = all_lists % rows_here
    rank_table = slot_ranks(owner_table)
    own_ids = neighbours.reshape(ref_count)
    own_owner = own_ids // rows_here
    position = own_owner * capacity + slot_ranks(own_owner)
    slot_ids = jnp.arange(capacity, dtype=jnp.int32)
    chosen = (owner_table == seq_index)[:, None, :] & (
        rank_table[:, None, :] == slot_ids[None, :, None]
    )
    filled = jnp.any(chosen, axis=-1)
    slot_row = jnp.sum(jnp.where(chosen, local_table[:, None, :], 0), axis=-1)
    select = filled[..., None] & (
        slot_row[..., None] == jnp.arange(rows_here, dtype=jnp.int32)[None, None, :]
    )
    select = select.astype(jnp.bfloat16).reshape(slot_count, rows_here)
    flat_enc = encodings.reshape(rows_here, neighbour_len * half_width)
    outgoing = jnp.dot(select, flat_enc, preferred_element_type=jnp.float32).astype(jnp.bfloat16)
    outgoing = outgoing.reshape(seq_count, capacity, neighbour_len, half_width)
    arrived = lax.all_to_all(outgoing, "seq", split_axis=0, concat_axis=0, tiled=True)
    flat_arrived = arrived.reshape(slot_count, neighbour_len, half_width)
    whole = lax.all_gather(flat_arrived, "head", axis=2, tiled=True)
    full_rows = jnp.take(whole, position, axis=0)
    flat_rows = full_rows.reshape(ref_count * neighbour_len, full_width)
    keys = jnp.dot(flat_rows, key_weight, preferred_element_type=jnp.float32).astype(jnp.bfloat16)
    values = jnp.dot(flat_rows, value_weight, preferred_element_type=jnp.float32).astype(
        jnp.bfloat16
    )
    query_heads = queries.reshape(spans_here, span_len, heads_here, head_size)
    grad_heads = out_grad.reshape(spans_here, span_len, heads_here, head_size)
    key_heads = keys.reshape(spans_here, 2 * neighbour_len, heads_here, head_size)
    value_heads = values.reshape(spans_here, 2 * neighbour_len, heads_here, head_size)
    scores = (
        jnp.einsum("cthd,cuhd->chtu", query_heads, key_heads, preferred_element_type=jnp.float32)
        * scaling
    )
    scores = scores - jnp.max(scores, axis=-1, keepdims=True)
    raised = jnp.exp(scores)
    probs = raised / jnp.sum(raised, axis=-1, keepdims=True)
    probs_b = probs.astype(jnp.bfloat16)
    attended = jnp.einsum(
        "chtu,cuhd->cthd", probs_b, value_heads, preferred_element_type=jnp.float32
    )
    delta = jnp.transpose(jnp.sum(grad_heads.astype(jnp.float32) * attended, axis=-1), (0, 2, 1))
    dprobs = jnp.einsum(
        "cthd,cuhd->chtu", grad_heads, value_heads, preferred_element_type=jnp.float32
    )
    dscores = (probs * (dprobs - delta[..., None])).astype(jnp.bfloat16)
    query_grad = (
        jnp.einsum("chtu,cuhd->cthd", dscores, key_heads, preferred_element_type=jnp.float32)
        * scaling
    )
    query_grad = query_grad.astype(jnp.bfloat16).reshape(tok_rows, half_width)
    key_grad = (
        jnp.einsum("chtu,cthd->cuhd", dscores, query_heads, preferred_element_type=jnp.float32)
        * scaling
    )
    key_grad = key_grad.astype(jnp.bfloat16).reshape(ref_count * neighbour_len, half_width)
    value_grad = jnp.einsum(
        "chtu,cthd->cuhd", probs_b, grad_heads, preferred_element_type=jnp.float32
    )
    value_grad = value_grad.astype(jnp.bfloat16).reshape(ref_count * neighbour_len, half_width)
    contract = (((1,), (1,)), ((), ()))
    partial_value = lax.dot_general(
        key_grad, key_weight, contract, preferred_element_type=jnp.float32
    )
    partial_value = partial_value + lax.dot_general(
        value_grad, value_weight, contract, preferred_element_type=jnp.float32
    )
    summed = lax.psum_scatter(
        partial_value.reshape(ref_count, neighbour_len, full_width),
        "head",
        scatter_dimension=2,
        tiled=True,
    )
    ref_grad = summed.astype(jnp.bfloat16)
    returning = (
        jnp.zeros((slot_count, neighbour_len, half_width), jnp.bfloat16).at[position].set(ref_grad)
    )
    returning = returning.reshape(seq_count, capacity, neighbour_len, half_width)
    came_back = lax.all_to_all(returning, "seq", split_axis=0, concat_axis=0, tiled=True).reshape(
        slot_count, neighbour_len * half_width
    )
    encoding_grad = lax.dot_general(
        select, came_back, (((0,), (0,)), ((), ())), preferred_element_type=jnp.float32
    )
    encoding_grad = encoding_grad.astype(jnp.bfloat16).reshape(rows_here, neighbour_len, half_width)
    return (query_grad, encoding_grad)


def solution(mesh):
    return jax.shard_map(
        on_device,
        mesh=mesh,
        in_specs=(
            P(("dp", "seq"), "head"),
            P(("dp", "seq"), "head"),
            P(("dp", "seq"), None, "head"),
            P(None, "head"),
            P(None, "head"),
            P(("dp", "seq"), None),
        ),
        out_specs=(P(("dp", "seq"), "head"), P(("dp", "seq"), None, "head")),
        check_vma=False,
    )
```

profile of v0, /device:TPU:2, one launch (start us, length us, event | category | flops | bytes accessed | tf_op | source)
XLA Modules:
  0.0 241.9 jit_solution(4702923652695932510)
XLA Ops:
  7.2 46.3 %all-gather = s32[32,11,2]{1,2,0:T(2,128)S(1)} all-gather(s32[1,11,2]{1,2,0:T(2,128)} %bitcast.115), channel_id=1, replica_groups=mesh['seq'=32,'head'=2,'dp'=4] {'seq'}, dimensions={0}, use_global_device_ids=true | all-gather | bytes 2904 | tf_op jit(solution)/shard_map/all_gather | solution.py:34
  56.5 1.2 copy.110
  57.7 46.8 %all_to_all.10 = bf16[32,2,16,1024]{3,2,1,0:T(8,128)(2,1)} all-to-all(bf16[32,2,16,1024]{3,2,1,0:T(8,128)(2,1)S(1)} %bitcast.94), channel_id=1, replica_groups=mesh['seq'=32,'head'=2,'dp'=4] {'seq'}, dimensions={0} | all-to-all | bytes 4194304 | tf_op jit(solution)/shard_map/all_to_all | solution.py:54
  107.6 1.5 copy.114
  109.1 11.6 %all-gather.3.cloned.1.call-done = bf16[64,16,2048]{2,1,0:T(8,128)(2,1)} async-done(((bf16[64,16,1024]{2,1,0:T(8,128)(2,1)}), bf16[64,16,2048]{2,1,0:T(8,128)(2,1)}) %all-gather.3.cloned.1.call-update) | async-done | bytes 4194320 | tf_op jit(solution)/shard_map/all_gather | solution.py:56
  120.7 2.8 %gather_fusion = bf16[22,16,2048]{2,1,0:T(8,128)(2,1)S(1)} fusion(bf16[64,16,2048]{2,1,0:T(8,128)(2,1)} %all-gather.3.cloned.1.call-done, s32[1024]{0:T(1024)S(1)} %pad_clamp_fusion), kind=kCustom, calls=%fused_computation | custom fusion | bytes 2883672 | tf_op jit(solution)/shard_map/jit(_take)/gather | solution.py:57
  123.8 4.4 %fusion.10 = bf16[44,8,8,128]{3,1,2,0:T(8,128)(2,1)S(1)} fusion(bf16[352,2048]{1,0:T(8,128)(2,1)S(1)} %bitcast_select_fusion, bf16[2048,1024]{1,0:T(8,128)(2,1)} %param.9), kind=kOutput, calls=%fused_computation.25 | convolution fusion | flops 1476755456 | bytes 6356992 | tf_op jit(solution)/shard_map/dot_general | solution.py:59
  128.4 2.0 fusion.41
  130.4 2.4 %fusion.13 = bf16[11,32,8,128]{3,1,2,0:T(8,128)(2,1)S(1)} fusion(bf16[11,64,8,128]{3,2,1,0:T(8,128)(2,1)} %bitcast.106, f32[11,8,64,32]{2,3,1,0:T(8,128)} %get-tuple-element.7, f32[11,8,64]{2,1,0:T(8,128)S(1)} %get-tuple-element.6), kind=kOutput, calls=%fused_computation.28 | convolution fusion | flops 46858240 | bytes 2906112 | tf_op jit(solution)/shard_map/chtu,cthd->cuhd/dot_general | solution.py:93
  134.3 1.7 fusion.11
  136.2 1.2 copy-done.2
  137.4 1.3 fusion.1
  140.3 1.4 copy-done.6
  141.7 1.7 fusion.20
  143.4 3.3 %convolution_add_fusion = f32[352,2048]{1,0:T(8,128)} fusion(f32[352,2048]{1,0:T(8,128)S(1)} %fusion.20, bf16[2048,1024]{1,0:T(8,128)(2,1)S(1)} %copy-done.7, bf16[44,8,8,128]{3,2,1,0:T(8,128)(2,1)S(1)} %bitcast.111), kind=kOutput, calls=%fused_computation.8 | convolution fusion | flops 1477115904 | bytes 10682368 | tf_op jit(solution)/shard_map/dot_general | solution.py:101
  146.8 17.5 %reduce-scatter.2.cloned.1.call-done = f32[22,16,1024]{2,1,0:T(8,128)} async-done(((f32[22,16,2048]{2,1,0:T(8,128)}), f32[22,16,1024]{2,1,0:T(8,128)}) %reduce-scatter.2.cloned.1.call-update) | async-done | bytes 1441808 | tf_op jit(solution)/shard_map/reduce_scatter | solution.py:104
  164.3 1.4 convert_element_type.63
  165.7 1.6 broadcast_in_dim.34
  167.4 4.6 %scatter_fusion = bf16[64,16,1024]{2,1,0:T(8,128)(2,1)} fusion(bf16[64,16,1024]{2,1,0:T(8,128)(2,1)} %broadcast_in_dim.34, s32[22]{0:T(128)S(1)} %fusion.38, bf16[22,16,1024]{2,1,0:T(8,128)(2,1)S(1)} %convert_element_type.63), kind=kCustom, calls=%fused_computation.1 | custom fusion | bytes 2162776 | tf_op jit(solution)/shard_map/scatter | solution.py:112
  171.9 9.9 %all-to-all-start.1 = ((bf16[32,2,16,1024]{3,2,1,0:T(8,128)(2,1)}), bf16[32,2,16,1024]{3,2,1,0:T(8,128)(2,1)S(1)}, u32[]{:S(2)}, u32[]{:S(2)}) async-start(bf16[32,2,16,1024]{3,2,1,0:T(8,128)(2,1)} %bitcast.13), calls=%async_computation.2 | async-start | bytes 4194304 | tf_op jit(solution)/shard_map/all_to_all | solution.py:115
  182.5 1.1 copy.103
  183.6 1.5 copy.150
  185.1 47.2 %all-to-all-done.1 = bf16[32,2,16,1024]{3,2,1,0:T(8,128)(2,1)S(1)} async-done(((bf16[32,2,16,1024]{3,2,1,0:T(8,128)(2,1)}), bf16[32,2,16,1024]{3,2,1,0:T(8,128)(2,1)S(1)}, u32[]{:S(2)}, u32[]{:S(2)}) %all-to-all-start.1) | async-done | bytes 2097184 | tf_op jit(solution)/shard_map/all_to_all | solution.py:115
  232.3 1.2 copy.118
  (66 shorter events, 11.9 us)
Async XLA Ops:
  7.2 113.5 %all-gather.3.cloned.1.call-start = ((), (), s32[]{:S(2)}) async-start(), calls=%async_computation.3 | async-start | bytes 6291456 | tf_op jit(solution)/shard_map/all_gather | solution.py:56
  104.5 0.7 copy-start.5
  104.5 1.6 copy-start
  104.6 59.7 %reduce-scatter.2.cloned.1.call-start = ((), (), s32[]{:S(2)}) async-start(), calls=%async_computation.4 | async-start | bytes 4325376 | tf_op jit(solution)/shard_map/reduce_scatter | solution.py:104
  106.2 1.4 copy-start.1
  123.8 4.4 %copy-start.3 = (bf16[352,2048]{1,0:T(8,128)(2,1)}, bf16[352,2048]{1,0:T(8,128)(2,1)S(1)}, u32[]{:S(2)}) copy-start(bf16[352,2048]{1,0:T(8,128)(2,1)S(1)} %bitcast_select_fusion) | copy-start | bytes 4325380
  130.4 3.1 %copy-start.7 = (bf16[2048,1024]{1,0:T(8,128)(2,1)S(1)}, bf16[2048,1024]{1,0:T(8,128)(2,1)}, u32[]{:S(2)}) copy-start(bf16[2048,1024]{1,0:T(8,128)(2,1)} %param.10) | copy-start | bytes 12582916
  132.8 1.5 copy-start.4
  134.3 1.9 copy-start.8
  136.0 1.4 copy-start.2
  139.5 2.2 copy-start.6
  171.9 60.4 %all-to-all-start.1 = ((bf16[32,2,16,1024]{3,2,1,0:T(8,128)(2,1)}), bf16[32,2,16,1024]{3,2,1,0:T(8,128)(2,1)S(1)}, u32[]{:S(2)}, u32[]{:S(2)}) async-start(bf16[32,2,16,1024]{3,2,1,0:T(8,128)(2,1)} %bitcast.13), calls=%async_computation.2 | async-start | bytes 4194304 | tf_op jit(solution)/shard_map/all_to_all | solution.py:115
Sparse Core Ops, SparseCore 0:
  104.7 15.9 all-gather.2
  146.9 17.3 reduce-scatter.1
where the time goes:
time: 243 us; the launch traced here: 242 us
  blocking collectives  93.1 us (38%)
  waiting for transfers between devices  76.3 us (31%)
  local copies, waits for them, and re-layouts  25.7 us (11%)
  matrix products  20 us (8%)
  between operations  14.4 us (6%)
  starting transfers between devices  10.1 us (4%)
    all_to_all x1, waiting for transfers between devices, on_device(): lax.all_to_all(returning, 'seq', split_axis=0, concat_axis=0, tiled=True)  47.2 us
    all_to_all x1, blocking collectives, on_device(): lax.all_to_all(outgoing, 'seq', split_axis=0, concat_axis=0, tiled=True)  46.8 us
    all_gather x1, blocking collectives, on_device(): lax.all_gather(neighbours, 'seq', axis=0, tiled=True)  46.3 us
    reduce_scatter x1, waiting for transfers between devices, on_device(): lax.psum_scatter(partial_value.reshape(ref_count, neighbour_len, full_wid...  17.5 us
    unnamed x28, local copies, waits for them, and re-layouts  12.9 us
    all_gather x1, waiting for transfers between devices, on_device(): whole = lax.all_gather(flat_arrived, 'head', axis=2, tiled=True)  11.6 us
    all_to_all x1, starting transfers between devices, on_device(): lax.all_to_all(returning, 'seq', split_axis=0, concat_axis=0, tiled=True)  9.86 us
  transfers between devices with their start and end apart: 3, of which 3 were waited for; matrix products, arithmetic and copies ran while one was open for 3% of the time, Pallas kernels for 0%

commit v1 on v0

v1 whole, which is shorter than its diff:
```python
import math

import jax
import jax.numpy as jnp
from jax import lax
from jax.experimental import pallas as pl
from jax.experimental.pallas import tpu as pltpu
from jax.sharding import PartitionSpec as P


D = 2048
HEADS = 16
NY = 4
CAP = 2


SMEM = pl.BlockSpec(memory_space=pltpu.SMEM)
VMEM = pl.BlockSpec(memory_space=pltpu.VMEM)
ANY = pl.BlockSpec(memory_space=pl.ANY)
BF = jnp.bfloat16
SMALL = pltpu.CompilerParams(vmem_limit_bytes=8 << 20)
F32 = jnp.float32

OUT = ((0, 1, 2), (3, 4))


def planes_of(step, nz):
    if step == 0 or 2 * step == nz:
        return (step,)
    return (step, nz - step)


def slots_of(phase, nz):
    return [(d, s) for step in phase for d in planes_of(step, nz) for s in range(CAP)]


def ring(seq, dz, dy):
    nz = seq // NY
    pairs = []
    for z in range(nz):
        for y in range(NY):
            pairs.append((z * NY + y, ((z + dz) % nz) * NY + (y + dy) % NY))
    return pairs


def pick_rows(table, place, blocks, phase, nz):
    slots = slots_of(phase, nz)
    flat, where = [], {}
    for d, pieces in blocks.items():
        where[d] = []
        start = 0
        for a in pieces:
            where[d].append((len(flat), start, a.shape[0]))
            start += a.shape[0]
            flat.append(a)
    tail = flat[0].shape[1:]

    def body(t_ref, p_ref, *refs):
        ins, outs = refs[: len(flat)], refs[len(flat) :]
        for j in range(NY):
            for k, (d, s) in enumerate(slots):
                row = jnp.maximum(t_ref[j, (p_ref[0] + d) % nz * CAP + s], 0)
                if len(where[d]) == 1:
                    outs[j][k] = ins[where[d][0][0]][row]
                    continue
                for n, start, size in where[d]:

                    @pl.when((row >= start) & (row < start + size))
                    def _():
                        outs[j][k] = ins[n][jnp.clip(row - start, 0, size - 1)]

    return pl.pallas_call(
        body,
        in_specs=[SMEM, SMEM] + [VMEM] * len(flat),
        out_specs=[VMEM] * NY,
        out_shape=[jax.ShapeDtypeStruct((len(slots),) + tail, BF)] * NY,
        name="pick",
        compiler_params=SMALL,
    )(table, place, *flat)


def compact(ref_of, place, groups, nz, ref_count):
    flat = [a for group in groups for a in group]
    tail = flat[0].shape[1:]

    def body(r_ref, p_ref, *refs):
        ins, out = refs[:-1], refs[-1]
        for n, phase in enumerate(OUT):
            for j in range(NY):
                for k, (d, s) in enumerate(slots_of(phase, nz)):
                    r = r_ref[j, (p_ref[0] + d) % nz * CAP + s]

                    @pl.when(r >= 0)
                    def _():
                        out[jnp.maximum(r, 0)] = ins[n * NY + j][k]

    return pl.pallas_call(
        body,
        in_specs=[SMEM, SMEM] + [VMEM] * len(flat),
        out_specs=VMEM,
        out_shape=jax.ShapeDtypeStruct((ref_count,) + tail, BF),
        name="compact",
        compiler_params=SMALL,
    )(ref_of, place, *flat)


def spread(ref_of, place, own, other, seq):
    tail = own.shape[1:]
    nz = seq // NY

    def body(r_ref, p_ref, own_ref, other_ref, out):
        for j in range(NY):
            for d in range(nz):
                holder = d * NY + (p_ref[1] + NY - j) % NY
                for s in range(CAP):
                    r = r_ref[j, d * CAP + s]

                    @pl.when(r >= 0)
                    def _():
                        at = jnp.maximum(r, 0)
                        total = own_ref[at] + other_ref[at].astype(F32)
                        out[holder * CAP + s] = total.astype(BF)

    return pl.pallas_call(
        body,
        in_specs=[SMEM, SMEM, VMEM, VMEM],
        out_specs=VMEM,
        out_shape=jax.ShapeDtypeStruct((seq * CAP,) + tail, BF),
        name="spread",
        compiler_params=SMALL,
    )(ref_of, place, own, other)


def combine(named, place, came, rows_here):
    slots = came.shape[0]
    tail = came.shape[1:]

    def body(n_ref, p_ref, in_ref, out, acc):
        def clear(r, carry):
            acc[r] = jnp.zeros(tail, F32)
            return carry

        def add(k, carry):
            reader = k // CAP
            j = (reader % NY + NY - p_ref[1]) % NY
            row = n_ref[j, reader // NY * CAP + k % CAP]

            @pl.when(row >= 0)
            def _():
                at = jnp.maximum(row, 0)
                acc[at] = acc[at] + in_ref[k].astype(F32)

            return carry

        def drain(r, carry):
            out[r] = acc[r].astype(BF)
            return carry

        lax.fori_loop(0, rows_here, clear, 0)
        lax.fori_loop(0, slots, add, 0)
        lax.fori_loop(0, rows_here, drain, 0)

    return pl.pallas_call(
        body,
        in_specs=[SMEM, SMEM, VMEM],
        out_specs=VMEM,
        out_shape=jax.ShapeDtypeStruct((rows_here,) + tail, BF),
        scratch_shapes=[pltpu.VMEM((rows_here,) + tail, F32)],
        name="combine",
        compiler_params=SMALL,
    )(named, place, came)


def fetch(*arrays):
    count = len(arrays)

    def body(*refs):
        sem = refs[-1]
        copies = [
            pltpu.make_async_copy(refs[n], refs[count + n], sem.at[n]) for n in range(count)
        ]
        for copy in copies:
            copy.start()
        for copy in copies:
            copy.wait()

    return pl.pallas_call(
        body,
        in_specs=[pl.BlockSpec(memory_space=pltpu.HBM)] * count,
        out_specs=[VMEM] * count,
        out_shape=[pltpu.VMEM(a.shape, a.dtype) for a in arrays],
        scratch_shapes=[pltpu.SemaphoreType.DMA((count,))],
        compiler_params=SMALL,
        name="fetch",
    )(*arrays)


def core_step(place, own, other, key_weight, value_weight, queries, out_grad, spans, head_size):
    rows, half = own.shape
    tok = queries.shape[0] // spans
    per = rows // spans
    heads = half // head_size
    scaling = 1.0 / math.sqrt(head_size)
    nt = (((1,), (1,)), ((), ()))
    tn = (((0,), (0,)), ((), ()))
    cols = [slice(n * head_size, (n + 1) * head_size) for n in range(heads)]

    def body(
        p_ref, own_ref, oth_ref, wk_ref, wv_ref, q_ref, g_ref, dq_hbm, pown_ref, poth_ref,
        dq_ref, k_ref, v_ref, dk_ref, dv_ref, sem,
    ):
        mine = pl.ds(pl.multiple_of(p_ref[2] * half, half), half)
        theirs = pl.ds(pl.multiple_of((1 - p_ref[2]) * half, half), half)
        for w_ref, out in ((wk_ref, k_ref), (wv_ref, v_ref)):
            total = jnp.dot(own_ref[...], w_ref[mine, :], preferred_element_type=F32)
            total += jnp.dot(oth_ref[...], w_ref[theirs, :], preferred_element_type=F32)
            out[...] = total.astype(BF)

        def span(u, carry):
            here = pl.ds(pl.multiple_of(u * per, per), per)
            there = pl.ds(pl.multiple_of(u * tok, tok), tok)
            q = [q_ref[there, c] for c in cols]
            g = [g_ref[there, c] for c in cols]
            k = [k_ref[here, c] for c in cols]
            v = [v_ref[here, c] for c in cols]
            scores = [
                lax.dot_general(a, b, nt, preferred_element_type=F32) for a, b in zip(k, q)
            ]
            dprobs = [
                lax.dot_general(a, b, nt, preferred_element_type=F32) for a, b in zip(v, g)
            ]
            probs_b, ds = [], []
            for sc, dp in zip(scores, dprobs):
                sc = sc * scaling
                raised = jnp.exp(sc - jnp.max(sc, axis=0, keepdims=True))
                probs = raised / jnp.sum(raised, axis=0, keepdims=True)
                pb = probs.astype(BF)
                delta = jnp.sum(pb.astype(F32) * dp, axis=0, keepdims=True)
                probs_b.append(pb)
                ds.append((probs * (dp - delta)).astype(BF))
            for n, c in enumerate(cols):
                dk = jnp.dot(ds[n], q[n], preferred_element_type=F32) * scaling
                dv = jnp.dot(probs_b[n], g[n], preferred_element_type=F32)
                dq = lax.dot_general(ds[n], k[n], tn, preferred_element_type=F32) * scaling
                dk_ref[here, c] = dk.astype(BF)
                dv_ref[here, c] = dv.astype(BF)
                dq_ref[there, c] = dq.astype(BF)
            return carry

        lax.fori_loop(0, spans, span, 0)
        store = pltpu.make_async_copy(dq_ref, dq_hbm, sem.at[0])
        store.start()
        for at, out in ((theirs, poth_ref), (mine, pown_ref)):
            total = lax.dot_general(dk_ref[...], wk_ref[at, :], nt, preferred_element_type=F32)
            total += lax.dot_general(dv_ref[...], wv_ref[at, :], nt, preferred_element_type=F32)
            out[...] = total.astype(out.dtype)
        store.wait()

    return pl.pallas_call(
        body,
        in_specs=[SMEM, VMEM, VMEM, VMEM, VMEM, VMEM, VMEM],
        out_specs=[ANY, VMEM, VMEM],
        compiler_params=pltpu.CompilerParams(vmem_limit_bytes=16 << 20),
        out_shape=[
            jax.ShapeDtypeStruct(queries.shape, BF),
            jax.ShapeDtypeStruct((rows, half), F32),
            jax.ShapeDtypeStruct((rows, half), BF),
        ],
        scratch_shapes=[pltpu.VMEM(queries.shape, BF)]
        + [pltpu.VMEM((rows, half), BF)] * 4
        + [pltpu.SemaphoreType.DMA((1,))],
        name="core_step",
    )(place, own, other, key_weight, value_weight, queries, out_grad)


def slot_tables(ids, y0, nz, rows_here):
    count = ids.shape[1]
    owner = ids // rows_here
    local = ids % rows_here
    plane = owner // NY
    column = owner % NY
    refs = jnp.arange(count, dtype=jnp.int32)
    same = (owner[:, :, None] == owner[:, None, :]) & (refs[None, None, :] < refs[None, :, None])
    rank = jnp.sum(same.astype(jnp.int32), axis=2)
    code = plane * CAP + rank
    slots = jnp.arange(nz * CAP, dtype=jnp.int32)
    hit = (slots[None, :, None] == code[:, None, :]) & (column == y0)[:, None, :]
    table = jnp.sum(jnp.where(hit, local[:, None, :] + 1, 0), axis=2) - 1
    back = (y0 - column[0]) % NY
    sides = jnp.arange(NY, dtype=jnp.int32)
    mine = (slots[None, :, None] == code[0][None, None, :]) & (
        sides[:, None, None] == back[None, None, :]
    )
    ref_of = jnp.sum(jnp.where(mine, refs[None, None, :] + 1, 0), axis=2) - 1
    return table, ref_of


def whole_step(queries, out_grad, encodings, key_weight, value_weight, neighbours):
    seq = lax.axis_size("seq")
    nz = seq // NY
    far = nz // 2
    index = lax.axis_index("seq")
    head = lax.axis_index("head").astype(jnp.int32)
    z0 = index // NY
    y0 = index % NY
    spans = neighbours.shape[0]
    ref_count = 2 * spans
    rows_here, length, half = encodings.shape
    cut = rows_here // 2

    def move(x, dz, dy):
        return lax.ppermute(x, "seq", ring(seq, dz, dy))

    def swap(x):
        return lax.ppermute(x, "head", [(0, 1), (1, 0)])

    place = jnp.stack([z0, y0, head]).astype(jnp.int32)

    blocks = {0: [encodings]}
    ahead = behind = encodings
    readers = None
    for step in range(1, far + 1):
        if step == far:
            ahead, behind = ahead[cut:], behind[:cut]
        behind = move(behind, 1, 0)
        ahead = move(ahead, -1, 0)
        if step == far:
            blocks[far] = [behind, ahead]
        else:
            blocks[step], blocks[nz - step] = [ahead], [behind]
        if readers is None:
            ids = neighbours.reshape(1, ref_count)
            readers = [ids] + [move(ids, 0, -j) for j in range(1, NY)]
            table, ref_of = slot_tables(jnp.concatenate(readers, axis=0), y0, nz, rows_here)
    groups = []
    for phase in OUT:
        need = {d: blocks[d] for step in phase for d in planes_of(step, nz)}
        picked = pick_rows(table, place, need, phase, nz)
        groups.append([picked[0]] + [move(picked[j], 0, j) for j in range(1, NY)])

    own = compact(ref_of, place, groups, nz, ref_count)
    other = swap(own)
    lines = [[z * NY + y for z in range(nz)] for y in range(NY)]
    named = lax.all_to_all(
        table.reshape(NY, nz, CAP), "seq", 1, 1, axis_index_groups=lines, tiled=True
    ).reshape(NY, nz * CAP)

    flat = (ref_count * length, half)
    key_weight, value_weight, queries, out_grad = (
        pltpu.with_memory_space_constraint(a, pltpu.VMEM)
        for a in fetch(
            *(
                pltpu.with_memory_space_constraint(a, pltpu.HBM)
                for a in (key_weight, value_weight, queries, out_grad)
            )
        )
    )
    query_grad, partial_own, partial_other = core_step(
        place, own.reshape(flat), other.reshape(flat), key_weight, value_weight,
        queries, out_grad, spans, D // HEADS,
    )
    came = swap(partial_other)
    shape = (ref_count, length, half)
    outgoing = spread(ref_of, place, partial_own.reshape(shape), came.reshape(shape), seq)
    outgoing = outgoing.reshape(seq, CAP, length, half)
    back = lax.all_to_all(outgoing, "seq", split_axis=0, concat_axis=0, tiled=True)
    total = combine(named, place, back.reshape(seq * CAP, length, half), rows_here)
    return (query_grad, total)


def solution(mesh):
    return jax.shard_map(
        whole_step,
        mesh=mesh,
        in_specs=(
            P(("dp", "seq"), "head"),
            P(("dp", "seq"), "head"),
            P(("dp", "seq"), None, "head"),
            P(None, "head"),
            P(None, "head"),
            P(("dp", "seq"), None),
        ),
        out_specs=(P(("dp", "seq"), "head"), P(("dp", "seq"), None, "head")),
        check_vma=False,
    )
```

time: 243 us -> 152 us (0.63)
  blocking collectives: 93.1 us -> 0 us
  starting transfers between devices: 10.1 us -> 40.3 us
  Pallas kernels: 0 us -> 26.2 us
  local copies, waits for them, and re-layouts: 25.7 us -> 2.79 us
  matrix products: 20 us -> 0 us
  between operations: 14.4 us -> 0.82 us
  waiting for transfers between devices: 76.3 us -> 80.6 us
    all_to_all x1 -> x0, blocking collectives: 46.8 us -> none  [on_device(): lax.all_to_all(outgoing, 'seq', split_axis=0, concat_axis=0, tiled=True)]
    all_gather x1 -> x0, blocking collectives: 46.3 us -> none  [on_device(): lax.all_gather(neighbours, 'seq', axis=0, tiled=True)]
    ppermute x0 -> x19, starting transfers between devices: none -> 31.4 us  [the longest x17 30.8 us: move(): return lax.ppermute(x, 'seq', ring(seq, dz, dy))]
    pallas_call x0 -> x7, Pallas kernels: none -> 26.2 us  [the longest x1 12.3 us: core_step(): pl.pallas_call(body, in_specs=[SMEM, VMEM, VMEM, VMEM, VMEM, VMEM, VMEM],...]
    ppermute x0 -> x19, waiting for transfers between devices: none -> 25.8 us  [the longest x17 25.8 us: move(): return lax.ppermute(x, 'seq', ring(seq, dz, dy))]
    dot_general x11 -> x0, matrix products: 18 us -> none  [the longest x1 4.39 us: on_device(): jnp.dot(flat_rows, key_weight, preferred_element_type=jnp.float32)]
    reduce_scatter x1 -> x0, waiting for transfers between devices: 17.5 us -> none  [on_device(): lax.psum_scatter(partial_value.reshape(ref_count, neighbour_len, full_wid...]
    all_gather x1 -> x0, waiting for transfers between devices: 11.6 us -> none  [on_device(): whole = lax.all_gather(flat_arrived, 'head', axis=2, tiled=True)]
  transfers between devices with their start and end apart: 3 -> 21, of which waited for: 3 -> 11; matrix products, arithmetic and copies ran while one was open for 3% -> 1% of each run, Pallas kernels for 0% -> 6%
where the time goes in v1:
time: 152 us
  waiting for transfers between devices  80.6 us (53%)
  starting transfers between devices  40.3 us (27%)
  Pallas kernels  26.2 us (17%)
  local copies, waits for them, and re-layouts  2.79 us (2%)
    all_to_all x1, waiting for transfers between devices, whole_step(): lax.all_to_all(outgoing, 'seq', split_axis=0, concat_axis=0, tiled=True)  49.7 us
    ppermute x17, starting transfers between devices, move(): return lax.ppermute(x, 'seq', ring(seq, dz, dy))  30.8 us
    ppermute x17, waiting for transfers between devices, move(): return lax.ppermute(x, 'seq', ring(seq, dz, dy))  25.8 us
    pallas_call x1, Pallas kernels, core_step(): pl.pallas_call(body, in_specs=[SMEM, VMEM, VMEM, VMEM, VMEM, VMEM, VMEM],...  12.3 us
    all_to_all x1, waiting for transfers between devices, whole_step(): lax.all_to_all(table.reshape(NY, nz, CAP), 'seq', 1, 1, axis_index_groups...  5.09 us
    all_to_all x1, starting transfers between devices, whole_step(): lax.all_to_all(outgoing, 'seq', split_axis=0, concat_axis=0, tiled=True)  4.68 us
    pallas_call x1, Pallas kernels, fetch(): pl.pallas_call(body, in_specs=[pl.BlockSpec(memory_space=pltpu.HBM)] * co...  4.27 us
    all_to_all x1, starting transfers between devices, whole_step(): lax.all_to_all(table.reshape(NY, nz, CAP), 'seq', 1, 1, axis_index_groups...  4.17 us
  transfers between devices with their start and end apart: 21, of which 11 were waited for; matrix products, arithmetic and copies ran while one was open for 1% of the time, Pallas kernels for 6%

profile of v1, /device:TPU:2, one launch (start us, length us, event | category | flops | bytes accessed | tf_op | source)
XLA Modules:
  0.0 151.6 jit_solution(9124190987217813793)
XLA Ops:
  1.5 1.6 %collective-permute-start.2 = (s32[1,22]{1,0:T(1,128)S(1)}, s32[1,22]{1,0:T(1,128)S(1)}, u32[]{:S(2)}, u32[]{:S(2)}) collective-permute-start(s32[1,22]{1,0:T(1,128)S(1)} %reshape.432), channel_id=1, source_target_pairs={{0,8},{8,16},{16,24},{24,0},{32,40},{40,48},{48,56},{56,32},{64,72... | collective-permute-start | bytes 272 | tf_op jit(solution)/shard_map/ppermute | solution.py:312
  3.1 2.9 %collective-permute-start.1 = (s32[1,22]{1,0:T(1,128)S(1)}, s32[1,22]{1,0:T(1,128)S(1)}, u32[]{:S(2)}, u32[]{:S(2)}) collective-permute-start(s32[1,22]{1,0:T(1,128)S(1)} %reshape.432), channel_id=1, source_target_pairs={{0,16},{8,24},{16,0},{24,8},{32,48},{40,56},{48,32},{56,40},{64,80... | collective-permute-start | bytes 272 | tf_op jit(solution)/shard_map/ppermute | solution.py:312
  7.4 5.9 %collective-permute-start.3 = (bf16[10,16,1024]{2,1,0:T(8,128)(2,1)}, bf16[10,16,1024]{2,1,0:T(8,128)(2,1)S(1)}, u32[]{:S(2)}, u32[]{:S(2)}) collective-permute-start(bf16[10,16,1024]{2,1,0:T(8,128)(2,1)} %refs_0_.2), channel_id=1, source_target_pairs={{0,224},{8,232},{16,240},{24,248},{32,0},{40,8},{48,16},{56,24},{6... | collective-permute-start | bytes 983048 | tf_op jit(solution)/shard_map/ppermute | solution.py:312
  14.1 5.5 %collective-permute-done.3.refs_1_ = bf16[10,16,1024]{2,1,0:T(8,128)(2,1)S(1)} collective-permute-done((bf16[10,16,1024]{2,1,0:T(8,128)(2,1)}, bf16[10,16,1024]{2,1,0:T(8,128)(2,1)S(1)}, u32[]{:S(2)}, u32[]{:S(2)}) %collective-permute-start.3) | collective-permute-done | bytes 327712 | tf_op jit(solution)/shard_map/ppermute | solution.py:312
  19.7 3.6 %collective-permute-start.5 = (bf16[10,16,1024]{2,1,0:T(8,128)(2,1)S(1)}, bf16[10,16,1024]{2,1,0:T(8,128)(2,1)S(1)}, u32[]{:S(2)}, u32[]{:S(2)}) collective-permute-start(bf16[10,16,1024]{2,1,0:T(8,128)(2,1)S(1)} %collective-permute-done.3.refs_1_), channel_id=1, source_target_pairs={{0,224},{8,232},{16,240},{24,248},{32,0},{40,8},{48,16},{56,24},{6... | collective-permute-start | bytes 983048 | tf_op jit(solution)/shard_map/ppermute | solution.py:312
  23.3 5.2 %collective-permute-done.5.refs_3_ = bf16[10,16,1024]{2,1,0:T(8,128)(2,1)S(1)} collective-permute-done((bf16[10,16,1024]{2,1,0:T(8,128)(2,1)S(1)}, bf16[10,16,1024]{2,1,0:T(8,128)(2,1)S(1)}, u32[]{:S(2)}, u32[]{:S(2)}) %collective-permute-start.5) | collective-permute-done | bytes 327712 | tf_op jit(solution)/shard_map/ppermute | solution.py:312
  28.5 3.7 %collective-permute-start.10 = (bf16[10,16,1024]{2,1,0:T(8,128)(2,1)S(1)}, bf16[10,16,1024]{2,1,0:T(8,128)(2,1)S(1)}, u32[]{:S(2)}, u32[]{:S(2)}) collective-permute-start(bf16[10,16,1024]{2,1,0:T(8,128)(2,1)S(1)} %collective-permute-done.5.refs_3_), channel_id=1, source_target_pairs={{0,224},{8,232},{16,240},{24,248},{32,0},{40,8},{48,16},{56,24},{6... | collective-permute-start | bytes 983048 | tf_op jit(solution)/shard_map/ppermute | solution.py:312
  34.8 2.0 %collective-permute-done.10.refs_0_ = bf16[10,16,1024]{2,1,0:T(8,128)(2,1)S(1)} collective-permute-done((bf16[10,16,1024]{2,1,0:T(8,128)(2,1)S(1)}, bf16[10,16,1024]{2,1,0:T(8,128)(2,1)S(1)}, u32[]{:S(2)}, u32[]{:S(2)}) %collective-permute-start.10) | collective-permute-done | bytes 327712 | tf_op jit(solution)/shard_map/ppermute | solution.py:312
  36.8 3.8 %collective-permute-start.13 = (bf16[5,16,1024]{2,1,0:T(8,128)(2,1)S(1)}, bf16[5,16,1024]{2,1,0:T(8,128)(2,1)S(1)}, u32[]{:S(2)}, u32[]{:S(2)}) collective-permute-start(bf16[5,16,1024]{2,1,0:T(8,128)(2,1)S(1)} %slice.20), channel_id=1, source_target_pairs={{0,224},{8,232},{16,240},{24,248},{32,0},{40,8},{48,16},{56,24},{6... | collective-permute-start | bytes 491528 | tf_op jit(solution)/shard_map/ppermute | solution.py:312
  41.5 2.8 %collective-permute-start.9 = (bf16[10,16,1024]{2,1,0:T(8,128)(2,1)S(1)}, bf16[10,16,1024]{2,1,0:T(8,128)(2,1)S(1)}, u32[]{:S(2)}, u32[]{:S(2)}) collective-permute-start(bf16[10,16,1024]{2,1,0:T(8,128)(2,1)S(1)} %get-tuple-element.20), channel_id=1, source_target_pairs={{0,24},{8,0},{16,8},{24,16},{32,56},{40,32},{48,40},{56,48},{64,88... | collective-permute-start | bytes 983048 | tf_op jit(solution)/shard_map/ppermute | solution.py:312
  44.4 2.9 %collective-permute-done.12.refs_2_ = bf16[5,16,1024]{2,1,0:T(8,128)(2,1)S(1)} collective-permute-done((bf16[5,16,1024]{2,1,0:T(8,128)(2,1)S(1)}, bf16[5,16,1024]{2,1,0:T(8,128)(2,1)S(1)}, u32[]{:S(2)}, u32[]{:S(2)}) %collective-permute-start.12) | collective-permute-done | bytes 163872 | tf_op jit(solution)/shard_map/ppermute | solution.py:312
  48.9 1.4 collective-permute-start.15
  50.3 1.6 %collective-permute-start.16 = (bf16[6,16,1024]{2,1,0:T(8,128)(2,1)S(1)}, bf16[6,16,1024]{2,1,0:T(8,128)(2,1)S(1)}, u32[]{:S(2)}, u32[]{:S(2)}) collective-permute-start(bf16[6,16,1024]{2,1,0:T(8,128)(2,1)S(1)} %get-tuple-element.24), channel_id=1, source_target_pairs={{0,24},{8,0},{16,8},{24,16},{32,56},{40,32},{48,40},{56,48},{64,88... | collective-permute-start | bytes 589832 | tf_op jit(solution)/shard_map/ppermute | solution.py:312
  52.8 4.8 %collective-permute-done.9.refs_3_ = bf16[10,16,1024]{2,1,0:T(8,128)(2,1)S(1)} collective-permute-done((bf16[10,16,1024]{2,1,0:T(8,128)(2,1)S(1)}, bf16[10,16,1024]{2,1,0:T(8,128)(2,1)S(1)}, u32[]{:S(2)}, u32[]{:S(2)}) %collective-permute-start.9) | collective-permute-done | bytes 327712 | tf_op jit(solution)/shard_map/ppermute | solution.py:312
  58.4 3.5 %collective-permute-done.16.refs_7_ = bf16[6,16,1024]{2,1,0:T(8,128)(2,1)S(1)} collective-permute-done((bf16[6,16,1024]{2,1,0:T(8,128)(2,1)S(1)}, bf16[6,16,1024]{2,1,0:T(8,128)(2,1)S(1)}, u32[]{:S(2)}, u32[]{:S(2)}) %collective-permute-start.16) | collective-permute-done | bytes 196640 | tf_op jit(solution)/shard_map/ppermute | solution.py:312
  61.9 1.8 %compact.1 = bf16[22,16,1024]{2,1,0:T(8,128)(2,1)S(1)} custom-call(s32[4,16]{1,0:T(4,128)S(1)} %broadcast_add_fusion.1.r_ref, s32[3]{0:T(128)S(1)} %pad_add_fusion.1.p_ref, bf16[10,16,1024]{2,1,0:T(8,128)(2,1)S(1)} %get-tuple-element.17.refs_0_, bf16[10,16,1024]{2,1,0:T(8,128)(2,1)S(1)} %collective-permute-done.7.refs_1_, ...), custom_call_target="tpu_custom_call" | custom-call | tf_op jit(solution)/shard_map/compact/pallas_call | solution.py:97
  63.8 4.3 %fetch.1 = (bf16[2048,1024]{1,0:T(8,128)(2,1)S(1)}, bf16[2048,1024]{1,0:T(8,128)(2,1)S(1)}, bf16[704,1024]{1,0:T(8,128)(2,1)S(1)}, bf16[704,1024]{1,0:T(8,128)(2,1)S(1)}) custom-call(bf16[2048,1024]{1,0:T(8,128)(2,1)} %refs_0_.3, bf16[2048,1024]{1,0:T(8,128)(2,1)} %refs_1_.1, bf16[704,1024]{1,0:T(8,128)(2,1)} %refs_2_.1, bf16[704,1024]{1,0:T(8,128)(2,1)} %refs_3_.1), custom_call_target="tpu_custom_call" | custom-call | tf_op jit(solution)/shard_map/fetch/pallas_call | solution.py:187
  68.1 12.3 %core_step.1 = (bf16[704,1024]{1,0:T(8,128)(2,1)}, f32[352,1024]{1,0:T(8,128)S(1)}, bf16[352,1024]{1,0:T(8,128)(2,1)S(1)}) custom-call(s32[3]{0:T(128)S(1)} %pad_add_fusion.1.p_ref, bf16[352,1024]{1,0:T(8,128)(2,1)S(1)} %bitcast.16, bf16[352,1024]{1,0:T(8,128)(2,1)S(1)} %bitcast.18, bf16[2048,1024]{1,0:T(8,128)(2,1)S(1)} %get-tuple-element.25.wk_ref, ...), custom_call_target="tpu_custom_call" | custom-call | tf_op jit(solution)/shard_map/core_step/pallas_call | solution.py:259
  81.6 4.2 %all-to-all-start = ((s32[4,8,2]{0,2,1:T(2,128)}), s32[4,8,2]{0,2,1:T(2,128)S(1)}, u32[]{:S(2)}, u32[]{:S(2)}) async-start(s32[4,8,2]{0,2,1:T(2,128)} %bitcast.7), calls=%async_computation | async-start | bytes 16384 | tf_op jit(solution)/shard_map/all_to_all | solution.py:344
  85.8 2.6 %spread.1 = bf16[64,16,1024]{2,1,0:T(8,128)(2,1)} custom-call(s32[4,16]{1,0:T(4,128)S(1)} %broadcast_add_fusion.1.r_ref, s32[3]{0:T(128)S(1)} %pad_add_fusion.1.p_ref, f32[22,16,1024]{2,1,0:T(8,128)S(1)} %bitcast.17, bf16[22,16,1024]{2,1,0:T(8,128)(2,1)S(1)} %bitcast.19), custom_call_target="tpu_custom_call" | custom-call | tf_op jit(solution)/shard_map/spread/pallas_call | solution.py:124
  88.4 5.1 %all-to-all-done = s32[4,8,2]{0,2,1:T(2,128)S(1)} async-done(((s32[4,8,2]{0,2,1:T(2,128)}), s32[4,8,2]{0,2,1:T(2,128)S(1)}, u32[]{:S(2)}, u32[]{:S(2)}) %all-to-all-start) | async-done | bytes 288 | tf_op jit(solution)/shard_map/all_to_all | solution.py:344
  93.5 4.7 %all-to-all-start.1 = ((bf16[32,2,16,1024]{3,2,1,0:T(8,128)(2,1)}), bf16[32,2,16,1024]{3,2,1,0:T(8,128)(2,1)S(1)}, u32[]{:S(2)}, u32[]{:S(2)}) async-start(bf16[32,2,16,1024]{3,2,1,0:T(8,128)(2,1)} %bitcast.11), calls=%async_computation.1 | async-start | bytes 4194304 | tf_op jit(solution)/shard_map/all_to_all | solution.py:366
  98.3 49.7 %all-to-all-done.1 = bf16[32,2,16,1024]{3,2,1,0:T(8,128)(2,1)S(1)} async-done(((bf16[32,2,16,1024]{3,2,1,0:T(8,128)(2,1)}), bf16[32,2,16,1024]{3,2,1,0:T(8,128)(2,1)S(1)}, u32[]{:S(2)}, u32[]{:S(2)}) %all-to-all-start.1) | async-done | bytes 2097184 | tf_op jit(solution)/shard_map/all_to_all | solution.py:366
  148.0 3.6 %combine.1 = bf16[10,16,1024]{2,1,0:T(8,128)(2,1)} custom-call(s32[4,16]{1,0:T(4,128)S(1)} %copy.50.n_ref, s32[3]{0:T(128)S(1)} %pad_add_fusion.1.p_ref, bf16[64,16,1024]{2,1,0:T(8,128)(2,1)S(1)} %bitcast.15), custom_call_target="tpu_custom_call" | custom-call | tf_op jit(solution)/shard_map/combine/pallas_call | solution.py:163
  (49 shorter events, 11.4 us)
Async XLA Ops:
  1.5 11.9 %collective-permute-start.2 = (s32[1,22]{1,0:T(1,128)S(1)}, s32[1,22]{1,0:T(1,128)S(1)}, u32[]{:S(2)}, u32[]{:S(2)}) collective-permute-start(s32[1,22]{1,0:T(1,128)S(1)} %reshape.432), channel_id=1, source_target_pairs={{0,8},{8,16},{16,24},{24,0},{32,40},{40,48},{48,56},{56,32},{64,72... | collective-permute-start | bytes 272 | tf_op jit(solution)/shard_map/ppermute | solution.py:312
  3.1 10.2 %collective-permute-start.1 = (s32[1,22]{1,0:T(1,128)S(1)}, s32[1,22]{1,0:T(1,128)S(1)}, u32[]{:S(2)}, u32[]{:S(2)}) collective-permute-start(s32[1,22]{1,0:T(1,128)S(1)} %reshape.432), channel_id=1, source_target_pairs={{0,16},{8,24},{16,0},{24,8},{32,48},{40,56},{48,32},{56,40},{64,80... | collective-permute-start | bytes 272 | tf_op jit(solution)/shard_map/ppermute | solution.py:312
  6.0 7.3 %collective-permute-start = (s32[1,22]{1,0:T(1,128)S(1)}, s32[1,22]{1,0:T(1,128)S(1)}, u32[]{:S(2)}, u32[]{:S(2)}) collective-permute-start(s32[1,22]{1,0:T(1,128)S(1)} %reshape.432), channel_id=1, source_target_pairs={{0,24},{8,0},{16,8},{24,16},{32,56},{40,32},{48,40},{56,48},{64,88... | collective-permute-start | bytes 272 | tf_op jit(solution)/shard_map/ppermute | solution.py:312
  7.4 12.3 %collective-permute-start.3 = (bf16[10,16,1024]{2,1,0:T(8,128)(2,1)}, bf16[10,16,1024]{2,1,0:T(8,128)(2,1)S(1)}, u32[]{:S(2)}, u32[]{:S(2)}) collective-permute-start(bf16[10,16,1024]{2,1,0:T(8,128)(2,1)} %refs_0_.2), channel_id=1, source_target_pairs={{0,224},{8,232},{16,240},{24,248},{32,0},{40,8},{48,16},{56,24},{6... | collective-permute-start | bytes 983048 | tf_op jit(solution)/shard_map/ppermute | solution.py:312
  13.2 10.0 %collective-permute-start.4 = (bf16[10,16,1024]{2,1,0:T(8,128)(2,1)}, bf16[10,16,1024]{2,1,0:T(8,128)(2,1)S(1)}, u32[]{:S(2)}, u32[]{:S(2)}) collective-permute-start(bf16[10,16,1024]{2,1,0:T(8,128)(2,1)} %refs_0_.2), channel_id=1, source_target_pairs={{0,32},{8,40},{16,48},{24,56},{32,64},{40,72},{48,80},{56,88},{64,... | collective-permute-start | bytes 983048 | tf_op jit(solution)/shard_map/ppermute | solution.py:312
  19.7 8.9 %collective-permute-start.5 = (bf16[10,16,1024]{2,1,0:T(8,128)(2,1)S(1)}, bf16[10,16,1024]{2,1,0:T(8,128)(2,1)S(1)}, u32[]{:S(2)}, u32[]{:S(2)}) collective-permute-start(bf16[10,16,1024]{2,1,0:T(8,128)(2,1)S(1)} %collective-permute-done.3.refs_1_), channel_id=1, source_target_pairs={{0,224},{8,232},{16,240},{24,248},{32,0},{40,8},{48,16},{56,24},{6... | collective-permute-start | bytes 983048 | tf_op jit(solution)/shard_map/ppermute | solution.py:312
  23.3 9.0 %collective-permute-start.6 = (bf16[10,16,1024]{2,1,0:T(8,128)(2,1)S(1)}, bf16[10,16,1024]{2,1,0:T(8,128)(2,1)S(1)}, u32[]{:S(2)}, u32[]{:S(2)}) collective-permute-start(bf16[10,16,1024]{2,1,0:T(8,128)(2,1)S(1)} %collective-permute-done.4.refs_2_), channel_id=1, source_target_pairs={{0,32},{8,40},{16,48},{24,56},{32,64},{40,72},{48,80},{56,88},{64,... | collective-permute-start | bytes 983048 | tf_op jit(solution)/shard_map/ppermute | solution.py:312
  28.5 8.3 %collective-permute-start.10 = (bf16[10,16,1024]{2,1,0:T(8,128)(2,1)S(1)}, bf16[10,16,1024]{2,1,0:T(8,128)(2,1)S(1)}, u32[]{:S(2)}, u32[]{:S(2)}) collective-permute-start(bf16[10,16,1024]{2,1,0:T(8,128)(2,1)S(1)} %collective-permute-done.5.refs_3_), channel_id=1, source_target_pairs={{0,224},{8,232},{16,240},{24,248},{32,0},{40,8},{48,16},{56,24},{6... | collective-permute-start | bytes 983048 | tf_op jit(solution)/shard_map/ppermute | solution.py:312
  32.2 8.4 %collective-permute-start.11 = (bf16[10,16,1024]{2,1,0:T(8,128)(2,1)S(1)}, bf16[10,16,1024]{2,1,0:T(8,128)(2,1)S(1)}, u32[]{:S(2)}, u32[]{:S(2)}) collective-permute-start(bf16[10,16,1024]{2,1,0:T(8,128)(2,1)S(1)} %collective-permute-done.6.refs_4_), channel_id=1, source_target_pairs={{0,32},{8,40},{16,48},{24,56},{32,64},{40,72},{48,80},{56,88},{64,... | collective-permute-start | bytes 983048 | tf_op jit(solution)/shard_map/ppermute | solution.py:312
  32.4 1.0 copy-start
  34.1 16.2 %collective-permute-start.7 = (bf16[10,16,1024]{2,1,0:T(8,128)(2,1)S(1)}, bf16[10,16,1024]{2,1,0:T(8,128)(2,1)S(1)}, u32[]{:S(2)}, u32[]{:S(2)}) collective-permute-start(bf16[10,16,1024]{2,1,0:T(8,128)(2,1)S(1)} %get-tuple-element.18), channel_id=1, source_target_pairs={{0,8},{8,16},{16,24},{24,0},{32,40},{40,48},{48,56},{56,32},{64,72... | collective-permute-start | bytes 983048 | tf_op jit(solution)/shard_map/ppermute | solution.py:312
  36.8 7.5 %collective-permute-start.13 = (bf16[5,16,1024]{2,1,0:T(8,128)(2,1)S(1)}, bf16[5,16,1024]{2,1,0:T(8,128)(2,1)S(1)}, u32[]{:S(2)}, u32[]{:S(2)}) collective-permute-start(bf16[5,16,1024]{2,1,0:T(8,128)(2,1)S(1)} %slice.20), channel_id=1, source_target_pairs={{0,224},{8,232},{16,240},{24,248},{32,0},{40,8},{48,16},{56,24},{6... | collective-permute-start | bytes 491528 | tf_op jit(solution)/shard_map/ppermute | solution.py:312
  40.7 6.6 %collective-permute-start.12 = (bf16[5,16,1024]{2,1,0:T(8,128)(2,1)S(1)}, bf16[5,16,1024]{2,1,0:T(8,128)(2,1)S(1)}, u32[]{:S(2)}, u32[]{:S(2)}) collective-permute-start(bf16[5,16,1024]{2,1,0:T(8,128)(2,1)S(1)} %slice.19), channel_id=1, source_target_pairs={{0,32},{8,40},{16,48},{24,56},{32,64},{40,72},{48,80},{56,88},{64,... | collective-permute-start | bytes 491528 | tf_op jit(solution)/shard_map/ppermute | solution.py:312
  40.8 12.0 %collective-permute-start.8 = (bf16[10,16,1024]{2,1,0:T(8,128)(2,1)S(1)}, bf16[10,16,1024]{2,1,0:T(8,128)(2,1)S(1)}, u32[]{:S(2)}, u32[]{:S(2)}) collective-permute-start(bf16[10,16,1024]{2,1,0:T(8,128)(2,1)S(1)} %get-tuple-element.19), channel_id=1, source_target_pairs={{0,16},{8,24},{16,0},{24,8},{32,48},{40,56},{48,32},{56,40},{64,80... | collective-permute-start | bytes 983048 | tf_op jit(solution)/shard_map/ppermute | solution.py:312
  41.5 16.2 %collective-permute-start.9 = (bf16[10,16,1024]{2,1,0:T(8,128)(2,1)S(1)}, bf16[10,16,1024]{2,1,0:T(8,128)(2,1)S(1)}, u32[]{:S(2)}, u32[]{:S(2)}) collective-permute-start(bf16[10,16,1024]{2,1,0:T(8,128)(2,1)S(1)} %get-tuple-element.20), channel_id=1, source_target_pairs={{0,24},{8,0},{16,8},{24,16},{32,56},{40,32},{48,40},{56,48},{64,88... | collective-permute-start | bytes 983048 | tf_op jit(solution)/shard_map/ppermute | solution.py:312
  48.1 10.2 %collective-permute-start.14 = (bf16[6,16,1024]{2,1,0:T(8,128)(2,1)S(1)}, bf16[6,16,1024]{2,1,0:T(8,128)(2,1)S(1)}, u32[]{:S(2)}, u32[]{:S(2)}) collective-permute-start(bf16[6,16,1024]{2,1,0:T(8,128)(2,1)S(1)} %get-tuple-element.22), channel_id=1, source_target_pairs={{0,8},{8,16},{16,24},{24,0},{32,40},{40,48},{48,56},{56,32},{64,72... | collective-permute-start | bytes 589832 | tf_op jit(solution)/shard_map/ppermute | solution.py:312
  48.9 9.5 %collective-permute-start.15 = (bf16[6,16,1024]{2,1,0:T(8,128)(2,1)S(1)}, bf16[6,16,1024]{2,1,0:T(8,128)(2,1)S(1)}, u32[]{:S(2)}, u32[]{:S(2)}) collective-permute-start(bf16[6,16,1024]{2,1,0:T(8,128)(2,1)S(1)} %get-tuple-element.23), channel_id=1, source_target_pairs={{0,16},{8,24},{16,0},{24,8},{32,48},{40,56},{48,32},{56,40},{64,80... | collective-permute-start | bytes 589832 | tf_op jit(solution)/shard_map/ppermute | solution.py:312
  50.3 11.6 %collective-permute-start.16 = (bf16[6,16,1024]{2,1,0:T(8,128)(2,1)S(1)}, bf16[6,16,1024]{2,1,0:T(8,128)(2,1)S(1)}, u32[]{:S(2)}, u32[]{:S(2)}) collective-permute-start(bf16[6,16,1024]{2,1,0:T(8,128)(2,1)S(1)} %get-tuple-element.24), channel_id=1, source_target_pairs={{0,24},{8,0},{16,8},{24,16},{32,56},{40,32},{48,40},{56,48},{64,88... | collective-permute-start | bytes 589832 | tf_op jit(solution)/shard_map/ppermute | solution.py:312
  63.7 4.4 %collective-permute-start.17 = (bf16[22,16,1024]{2,1,0:T(8,128)(2,1)S(1)}, bf16[22,16,1024]{2,1,0:T(8,128)(2,1)S(1)}, u32[]{:S(2)}, u32[]{:S(2)}) collective-permute-start(bf16[22,16,1024]{2,1,0:T(8,128)(2,1)S(1)} %compact.1), channel_id=1, source_target_pairs={{0,4},{4,0},{1,5},{5,1},{2,6},{6,2},{3,7},{7,3},{8,12},{12,8},{9,1... | collective-permute-start | bytes 2162696 | tf_op jit(solution)/shard_map/ppermute | solution.py:315
  80.4 5.4 %collective-permute-start.18 = (bf16[352,1024]{1,0:T(8,128)(2,1)S(1)}, bf16[352,1024]{1,0:T(8,128)(2,1)S(1)}, u32[]{:S(2)}, u32[]{:S(2)}) collective-permute-start(bf16[352,1024]{1,0:T(8,128)(2,1)S(1)} %get-tuple-element.31), channel_id=1, source_target_pairs={{0,4},{4,0},{1,5},{5,1},{2,6},{6,2},{3,7},{7,3},{8,12},{12,8},{9,1... | collective-permute-start | bytes 2162696 | tf_op jit(solution)/shard_map/ppermute | solution.py:315
  81.6 11.9 %all-to-all-start = ((s32[4,8,2]{0,2,1:T(2,128)}), s32[4,8,2]{0,2,1:T(2,128)S(1)}, u32[]{:S(2)}, u32[]{:S(2)}) async-start(s32[4,8,2]{0,2,1:T(2,128)} %bitcast.7), calls=%async_computation | async-start | bytes 16384 | tf_op jit(solution)/shard_map/all_to_all | solution.py:344
  93.5 54.5 %all-to-all-start.1 = ((bf16[32,2,16,1024]{3,2,1,0:T(8,128)(2,1)}), bf16[32,2,16,1024]{3,2,1,0:T(8,128)(2,1)S(1)}, u32[]{:S(2)}, u32[]{:S(2)}) async-start(bf16[32,2,16,1024]{3,2,1,0:T(8,128)(2,1)} %bitcast.11), calls=%async_computation.1 | async-start | bytes 4194304 | tf_op jit(solution)/shard_map/all_to_all | solution.py:366

commit v2 on v1

--- a/solution.py
+++ b/solution.py
@@ -22,6 +22,7 @@
 F32 = jnp.float32
 
 OUT = ((0, 1, 2), (3, 4))
+BACK = ((4,), (3, 2), (1, 0))
 
 
 def planes_of(step, nz):
@@ -104,71 +105,111 @@
     )(ref_of, place, *flat)
 
 
-def spread(ref_of, place, own, other, seq):
+def spread(ref_of, place, own, other, phase, nz):
     tail = own.shape[1:]
-    nz = seq // NY
-
-    def body(r_ref, p_ref, own_ref, other_ref, out):
+    slots = slots_of(phase, nz)
+
+    def body(r_ref, p_ref, own_ref, other_ref, *outs):
         for j in range(NY):
-            for d in range(nz):
-                holder = d * NY + (p_ref[1] + NY - j) % NY
+            for k, (d, s) in enumerate(slots):
+                r = r_ref[j, (p_ref[0] + d) % nz * CAP + s]
+
+                @pl.when(r >= 0)
+                def _():
+                    at = jnp.maximum(r, 0)
+                    total = own_ref[at] + other_ref[at].astype(F32)
+                    outs[j][k] = total.astype(BF)
+
+    return pl.pallas_call(
+        body,
+        in_specs=[SMEM, SMEM, VMEM, VMEM],
+        out_specs=[VMEM] * NY,
+        out_shape=[jax.ShapeDtypeStruct((len(slots),) + tail, BF)] * NY,
+        compiler_params=SMALL,
+        name="spread",
+    )(ref_of, place, own, other)
+
+
+def gather_grads(table, place, parts, phase, before, step, nz, rows_here):
+    planes = planes_of(step, nz)
+    tail = parts[0].shape[1:]
+    cut = rows_here // 2
+    far = 2 * step == nz
+    slots = slots_of(phase, nz)
+    if far:
+        shapes = [(cut,) + tail, (rows_here - cut,) + tail]
+    else:
+        shapes = [(rows_here,) + tail] * len(planes)
+    halves = bool(before) and before[0].shape[0] != rows_here
+
+    def body(t_ref, p_ref, *refs):
+        ins = refs[:NY]
+        prev = refs[NY : NY + len(before)]
+        outs = refs[NY + len(before) : -1]
+        acc = refs[-1]
+
+        def fill(r, carry):
+            for p in range(len(planes)):
+                if step == 0:
+                    acc[p, r] = prev[0][r].astype(F32) + prev[1][r].astype(F32)
+                elif before and not halves:
+                    acc[p, r] = prev[p][r].astype(F32)
+                else:
+                    acc[p, r] = jnp.zeros(tail, F32)
+            return carry
+
+        def low(r, carry):
+            acc[0, r] = prev[0][r].astype(F32)
+            return carry
+
+        def high(r, carry):
+            acc[1, r + cut] = prev[1][r].astype(F32)
+            return carry
+
+        lax.fori_loop(0, rows_here, fill, 0)
+        if halves:
+            lax.fori_loop(0, cut, low, 0)
+            lax.fori_loop(0, rows_here - cut, high, 0)
+        for p, d in enumerate(planes):
+            at_plane = (p_ref[0] + d) % nz * CAP
+            for j in range(NY):
                 for s in range(CAP):
-                    r = r_ref[j, d * CAP + s]
-
-                    @pl.when(r >= 0)
+                    row = t_ref[j, at_plane + s]
+                    k = slots.index((d, s))
+
+                    @pl.when(row >= 0)
                     def _():
-                        at = jnp.maximum(r, 0)
-                        total = own_ref[at] + other_ref[at].astype(F32)
-                        out[holder * CAP + s] = total.astype(BF)
-
-    return pl.pallas_call(
-        body,
-        in_specs=[SMEM, SMEM, VMEM, VMEM],
-        out_specs=VMEM,
-        out_shape=jax.ShapeDtypeStruct((seq * CAP,) + tail, BF),
-        name="spread",
+                        at = jnp.maximum(row, 0)
+                        acc[p, at] = acc[p, at] + ins[j][k].astype(F32)
+
+        def drain(r, carry):
+            for p in range(len(planes)):
+                outs[p][r] = acc[p, r].astype(BF)
+            return carry
+
+        def drain_low(r, carry):
+            outs[0][r] = acc[0, r].astype(BF)
+            return carry
+
+        def drain_high(r, carry):
+            outs[1][r] = acc[0, r + cut].astype(BF)
+            return carry
+
+        if far:
+            lax.fori_loop(0, cut, drain_low, 0)
+            lax.fori_loop(0, rows_here - cut, drain_high, 0)
+        else:
+            lax.fori_loop(0, rows_here, drain, 0)
+
+    return pl.pallas_call(
+        body,
+        in_specs=[SMEM, SMEM] + [VMEM] * (NY + len(before)),
+        out_specs=[VMEM] * len(shapes),
+        out_shape=[jax.ShapeDtypeStruct(s, BF) for s in shapes],
+        scratch_shapes=[pltpu.VMEM((len(planes), rows_here) + tail, F32)],
         compiler_params=SMALL,
-    )(ref_of, place, own, other)
-
-
-def combine(named, place, came, rows_here):
-    slots = came.shape[0]
-    tail = came.shape[1:]
-
-    def body(n_ref, p_ref, in_ref, out, acc):
-        def clear(r, carry):
-            acc[r] = jnp.zeros(tail, F32)
-            return carry
-
-        def add(k, carry):
-            reader = k // CAP
-            j = (reader % NY + NY - p_ref[1]) % NY
-            row = n_ref[j, reader // NY * CAP + k % CAP]
-
-            @pl.when(row >= 0)
-            def _():
-                at = jnp.maximum(row, 0)
-                acc[at] = acc[at] + in_ref[k].astype(F32)
-
-            return carry
-
-        def drain(r, carry):
-            out[r] = acc[r].astype(BF)
-            return carry
-
-        lax.fori_loop(0, rows_here, clear, 0)
-        lax.fori_loop(0, slots, add, 0)
-        lax.fori_loop(0, rows_here, drain, 0)
-
-    return pl.pallas_call(
-        body,
-        in_specs=[SMEM, SMEM, VMEM],
-        out_specs=VMEM,
-        out_shape=jax.ShapeDtypeStruct((rows_here,) + tail, BF),
-        scratch_shapes=[pltpu.VMEM((rows_here,) + tail, F32)],
-        name="combine",
-        compiler_params=SMALL,
-    )(named, place, came)
+        name="gather",
+    )(table, place, *parts, *before)
 
 
 def fetch(*arrays):
@@ -340,11 +381,6 @@
 
     own = compact(ref_of, place, groups, nz, ref_count)
     other = swap(own)
-    lines = [[z * NY + y for z in range(nz)] for y in range(NY)]
-    named = lax.all_to_all(
-        table.reshape(NY, nz, CAP), "seq", 1, 1, axis_index_groups=lines, tiled=True
-    ).reshape(NY, nz * CAP)
-
     flat = (ref_count * length, half)
     key_weight, value_weight, queries, out_grad = (
         pltpu.with_memory_space_constraint(a, pltpu.VMEM)
@@ -361,11 +397,17 @@
     )
     came = swap(partial_other)
     shape = (ref_count, length, half)
-    outgoing = spread(ref_of, place, partial_own.reshape(shape), came.reshape(shape), seq)
-    outgoing = outgoing.reshape(seq, CAP, length, half)
-    back = lax.all_to_all(outgoing, "seq", split_axis=0, concat_axis=0, tiled=True)
-    total = combine(named, place, back.reshape(seq * CAP, length, half), rows_here)
-    return (query_grad, total)
+    partial_own, came = partial_own.reshape(shape), came.reshape(shape)
+
+    before = ()
+    for phase in BACK:
+        parts = spread(ref_of, place, partial_own, came, phase, nz)
+        parts = [parts[0]] + [move(parts[j], 0, -j) for j in range(1, NY)]
+        for step in phase:
+            total = gather_grads(table, place, parts, phase, before, step, nz, rows_here)
+            if step > 0:
+                before = (move(total[0], 1, 0), move(total[1], -1, 0))
+    return (query_grad, total[0])
 
 
 def solution(mesh):

time: 152 us -> 154 us (1.013)
  starting transfers between devices: 40.3 us -> 55.9 us
  waiting for transfers between devices: 80.6 us -> 65.1 us
  Pallas kernels: 26.2 us -> 28.3 us
    all_to_all x2 -> x0, waiting for transfers between devices: 54.8 us -> none  [the longest x1 49.7 us: whole_step(): lax.all_to_all(outgoing, 'seq', split_axis=0, concat_axis=0, tiled=True)]
    ppermute x17 -> x34, waiting for transfers between devices: 25.8 us -> 63.3 us  [move(): return lax.ppermute(x, 'seq', ring(seq, dz, dy))]
    ppermute x17 -> x34, starting transfers between devices: 30.8 us -> 55.2 us  [move(): return lax.ppermute(x, 'seq', ring(seq, dz, dy))]
    all_to_all x2 -> x0, starting transfers between devices: 8.84 us -> none  [the longest x1 4.68 us: whole_step(): lax.all_to_all(outgoing, 'seq', split_axis=0, concat_axis=0, tiled=True)]
    pallas_call x2 -> x8, Pallas kernels: 6.21 us -> 8.38 us  [the longest x5 5.32 us: gather_grads(): pl.pallas_call(body, in_specs=[SMEM, SMEM] + [VMEM] * (NY + len(before)),...]
    ppermute x2, waiting for transfers between devices: 0.01 us -> 1.82 us  [swap(): return lax.ppermute(x, 'head', [(0, 1), (1, 0)])]
  transfers between devices with their start and end apart: 21 -> 36, of which waited for: 11 -> 18; matrix products, arithmetic and copies ran while one was open for 1% -> 1% of each run, Pallas kernels for 6% -> 6%
where the time goes in v2:
time: 154 us; the launch traced here: 153 us
  waiting for transfers between devices  65.1 us (42%)
  starting transfers between devices  55.9 us (36%)
  Pallas kernels  28.3 us (18%)
  local copies, waits for them, and re-layouts  2.03 us (1%)
    ppermute x34, waiting for transfers between devices, move(): return lax.ppermute(x, 'seq', ring(seq, dz, dy))  63.3 us
    ppermute x34, starting transfers between devices, move(): return lax.ppermute(x, 'seq', ring(seq, dz, dy))  55.2 us
    pallas_call x1, Pallas kernels, core_step(): pl.pallas_call(body, in_specs=[SMEM, VMEM, VMEM, VMEM, VMEM, VMEM, VMEM],...  12.3 us
    pallas_call x5, Pallas kernels, gather_grads(): pl.pallas_call(body, in_specs=[SMEM, SMEM] + [VMEM] * (NY + len(before)),...  5.32 us
    pallas_call x1, Pallas kernels, fetch(): pl.pallas_call(body, in_specs=[pl.BlockSpec(memory_space=pltpu.HBM)] * co...  4.27 us
  transfers between devices with their start and end apart: 36, of which 18 were waited for; matrix products, arithmetic and copies ran while one was open for 1% of the time, Pallas kernels for 6%

profile of v2, /device:TPU:2, one launch (start us, length us, event | category | flops | bytes accessed | tf_op | source)
XLA Modules:
  0.0 153.3 jit_solution(14887139531667543088)
XLA Ops:
  3.1 2.9 %collective-permute-start.1 = (s32[1,22]{1,0:T(1,128)S(1)}, s32[1,22]{1,0:T(1,128)S(1)}, u32[]{:S(2)}, u32[]{:S(2)}) collective-permute-start(s32[1,22]{1,0:T(1,128)S(1)} %reshape.419), channel_id=1, source_target_pairs={{0,16},{8,24},{16,0},{24,8},{32,48},{40,56},{48,32},{56,40},{64,80... | collective-permute-start | bytes 272 | tf_op jit(solution)/shard_map/ppermute | solution.py:353
  7.4 5.9 %collective-permute-start.3 = (bf16[10,16,1024]{2,1,0:T(8,128)(2,1)}, bf16[10,16,1024]{2,1,0:T(8,128)(2,1)S(1)}, u32[]{:S(2)}, u32[]{:S(2)}) collective-permute-start(bf16[10,16,1024]{2,1,0:T(8,128)(2,1)} %refs_0_.2), channel_id=1, source_target_pairs={{0,224},{8,232},{16,240},{24,248},{32,0},{40,8},{48,16},{56,24},{6... | collective-permute-start | bytes 983048 | tf_op jit(solution)/shard_map/ppermute | solution.py:353
  14.1 5.5 %collective-permute-done.3.refs_1_ = bf16[10,16,1024]{2,1,0:T(8,128)(2,1)S(1)} collective-permute-done((bf16[10,16,1024]{2,1,0:T(8,128)(2,1)}, bf16[10,16,1024]{2,1,0:T(8,128)(2,1)S(1)}, u32[]{:S(2)}, u32[]{:S(2)}) %collective-permute-start.3) | collective-permute-done | bytes 327712 | tf_op jit(solution)/shard_map/ppermute | solution.py:353
  19.7 3.6 %collective-permute-start.5 = (bf16[10,16,1024]{2,1,0:T(8,128)(2,1)S(1)}, bf16[10,16,1024]{2,1,0:T(8,128)(2,1)S(1)}, u32[]{:S(2)}, u32[]{:S(2)}) collective-permute-start(bf16[10,16,1024]{2,1,0:T(8,128)(2,1)S(1)} %collective-permute-done.3.refs_1_), channel_id=1, source_target_pairs={{0,224},{8,232},{16,240},{24,248},{32,0},{40,8},{48,16},{56,24},{6... | collective-permute-start | bytes 983048 | tf_op jit(solution)/shard_map/ppermute | solution.py:353
  23.3 5.2 %collective-permute-done.5.refs_3_ = bf16[10,16,1024]{2,1,0:T(8,128)(2,1)S(1)} collective-permute-done((bf16[10,16,1024]{2,1,0:T(8,128)(2,1)S(1)}, bf16[10,16,1024]{2,1,0:T(8,128)(2,1)S(1)}, u32[]{:S(2)}, u32[]{:S(2)}) %collective-permute-start.5) | collective-permute-done | bytes 327712 | tf_op jit(solution)/shard_map/ppermute | solution.py:353
  28.5 3.7 %collective-permute-start.10 = (bf16[10,16,1024]{2,1,0:T(8,128)(2,1)S(1)}, bf16[10,16,1024]{2,1,0:T(8,128)(2,1)S(1)}, u32[]{:S(2)}, u32[]{:S(2)}) collective-permute-start(bf16[10,16,1024]{2,1,0:T(8,128)(2,1)S(1)} %collective-permute-done.5.refs_3_), channel_id=1, source_target_pairs={{0,224},{8,232},{16,240},{24,248},{32,0},{40,8},{48,16},{56,24},{6... | collective-permute-start | bytes 983048 | tf_op jit(solution)/shard_map/ppermute | solution.py:353
  36.8 3.8 %collective-permute-start.13 = (bf16[5,16,1024]{2,1,0:T(8,128)(2,1)S(1)}, bf16[5,16,1024]{2,1,0:T(8,128)(2,1)S(1)}, u32[]{:S(2)}, u32[]{:S(2)}) collective-permute-start(bf16[5,16,1024]{2,1,0:T(8,128)(2,1)S(1)} %slice.20), channel_id=1, source_target_pairs={{0,224},{8,232},{16,240},{24,248},{32,0},{40,8},{48,16},{56,24},{6... | collective-permute-start | bytes 491528 | tf_op jit(solution)/shard_map/ppermute | solution.py:353
  41.5 2.8 %collective-permute-start.9 = (bf16[10,16,1024]{2,1,0:T(8,128)(2,1)S(1)}, bf16[10,16,1024]{2,1,0:T(8,128)(2,1)S(1)}, u32[]{:S(2)}, u32[]{:S(2)}) collective-permute-start(bf16[10,16,1024]{2,1,0:T(8,128)(2,1)S(1)} %get-tuple-element.40), channel_id=1, source_target_pairs={{0,24},{8,0},{16,8},{24,16},{32,56},{40,32},{48,40},{56,48},{64,88... | collective-permute-start | bytes 983048 | tf_op jit(solution)/shard_map/ppermute | solution.py:353
  44.4 2.9 %collective-permute-done.12.refs_2_ = bf16[5,16,1024]{2,1,0:T(8,128)(2,1)S(1)} collective-permute-done((bf16[5,16,1024]{2,1,0:T(8,128)(2,1)S(1)}, bf16[5,16,1024]{2,1,0:T(8,128)(2,1)S(1)}, u32[]{:S(2)}, u32[]{:S(2)}) %collective-permute-start.12) | collective-permute-done | bytes 163872 | tf_op jit(solution)/shard_map/ppermute | solution.py:353
  52.8 4.8 %collective-permute-done.9.refs_3_ = bf16[10,16,1024]{2,1,0:T(8,128)(2,1)S(1)} collective-permute-done((bf16[10,16,1024]{2,1,0:T(8,128)(2,1)S(1)}, bf16[10,16,1024]{2,1,0:T(8,128)(2,1)S(1)}, u32[]{:S(2)}, u32[]{:S(2)}) %collective-permute-start.9) | collective-permute-done | bytes 327712 | tf_op jit(solution)/shard_map/ppermute | solution.py:353
  58.4 3.5 %collective-permute-done.16.refs_7_ = bf16[6,16,1024]{2,1,0:T(8,128)(2,1)S(1)} collective-permute-done((bf16[6,16,1024]{2,1,0:T(8,128)(2,1)S(1)}, bf16[6,16,1024]{2,1,0:T(8,128)(2,1)S(1)}, u32[]{:S(2)}, u32[]{:S(2)}) %collective-permute-start.16) | collective-permute-done | bytes 196640 | tf_op jit(solution)/shard_map/ppermute | solution.py:353
  63.8 4.3 %fetch.1 = (bf16[2048,1024]{1,0:T(8,128)(2,1)S(1)}, bf16[2048,1024]{1,0:T(8,128)(2,1)S(1)}, bf16[704,1024]{1,0:T(8,128)(2,1)S(1)}, bf16[704,1024]{1,0:T(8,128)(2,1)S(1)}) custom-call(bf16[2048,1024]{1,0:T(8,128)(2,1)} %refs_0_.3, bf16[2048,1024]{1,0:T(8,128)(2,1)} %refs_1_.1, bf16[704,1024]{1,0:T(8,128)(2,1)} %refs_2_.1, bf16[704,1024]{1,0:T(8,128)(2,1)} %refs_3_.1), custom_call_target="tpu_custom_call" | custom-call | tf_op jit(solution)/shard_map/fetch/pallas_call | solution.py:228
  68.1 12.3 %core_step.1 = (bf16[704,1024]{1,0:T(8,128)(2,1)}, f32[352,1024]{1,0:T(8,128)S(1)}, bf16[352,1024]{1,0:T(8,128)(2,1)S(1)}) custom-call(s32[3]{0:T(128)S(1)} %pad_add_fusion.1.p_ref, bf16[352,1024]{1,0:T(8,128)(2,1)S(1)} %bitcast.17, bf16[352,1024]{1,0:T(8,128)(2,1)S(1)} %bitcast.18, bf16[2048,1024]{1,0:T(8,128)(2,1)S(1)} %get-tuple-element.45.wk_ref, ...), custom_call_target="tpu_custom_call" | custom-call | tf_op jit(solution)/shard_map/core_step/pallas_call | solution.py:300
  83.5 2.6 %collective-permute-start.25 = (bf16[2,16,1024]{2,1,0:T(8,128)(2,1)S(1)}, bf16[2,16,1024]{2,1,0:T(8,128)(2,1)S(1)}, u32[]{:S(2)}, u32[]{:S(2)}) collective-permute-start(bf16[2,16,1024]{2,1,0:T(8,128)(2,1)S(1)} %get-tuple-element.61), channel_id=1, source_target_pairs={{0,24},{8,0},{16,8},{24,16},{32,56},{40,32},{48,40},{56,48},{64,88... | collective-permute-start | bytes 196616 | tf_op jit(solution)/shard_map/ppermute | solution.py:353
  90.1 3.6 %collective-permute-start.26 = (bf16[2,16,1024]{2,1,0:T(8,128)(2,1)S(1)}, bf16[2,16,1024]{2,1,0:T(8,128)(2,1)S(1)}, u32[]{:S(2)}, u32[]{:S(2)}) collective-permute-start(bf16[2,16,1024]{2,1,0:T(8,128)(2,1)S(1)} %get-tuple-element.62), channel_id=1, source_target_pairs={{0,16},{8,24},{16,0},{24,8},{32,48},{40,56},{48,32},{56,40},{64,80... | collective-permute-start | bytes 196616 | tf_op jit(solution)/shard_map/ppermute | solution.py:353
  93.7 12.0 %collective-permute-done.26.refs_2_ = bf16[2,16,1024]{2,1,0:T(8,128)(2,1)S(1)} collective-permute-done((bf16[2,16,1024]{2,1,0:T(8,128)(2,1)S(1)}, bf16[2,16,1024]{2,1,0:T(8,128)(2,1)S(1)}, u32[]{:S(2)}, u32[]{:S(2)}) %collective-permute-start.26) | collective-permute-done | bytes 65568 | tf_op jit(solution)/shard_map/ppermute | solution.py:353
  107.1 3.2 %collective-permute-start.29 = (bf16[5,16,1024]{2,1,0:T(8,128)(2,1)S(1)}, bf16[5,16,1024]{2,1,0:T(8,128)(2,1)S(1)}, u32[]{:S(2)}, u32[]{:S(2)}) collective-permute-start(bf16[5,16,1024]{2,1,0:T(8,128)(2,1)S(1)} %get-tuple-element.65), channel_id=1, source_target_pairs={{0,224},{8,232},{16,240},{24,248},{32,0},{40,8},{48,16},{56,24},{6... | collective-permute-start | bytes 491528 | tf_op jit(solution)/shard_map/ppermute | solution.py:353
  110.3 4.1 %collective-permute-done.28.refs_4_ = bf16[5,16,1024]{2,1,0:T(8,128)(2,1)S(1)} collective-permute-done((bf16[5,16,1024]{2,1,0:T(8,128)(2,1)S(1)}, bf16[5,16,1024]{2,1,0:T(8,128)(2,1)S(1)}, u32[]{:S(2)}, u32[]{:S(2)}) %collective-permute-start.28) | collective-permute-done | bytes 163872 | tf_op jit(solution)/shard_map/ppermute | solution.py:353
  115.6 3.2 %collective-permute-start.31 = (bf16[10,16,1024]{2,1,0:T(8,128)(2,1)S(1)}, bf16[10,16,1024]{2,1,0:T(8,128)(2,1)S(1)}, u32[]{:S(2)}, u32[]{:S(2)}) collective-permute-start(bf16[10,16,1024]{2,1,0:T(8,128)(2,1)S(1)} %get-tuple-element.67), channel_id=1, source_target_pairs={{0,224},{8,232},{16,240},{24,248},{32,0},{40,8},{48,16},{56,24},{6... | collective-permute-start | bytes 983048 | tf_op jit(solution)/shard_map/ppermute | solution.py:353
  118.8 6.7 %collective-permute-done.30.refs_4_ = bf16[10,16,1024]{2,1,0:T(8,128)(2,1)S(1)} collective-permute-done((bf16[10,16,1024]{2,1,0:T(8,128)(2,1)S(1)}, bf16[10,16,1024]{2,1,0:T(8,128)(2,1)S(1)}, u32[]{:S(2)}, u32[]{:S(2)}) %collective-permute-start.30) | collective-permute-done | bytes 327712 | tf_op jit(solution)/shard_map/ppermute | solution.py:353
  126.6 3.2 %collective-permute-start.33 = (bf16[10,16,1024]{2,1,0:T(8,128)(2,1)S(1)}, bf16[10,16,1024]{2,1,0:T(8,128)(2,1)S(1)}, u32[]{:S(2)}, u32[]{:S(2)}) collective-permute-start(bf16[10,16,1024]{2,1,0:T(8,128)(2,1)S(1)} %get-tuple-element.69), channel_id=1, source_target_pairs={{0,224},{8,232},{16,240},{24,248},{32,0},{40,8},{48,16},{56,24},{6... | collective-permute-start | bytes 983048 | tf_op jit(solution)/shard_map/ppermute | solution.py:353
  133.3 4.4 %collective-permute-done.19.refs_1_ = bf16[6,16,1024]{2,1,0:T(8,128)(2,1)S(1)} collective-permute-done((bf16[6,16,1024]{2,1,0:T(8,128)(2,1)S(1)}, bf16[6,16,1024]{2,1,0:T(8,128)(2,1)S(1)}, u32[]{:S(2)}, u32[]{:S(2)}) %collective-permute-start.19) | collective-permute-done | bytes 196640 | tf_op jit(solution)/shard_map/ppermute | solution.py:353
  142.4 3.2 %collective-permute-start.35 = (bf16[10,16,1024]{2,1,0:T(8,128)(2,1)S(1)}, bf16[10,16,1024]{2,1,0:T(8,128)(2,1)S(1)}, u32[]{:S(2)}, u32[]{:S(2)}) collective-permute-start(bf16[10,16,1024]{2,1,0:T(8,128)(2,1)S(1)} %get-tuple-element.71), channel_id=1, source_target_pairs={{0,224},{8,232},{16,240},{24,248},{32,0},{40,8},{48,16},{56,24},{6... | collective-permute-start | bytes 983048 | tf_op jit(solution)/shard_map/ppermute | solution.py:353
  145.7 6.0 %collective-permute-done.34.refs_4_ = bf16[10,16,1024]{2,1,0:T(8,128)(2,1)S(1)} collective-permute-done((bf16[10,16,1024]{2,1,0:T(8,128)(2,1)S(1)}, bf16[10,16,1024]{2,1,0:T(8,128)(2,1)S(1)}, u32[]{:S(2)}, u32[]{:S(2)}) %collective-permute-start.34) | collective-permute-done | bytes 327712 | tf_op jit(solution)/shard_map/ppermute | solution.py:353
  (83 shorter events, 38.9 us)
Async XLA Ops:
  1.5 11.9 %collective-permute-start.2 = (s32[1,22]{1,0:T(1,128)S(1)}, s32[1,22]{1,0:T(1,128)S(1)}, u32[]{:S(2)}, u32[]{:S(2)}) collective-permute-start(s32[1,22]{1,0:T(1,128)S(1)} %reshape.419), channel_id=1, source_target_pairs={{0,8},{8,16},{16,24},{24,0},{32,40},{40,48},{48,56},{56,32},{64,72... | collective-permute-start | bytes 272 | tf_op jit(solution)/shard_map/ppermute | solution.py:353
  3.1 10.2 %collective-permute-start.1 = (s32[1,22]{1,0:T(1,128)S(1)}, s32[1,22]{1,0:T(1,128)S(1)}, u32[]{:S(2)}, u32[]{:S(2)}) collective-permute-start(s32[1,22]{1,0:T(1,128)S(1)} %reshape.419), channel_id=1, source_target_pairs={{0,16},{8,24},{16,0},{24,8},{32,48},{40,56},{48,32},{56,40},{64,80... | collective-permute-start | bytes 272 | tf_op jit(solution)/shard_map/ppermute | solution.py:353
  7.4 12.3 %collective-permute-start.3 = (bf16[10,16,1024]{2,1,0:T(8,128)(2,1)}, bf16[10,16,1024]{2,1,0:T(8,128)(2,1)S(1)}, u32[]{:S(2)}, u32[]{:S(2)}) collective-permute-start(bf16[10,16,1024]{2,1,0:T(8,128)(2,1)} %refs_0_.2), channel_id=1, source_target_pairs={{0,224},{8,232},{16,240},{24,248},{32,0},{40,8},{48,16},{56,24},{6... | collective-permute-start | bytes 983048 | tf_op jit(solution)/shard_map/ppermute | solution.py:353
  13.2 10.0 %collective-permute-start.4 = (bf16[10,16,1024]{2,1,0:T(8,128)(2,1)}, bf16[10,16,1024]{2,1,0:T(8,128)(2,1)S(1)}, u32[]{:S(2)}, u32[]{:S(2)}) collective-permute-start(bf16[10,16,1024]{2,1,0:T(8,128)(2,1)} %refs_0_.2), channel_id=1, source_target_pairs={{0,32},{8,40},{16,48},{24,56},{32,64},{40,72},{48,80},{56,88},{64,... | collective-permute-start | bytes 983048 | tf_op jit(solution)/shard_map/ppermute | solution.py:353
  23.3 9.0 %collective-permute-start.6 = (bf16[10,16,1024]{2,1,0:T(8,128)(2,1)S(1)}, bf16[10,16,1024]{2,1,0:T(8,128)(2,1)S(1)}, u32[]{:S(2)}, u32[]{:S(2)}) collective-permute-start(bf16[10,16,1024]{2,1,0:T(8,128)(2,1)S(1)} %collective-permute-done.4.refs_2_), channel_id=1, source_target_pairs={{0,32},{8,40},{16,48},{24,56},{32,64},{40,72},{48,80},{56,88},{64,... | collective-permute-start | bytes 983048 | tf_op jit(solution)/shard_map/ppermute | solution.py:353
  34.1 16.2 %collective-permute-start.7 = (bf16[10,16,1024]{2,1,0:T(8,128)(2,1)S(1)}, bf16[10,16,1024]{2,1,0:T(8,128)(2,1)S(1)}, u32[]{:S(2)}, u32[]{:S(2)}) collective-permute-start(bf16[10,16,1024]{2,1,0:T(8,128)(2,1)S(1)} %get-tuple-element.38), channel_id=1, source_target_pairs={{0,8},{8,16},{16,24},{24,0},{32,40},{40,48},{48,56},{56,32},{64,72... | collective-permute-start | bytes 983048 | tf_op jit(solution)/shard_map/ppermute | solution.py:353
  40.8 12.0 %collective-permute-start.8 = (bf16[10,16,1024]{2,1,0:T(8,128)(2,1)S(1)}, bf16[10,16,1024]{2,1,0:T(8,128)(2,1)S(1)}, u32[]{:S(2)}, u32[]{:S(2)}) collective-permute-start(bf16[10,16,1024]{2,1,0:T(8,128)(2,1)S(1)} %get-tuple-element.39), channel_id=1, source_target_pairs={{0,16},{8,24},{16,0},{24,8},{32,48},{40,56},{48,32},{56,40},{64,80... | collective-permute-start | bytes 983048 | tf_op jit(solution)/shard_map/ppermute | solution.py:353
  41.5 16.2 %collective-permute-start.9 = (bf16[10,16,1024]{2,1,0:T(8,128)(2,1)S(1)}, bf16[10,16,1024]{2,1,0:T(8,128)(2,1)S(1)}, u32[]{:S(2)}, u32[]{:S(2)}) collective-permute-start(bf16[10,16,1024]{2,1,0:T(8,128)(2,1)S(1)} %get-tuple-element.40), channel_id=1, source_target_pairs={{0,24},{8,0},{16,8},{24,16},{32,56},{40,32},{48,40},{56,48},{64,88... | collective-permute-start | bytes 983048 | tf_op jit(solution)/shard_map/ppermute | solution.py:353
  48.1 10.2 %collective-permute-start.14 = (bf16[6,16,1024]{2,1,0:T(8,128)(2,1)S(1)}, bf16[6,16,1024]{2,1,0:T(8,128)(2,1)S(1)}, u32[]{:S(2)}, u32[]{:S(2)}) collective-permute-start(bf16[6,16,1024]{2,1,0:T(8,128)(2,1)S(1)} %get-tuple-element.42), channel_id=1, source_target_pairs={{0,8},{8,16},{16,24},{24,0},{32,40},{40,48},{48,56},{56,32},{64,72... | collective-permute-start | bytes 589832 | tf_op jit(solution)/shard_map/ppermute | solution.py:353
  48.9 9.5 %collective-permute-start.15 = (bf16[6,16,1024]{2,1,0:T(8,128)(2,1)S(1)}, bf16[6,16,1024]{2,1,0:T(8,128)(2,1)S(1)}, u32[]{:S(2)}, u32[]{:S(2)}) collective-permute-start(bf16[6,16,1024]{2,1,0:T(8,128)(2,1)S(1)} %get-tuple-element.43), channel_id=1, source_target_pairs={{0,16},{8,24},{16,0},{24,8},{32,48},{40,56},{48,32},{56,40},{64,80... | collective-permute-start | bytes 589832 | tf_op jit(solution)/shard_map/ppermute | solution.py:353
  50.3 11.6 %collective-permute-start.16 = (bf16[6,16,1024]{2,1,0:T(8,128)(2,1)S(1)}, bf16[6,16,1024]{2,1,0:T(8,128)(2,1)S(1)}, u32[]{:S(2)}, u32[]{:S(2)}) collective-permute-start(bf16[6,16,1024]{2,1,0:T(8,128)(2,1)S(1)} %get-tuple-element.44), channel_id=1, source_target_pairs={{0,24},{8,0},{16,8},{24,16},{32,56},{40,32},{48,40},{56,48},{64,88... | collective-permute-start | bytes 589832 | tf_op jit(solution)/shard_map/ppermute | solution.py:353
  83.5 10.1 %collective-permute-start.25 = (bf16[2,16,1024]{2,1,0:T(8,128)(2,1)S(1)}, bf16[2,16,1024]{2,1,0:T(8,128)(2,1)S(1)}, u32[]{:S(2)}, u32[]{:S(2)}) collective-permute-start(bf16[2,16,1024]{2,1,0:T(8,128)(2,1)S(1)} %get-tuple-element.61), channel_id=1, source_target_pairs={{0,24},{8,0},{16,8},{24,16},{32,56},{40,32},{48,40},{56,48},{64,88... | collective-permute-start | bytes 196616 | tf_op jit(solution)/shard_map/ppermute | solution.py:353
  87.4 27.0 %collective-permute-start.22 = (bf16[8,16,1024]{2,1,0:T(8,128)(2,1)S(1)}, bf16[8,16,1024]{2,1,0:T(8,128)(2,1)S(1)}, u32[]{:S(2)}, u32[]{:S(2)}) collective-permute-start(bf16[8,16,1024]{2,1,0:T(8,128)(2,1)S(1)} %get-tuple-element.57), channel_id=1, source_target_pairs={{0,24},{8,0},{16,8},{24,16},{32,56},{40,32},{48,40},{56,48},{64,88... | collective-permute-start | bytes 786440 | tf_op jit(solution)/shard_map/ppermute | solution.py:353
  88.3 26.2 %collective-permute-start.23 = (bf16[8,16,1024]{2,1,0:T(8,128)(2,1)S(1)}, bf16[8,16,1024]{2,1,0:T(8,128)(2,1)S(1)}, u32[]{:S(2)}, u32[]{:S(2)}) collective-permute-start(bf16[8,16,1024]{2,1,0:T(8,128)(2,1)S(1)} %get-tuple-element.58), channel_id=1, source_target_pairs={{0,16},{8,24},{16,0},{24,8},{32,48},{40,56},{48,32},{56,40},{64,80... | collective-permute-start | bytes 786440 | tf_op jit(solution)/shard_map/ppermute | solution.py:353
  89.0 25.4 %collective-permute-start.24 = (bf16[8,16,1024]{2,1,0:T(8,128)(2,1)S(1)}, bf16[8,16,1024]{2,1,0:T(8,128)(2,1)S(1)}, u32[]{:S(2)}, u32[]{:S(2)}) collective-permute-start(bf16[8,16,1024]{2,1,0:T(8,128)(2,1)S(1)} %get-tuple-element.59), channel_id=1, source_target_pairs={{0,8},{8,16},{16,24},{24,0},{32,40},{40,48},{48,56},{56,32},{64,72... | collective-permute-start | bytes 786440 | tf_op jit(solution)/shard_map/ppermute | solution.py:353
  90.1 15.5 %collective-permute-start.26 = (bf16[2,16,1024]{2,1,0:T(8,128)(2,1)S(1)}, bf16[2,16,1024]{2,1,0:T(8,128)(2,1)S(1)}, u32[]{:S(2)}, u32[]{:S(2)}) collective-permute-start(bf16[2,16,1024]{2,1,0:T(8,128)(2,1)S(1)} %get-tuple-element.62), channel_id=1, source_target_pairs={{0,16},{8,24},{16,0},{24,8},{32,48},{40,56},{48,32},{56,40},{64,80... | collective-permute-start | bytes 196616 | tf_op jit(solution)/shard_map/ppermute | solution.py:353
  93.7 12.5 %collective-permute-start.27 = (bf16[2,16,1024]{2,1,0:T(8,128)(2,1)S(1)}, bf16[2,16,1024]{2,1,0:T(8,128)(2,1)S(1)}, u32[]{:S(2)}, u32[]{:S(2)}) collective-permute-start(bf16[2,16,1024]{2,1,0:T(8,128)(2,1)S(1)} %get-tuple-element.63), channel_id=1, source_target_pairs={{0,8},{8,16},{16,24},{24,0},{32,40},{40,48},{48,56},{56,32},{64,72... | collective-permute-start | bytes 196616 | tf_op jit(solution)/shard_map/ppermute | solution.py:353
  115.5 10.1 %collective-permute-start.30 = (bf16[10,16,1024]{2,1,0:T(8,128)(2,1)S(1)}, bf16[10,16,1024]{2,1,0:T(8,128)(2,1)S(1)}, u32[]{:S(2)}, u32[]{:S(2)}) collective-permute-start(bf16[10,16,1024]{2,1,0:T(8,128)(2,1)S(1)} %get-tuple-element.66), channel_id=1, source_target_pairs={{0,32},{8,40},{16,48},{24,56},{32,64},{40,72},{48,80},{56,88},{64,... | collective-permute-start | bytes 983048 | tf_op jit(solution)/shard_map/ppermute | solution.py:353
  115.6 9.9 %collective-permute-start.31 = (bf16[10,16,1024]{2,1,0:T(8,128)(2,1)S(1)}, bf16[10,16,1024]{2,1,0:T(8,128)(2,1)S(1)}, u32[]{:S(2)}, u32[]{:S(2)}) collective-permute-start(bf16[10,16,1024]{2,1,0:T(8,128)(2,1)S(1)} %get-tuple-element.67), channel_id=1, source_target_pairs={{0,224},{8,232},{16,240},{24,248},{32,0},{40,8},{48,16},{56,24},{6... | collective-permute-start | bytes 983048 | tf_op jit(solution)/shard_map/ppermute | solution.py:353
  126.5 14.8 %collective-permute-start.32 = (bf16[10,16,1024]{2,1,0:T(8,128)(2,1)S(1)}, bf16[10,16,1024]{2,1,0:T(8,128)(2,1)S(1)}, u32[]{:S(2)}, u32[]{:S(2)}) collective-permute-start(bf16[10,16,1024]{2,1,0:T(8,128)(2,1)S(1)} %get-tuple-element.68), channel_id=1, source_target_pairs={{0,32},{8,40},{16,48},{24,56},{32,64},{40,72},{48,80},{56,88},{64,... | collective-permute-start | bytes 983048 | tf_op jit(solution)/shard_map/ppermute | solution.py:353
  126.6 14.7 %collective-permute-start.33 = (bf16[10,16,1024]{2,1,0:T(8,128)(2,1)S(1)}, bf16[10,16,1024]{2,1,0:T(8,128)(2,1)S(1)}, u32[]{:S(2)}, u32[]{:S(2)}) collective-permute-start(bf16[10,16,1024]{2,1,0:T(8,128)(2,1)S(1)} %get-tuple-element.69), channel_id=1, source_target_pairs={{0,224},{8,232},{16,240},{24,248},{32,0},{40,8},{48,16},{56,24},{6... | collective-permute-start | bytes 983048 | tf_op jit(solution)/shard_map/ppermute | solution.py:353
  132.0 9.4 %collective-permute-start.21 = (bf16[6,16,1024]{2,1,0:T(8,128)(2,1)S(1)}, bf16[6,16,1024]{2,1,0:T(8,128)(2,1)S(1)}, u32[]{:S(2)}, u32[]{:S(2)}) collective-permute-start(bf16[6,16,1024]{2,1,0:T(8,128)(2,1)S(1)} %get-tuple-element.55), channel_id=1, source_target_pairs={{0,8},{8,16},{16,24},{24,0},{32,40},{40,48},{48,56},{56,32},{64,72... | collective-permute-start | bytes 589832 | tf_op jit(solution)/shard_map/ppermute | solution.py:353
  142.3 9.4 %collective-permute-start.34 = (bf16[10,16,1024]{2,1,0:T(8,128)(2,1)S(1)}, bf16[10,16,1024]{2,1,0:T(8,128)(2,1)S(1)}, u32[]{:S(2)}, u32[]{:S(2)}) collective-permute-start(bf16[10,16,1024]{2,1,0:T(8,128)(2,1)S(1)} %get-tuple-element.70), channel_id=1, source_target_pairs={{0,32},{8,40},{16,48},{24,56},{32,64},{40,72},{48,80},{56,88},{64,... | collective-permute-start | bytes 983048 | tf_op jit(solution)/shard_map/ppermute | solution.py:353
  142.4 9.3 %collective-permute-start.35 = (bf16[10,16,1024]{2,1,0:T(8,128)(2,1)S(1)}, bf16[10,16,1024]{2,1,0:T(8,128)(2,1)S(1)}, u32[]{:S(2)}, u32[]{:S(2)}) collective-permute-start(bf16[10,16,1024]{2,1,0:T(8,128)(2,1)S(1)} %get-tuple-element.71), channel_id=1, source_target_pairs={{0,224},{8,232},{16,240},{24,248},{32,0},{40,8},{48,16},{56,24},{6... | collective-permute-start | bytes 983048 | tf_op jit(solution)/shard_map/ppermute | solution.py:353
  (13 other events, 84.6 us)

commit v3 on v2

--- a/solution.py
+++ b/solution.py
@@ -22,7 +22,7 @@
 F32 = jnp.float32
 
 OUT = ((0, 1, 2), (3, 4))
-BACK = ((4,), (3, 2), (1, 0))
+BACK = ((4,), (3,), (2,), (1, 0))
 
 
 def planes_of(step, nz):
@@ -31,8 +31,18 @@
     return (step, nz - step)
 
 
+def span_of(phase, nz):
+    planes = sorted((d + nz // 2 - 1) % nz - (nz // 2 - 1) for t in phase for d in planes_of(t, nz))
+    if nz // 2 - 1 in planes or nz // 2 in planes:
+        planes = sorted(d % nz for d in planes)
+    stride = planes[1] - planes[0] if len(planes) > 1 else 1
+    assert planes == [planes[0] + stride * n for n in range(len(planes))]
+    return planes[0], stride, len(planes)
+
+
 def slots_of(phase, nz):
-    return [(d, s) for step in phase for d in planes_of(step, nz) for s in range(CAP)]
+    first, stride, count = span_of(phase, nz)
+    return [((first + stride * n) % nz, s) for n in range(count) for s in range(CAP)]
 
 
 def ring(seq, dz, dy):
@@ -87,13 +97,20 @@
     def body(r_ref, p_ref, *refs):
         ins, out = refs[:-1], refs[-1]
         for n, phase in enumerate(OUT):
+            first, stride, count = span_of(phase, nz)
             for j in range(NY):
-                for k, (d, s) in enumerate(slots_of(phase, nz)):
-                    r = r_ref[j, (p_ref[0] + d) % nz * CAP + s]
+
+                def place_one(k, carry):
+                    plane = (p_ref[0] + nz + first + stride * (k // CAP)) % nz
+                    r = r_ref[j, plane * CAP + k % CAP]
 
                     @pl.when(r >= 0)
                     def _():
                         out[jnp.maximum(r, 0)] = ins[n * NY + j][k]
+
+                    return carry
+
+                lax.fori_loop(0, count * CAP, place_one, 0, unroll=2)
 
     return pl.pallas_call(
         body,
@@ -108,17 +125,24 @@
 def spread(ref_of, place, own, other, phase, nz):
     tail = own.shape[1:]
     slots = slots_of(phase, nz)
+    first, stride, _ = span_of(phase, nz)
 
     def body(r_ref, p_ref, own_ref, other_ref, *outs):
         for j in range(NY):
-            for k, (d, s) in enumerate(slots):
-                r = r_ref[j, (p_ref[0] + d) % nz * CAP + s]
+
+            def place_one(k, carry):
+                plane = (p_ref[0] + nz + first + stride * (k // CAP)) % nz
+                r = r_ref[j, plane * CAP + k % CAP]
 
                 @pl.when(r >= 0)
                 def _():
                     at = jnp.maximum(r, 0)
                     total = own_ref[at] + other_ref[at].astype(F32)
                     outs[j][k] = total.astype(BF)
+
+                return carry
+
+            lax.fori_loop(0, len(slots), place_one, 0, unroll=2)
 
     return pl.pallas_call(
         body,
@@ -236,8 +260,48 @@
     )(*arrays)
 
 
-def core_step(place, own, other, key_weight, value_weight, queries, out_grad, spans, head_size):
+def project_own(place, own, key_weight, value_weight):
     rows, half = own.shape
+
+    def body(p_ref, own_ref, wk_ref, wv_ref, k_ref, v_ref):
+        mine = pl.ds(pl.multiple_of(p_ref[2] * half, half), half)
+        for w_ref, out in ((wk_ref, k_ref), (wv_ref, v_ref)):
+            out[...] = jnp.dot(own_ref[...], w_ref[mine, :], preferred_element_type=F32)
+
+    return pl.pallas_call(
+        body,
+        in_specs=[SMEM] + [VMEM] * 3,
+        out_specs=[VMEM] * 2,
+        out_shape=[jax.ShapeDtypeStruct((rows, half), F32)] * 2,
+        compiler_params=SMALL,
+        name="project_own",
+    )(place, own, key_weight, value_weight)
+
+
+def return_own(place, key_grad, value_grad, key_weight, value_weight):
+    rows, half = key_grad.shape
+    nt = (((1,), (1,)), ((), ()))
+
+    def body(p_ref, dk_ref, dv_ref, wk_ref, wv_ref, out):
+        mine = pl.ds(pl.multiple_of(p_ref[2] * half, half), half)
+        total = lax.dot_general(dk_ref[...], wk_ref[mine, :], nt, preferred_element_type=F32)
+        total += lax.dot_general(dv_ref[...], wv_ref[mine, :], nt, preferred_element_type=F32)
+        out[...] = total
+
+    return pl.pallas_call(
+        body,
+        in_specs=[SMEM] + [VMEM] * 4,
+        out_specs=VMEM,
+        out_shape=jax.ShapeDtypeStruct((rows, half), F32),
+        compiler_params=SMALL,
+        name="return_own",
+    )(place, key_grad, value_grad, key_weight, value_weight)
+
+
+def core_step(
+    place, key_part, value_part, other, key_weight, value_weight, queries, out_grad, spans, head_size
+):
+    rows, half = other.shape
     tok = queries.shape[0] // spans
     per = rows // spans
     heads = half // head_size
@@ -247,30 +311,31 @@
     cols = [slice(n * head_size, (n + 1) * head_size) for n in range(heads)]
 
     def body(
-        p_ref, own_ref, oth_ref, wk_ref, wv_ref, q_ref, g_ref, dq_hbm, pown_ref, poth_ref,
-        dq_ref, k_ref, v_ref, dk_ref, dv_ref, sem,
+        p_ref, ka_ref, va_ref, oth_ref, wk_ref, wv_ref, q_ref, g_ref,
+        dq_hbm, poth_ref, dk_ref, dv_ref, dq_ref, k_ref, v_ref, sem,
     ):
-        mine = pl.ds(pl.multiple_of(p_ref[2] * half, half), half)
         theirs = pl.ds(pl.multiple_of((1 - p_ref[2]) * half, half), half)
-        for w_ref, out in ((wk_ref, k_ref), (wv_ref, v_ref)):
-            total = jnp.dot(own_ref[...], w_ref[mine, :], preferred_element_type=F32)
-            total += jnp.dot(oth_ref[...], w_ref[theirs, :], preferred_element_type=F32)
-            out[...] = total.astype(BF)
-
-        def span(u, carry):
-            here = pl.ds(pl.multiple_of(u * per, per), per)
-            there = pl.ds(pl.multiple_of(u * tok, tok), tok)
-            q = [q_ref[there, c] for c in cols]
-            g = [g_ref[there, c] for c in cols]
-            k = [k_ref[here, c] for c in cols]
-            v = [v_ref[here, c] for c in cols]
+        for part, w_ref, out in ((ka_ref, wk_ref, k_ref), (va_ref, wv_ref, v_ref)):
+            total = jnp.dot(oth_ref[...], w_ref[theirs, :], preferred_element_type=F32)
+            out[...] = (part[...] + total).astype(BF)
+
+        def at(u):
+            return (
+                pl.ds(pl.multiple_of(u * per, per), per),
+                pl.ds(pl.multiple_of(u * tok, tok), tok),
+            )
+
+        def weigh(u):
+            here, there = at(u)
+            probs_b, ds = [], []
             scores = [
-                lax.dot_general(a, b, nt, preferred_element_type=F32) for a, b in zip(k, q)
+                lax.dot_general(k_ref[here, c], q_ref[there, c], nt, preferred_element_type=F32)
+                for c in cols
             ]
             dprobs = [
-                lax.dot_general(a, b, nt, preferred_element_type=F32) for a, b in zip(v, g)
+                lax.dot_general(v_ref[here, c], g_ref[there, c], nt, preferred_element_type=F32)
+                for c in cols
             ]
-            probs_b, ds = [], []
             for sc, dp in zip(scores, dprobs):
                 sc = sc * scaling
                 raised = jnp.exp(sc - jnp.max(sc, axis=0, keepdims=True))
@@ -279,39 +344,46 @@
                 delta = jnp.sum(pb.astype(F32) * dp, axis=0, keepdims=True)
                 probs_b.append(pb)
                 ds.append((probs * (dp - delta)).astype(BF))
+            return tuple(probs_b), tuple(ds)
+
+        def grads(u, probs_b, ds):
+            here, there = at(u)
             for n, c in enumerate(cols):
-                dk = jnp.dot(ds[n], q[n], preferred_element_type=F32) * scaling
-                dv = jnp.dot(probs_b[n], g[n], preferred_element_type=F32)
-                dq = lax.dot_general(ds[n], k[n], tn, preferred_element_type=F32) * scaling
+                q, g, k = q_ref[there, c], g_ref[there, c], k_ref[here, c]
+                dk = jnp.dot(ds[n], q, preferred_element_type=F32) * scaling
+                dv = jnp.dot(probs_b[n], g, preferred_element_type=F32)
+                dq = lax.dot_general(ds[n], k, tn, preferred_element_type=F32) * scaling
                 dk_ref[here, c] = dk.astype(BF)
                 dv_ref[here, c] = dv.astype(BF)
                 dq_ref[there, c] = dq.astype(BF)
-            return carry
-
-        lax.fori_loop(0, spans, span, 0)
+
+        def both(u, carry):
+            after = weigh(u + 1)
+            grads(u, *carry)
+            return after
+
+        grads(spans - 1, *lax.fori_loop(0, spans - 1, both, weigh(0)))
         store = pltpu.make_async_copy(dq_ref, dq_hbm, sem.at[0])
         store.start()
-        for at, out in ((theirs, poth_ref), (mine, pown_ref)):
-            total = lax.dot_general(dk_ref[...], wk_ref[at, :], nt, preferred_element_type=F32)
-            total += lax.dot_general(dv_ref[...], wv_ref[at, :], nt, preferred_element_type=F32)
-            out[...] = total.astype(out.dtype)
+        total = lax.dot_general(dk_ref[...], wk_ref[theirs, :], nt, preferred_element_type=F32)
+        total += lax.dot_general(dv_ref[...], wv_ref[theirs, :], nt, preferred_element_type=F32)
+        poth_ref[...] = total.astype(BF)
         store.wait()
 
     return pl.pallas_call(
         body,
-        in_specs=[SMEM, VMEM, VMEM, VMEM, VMEM, VMEM, VMEM],
-        out_specs=[ANY, VMEM, VMEM],
+        in_specs=[SMEM] + [VMEM] * 7,
+        out_specs=[ANY] + [VMEM] * 3,
         compiler_params=pltpu.CompilerParams(vmem_limit_bytes=16 << 20),
         out_shape=[
             jax.ShapeDtypeStruct(queries.shape, BF),
-            jax.ShapeDtypeStruct((rows, half), F32),
-            jax.ShapeDtypeStruct((rows, half), BF),
-        ],
+        ]
+        + [jax.ShapeDtypeStruct((rows, half), BF)] * 3,
         scratch_shapes=[pltpu.VMEM(queries.shape, BF)]
-        + [pltpu.VMEM((rows, half), BF)] * 4
+        + [pltpu.VMEM((rows, half), BF)] * 2
         + [pltpu.SemaphoreType.DMA((1,))],
         name="core_step",
-    )(place, own, other, key_weight, value_weight, queries, out_grad)
+    )(place, key_part, value_part, other, key_weight, value_weight, queries, out_grad)
 
 
 def slot_tables(ids, y0, nz, rows_here):
@@ -362,7 +434,7 @@
     readers = None
     for step in range(1, far + 1):
         if step == far:
-            ahead, behind = ahead[cut:], behind[:cut]
+            ahead, behind = lax.optimization_barrier((ahead[cut:], behind[:cut]))
         behind = move(behind, 1, 0)
         ahead = move(ahead, -1, 0)
         if step == far:
@@ -371,17 +443,15 @@
             blocks[step], blocks[nz - step] = [ahead], [behind]
         if readers is None:
             ids = neighbours.reshape(1, ref_count)
-            readers = [ids] + [move(ids, 0, -j) for j in range(1, NY)]
-            table, ref_of = slot_tables(jnp.concatenate(readers, axis=0), y0, nz, rows_here)
+            two = jnp.concatenate([ids, move(ids, 0, -1)], axis=0)
+            readers = jnp.concatenate([two, move(two, 0, -2)], axis=0)
+            table, ref_of = slot_tables(readers, y0, nz, rows_here)
     groups = []
     for phase in OUT:
         need = {d: blocks[d] for step in phase for d in planes_of(step, nz)}
         picked = pick_rows(table, place, need, phase, nz)
         groups.append([picked[0]] + [move(picked[j], 0, j) for j in range(1, NY)])
 
-    own = compact(ref_of, place, groups, nz, ref_count)
-    other = swap(own)
-    flat = (ref_count * length, half)
     key_weight, value_weight, queries, out_grad = (
         pltpu.with_memory_space_constraint(a, pltpu.VMEM)
         for a in fetch(
@@ -391,11 +461,16 @@
             )
         )
     )
-    query_grad, partial_own, partial_other = core_step(
-        place, own.reshape(flat), other.reshape(flat), key_weight, value_weight,
-        queries, out_grad, spans, D // HEADS,
+    flat = (ref_count * length, half)
+    own = compact(ref_of, place, groups, nz, ref_count)
+    other = swap(own)
+    parts = project_own(place, own.reshape(flat), key_weight, value_weight)
+    query_grad, partial_other, key_grad, value_grad = core_step(
+        place, *parts, other.reshape(flat), key_weight, value_weight, queries, out_grad,
+        spans, D // HEADS,
     )
     came = swap(partial_other)
+    partial_own = return_own(place, key_grad, value_grad, key_weight, value_weight)
     shape = (ref_count, length, half)
     partial_own, came = partial_own.reshape(shape), came.reshape(shape)
 

time: 154 us -> 147 us (0.955)
  waiting for transfers between devices: 65.1 us -> 56.2 us
  starting transfers between devices: 55.9 us -> 57.5 us
    ppermute x34 -> x36, waiting for transfers between devices: 63.3 us -> 56.2 us  [move(): return lax.ppermute(x, 'seq', ring(seq, dz, dy))]
    ppermute x2, waiting for transfers between devices: 1.82 us -> 0.01 us  [swap(): return lax.ppermute(x, 'head', [(0, 1), (1, 0)])]
    ppermute x34 -> x36, starting transfers between devices: 55.2 us -> 56.8 us  [move(): return lax.ppermute(x, 'seq', ring(seq, dz, dy))]
    pallas_call x3 -> x4, Pallas kernels: 3.07 us -> 4 us  [spread(): pl.pallas_call(body, in_specs=[SMEM, SMEM, VMEM, VMEM], out_specs=[VMEM]...]
    pallas_call x1 -> x3, Pallas kernels: 12.3 us -> 12.2 us  [the longest x1 7.75 us: core_step(): pl.pallas_call(body, in_specs=[SMEM] + [VMEM] * 7, out_specs=[ANY] + [VME...]
  transfers between devices with their start and end apart: 36 -> 38, of which waited for: 18 -> 22; matrix products, arithmetic and copies ran while one was open for 1% -> 1% of each run, Pallas kernels for 6% -> 9%
where the time goes in v3:
time: 147 us
  starting transfers between devices  57.5 us (39%)
  waiting for transfers between devices  56.2 us (38%)
  Pallas kernels  29.6 us (20%)
  local copies, waits for them, and re-layouts  2.03 us (1%)
    ppermute x36, starting transfers between devices, move(): return lax.ppermute(x, 'seq', ring(seq, dz, dy))  56.8 us
    ppermute x36, waiting for transfers between devices, move(): return lax.ppermute(x, 'seq', ring(seq, dz, dy))  56.2 us
    pallas_call x1, Pallas kernels, core_step(): pl.pallas_call(body, in_specs=[SMEM] + [VMEM] * 7, out_specs=[ANY] + [VME...  7.75 us
    pallas_call x5, Pallas kernels, gather_grads(): pl.pallas_call(body, in_specs=[SMEM, SMEM] + [VMEM] * (NY + len(before)),...  5.32 us
    pallas_call x1, Pallas kernels, fetch(): pl.pallas_call(body, in_specs=[pl.BlockSpec(memory_space=pltpu.HBM)] * co...  4.27 us
    pallas_call x4, Pallas kernels, spread(): pl.pallas_call(body, in_specs=[SMEM, SMEM, VMEM, VMEM], out_specs=[VMEM]...  4 us
  transfers between devices with their start and end apart: 38, of which 22 were waited for; matrix products, arithmetic and copies ran while one was open for 1% of the time, Pallas kernels for 9%

profile of v3, /device:TPU:2, one launch (start us, length us, event | category | flops | bytes accessed | tf_op | source)
XLA Modules:
  0.0 147.2 jit_solution(15063389035568996074)
XLA Ops:
  0.6 5.9 %collective-permute-start.2 = (bf16[10,16,1024]{2,1,0:T(8,128)(2,1)}, bf16[10,16,1024]{2,1,0:T(8,128)(2,1)S(1)}, u32[]{:S(2)}, u32[]{:S(2)}) collective-permute-start(bf16[10,16,1024]{2,1,0:T(8,128)(2,1)} %refs_0_.2), channel_id=1, source_target_pairs={{0,224},{8,232},{16,240},{24,248},{32,0},{40,8},{48,16},{56,24},{6... | collective-permute-start | bytes 983048 | tf_op jit(solution)/shard_map/ppermute | solution.py:425
  7.4 3.1 %collective-permute-start = (s32[1,22]{1,0:T(1,128)S(1)}, s32[1,22]{1,0:T(1,128)S(1)}, u32[]{:S(2)}, u32[]{:S(2)}) collective-permute-start(s32[1,22]{1,0:T(1,128)S(1)} %reshape.357), channel_id=1, source_target_pairs={{0,24},{8,0},{16,8},{24,16},{32,56},{40,32},{48,40},{56,48},{64,88... | collective-permute-start | bytes 272 | tf_op jit(solution)/shard_map/ppermute | solution.py:425
  11.8 2.5 %collective-permute-start.1 = (s32[2,22]{1,0:T(2,128)S(1)}, s32[2,22]{1,0:T(2,128)S(1)}, u32[]{:S(2)}, u32[]{:S(2)}) collective-permute-start(s32[2,22]{1,0:T(2,128)S(1)} %pad_add_fusion.1), channel_id=1, source_target_pairs={{0,16},{8,24},{16,0},{24,8},{32,48},{40,56},{48,32},{56,40},{64,80... | collective-permute-start | bytes 536 | tf_op jit(solution)/shard_map/ppermute | solution.py:425
  14.4 2.5 %collective-permute-done.1 = s32[2,22]{1,0:T(2,128)S(1)} collective-permute-done((s32[2,22]{1,0:T(2,128)S(1)}, s32[2,22]{1,0:T(2,128)S(1)}, u32[]{:S(2)}, u32[]{:S(2)}) %collective-permute-start.1) | collective-permute-done | bytes 208 | tf_op jit(solution)/shard_map/ppermute | solution.py:425
  17.7 3.3 %collective-permute-start.4 = (bf16[10,16,1024]{2,1,0:T(8,128)(2,1)S(1)}, bf16[10,16,1024]{2,1,0:T(8,128)(2,1)S(1)}, u32[]{:S(2)}, u32[]{:S(2)}) collective-permute-start(bf16[10,16,1024]{2,1,0:T(8,128)(2,1)S(1)} %collective-permute-done.2.refs_1_), channel_id=1, source_target_pairs={{0,224},{8,232},{16,240},{24,248},{32,0},{40,8},{48,16},{56,24},{6... | collective-permute-start | bytes 983048 | tf_op jit(solution)/shard_map/ppermute | solution.py:425
  21.0 4.6 %collective-permute-done.4.refs_3_ = bf16[10,16,1024]{2,1,0:T(8,128)(2,1)S(1)} collective-permute-done((bf16[10,16,1024]{2,1,0:T(8,128)(2,1)S(1)}, bf16[10,16,1024]{2,1,0:T(8,128)(2,1)S(1)}, u32[]{:S(2)}, u32[]{:S(2)}) %collective-permute-start.4) | collective-permute-done | bytes 327712 | tf_op jit(solution)/shard_map/ppermute | solution.py:425
  25.6 3.8 %collective-permute-start.9 = (bf16[10,16,1024]{2,1,0:T(8,128)(2,1)S(1)}, bf16[10,16,1024]{2,1,0:T(8,128)(2,1)S(1)}, u32[]{:S(2)}, u32[]{:S(2)}) collective-permute-start(bf16[10,16,1024]{2,1,0:T(8,128)(2,1)S(1)} %collective-permute-done.4.refs_3_), channel_id=1, source_target_pairs={{0,224},{8,232},{16,240},{24,248},{32,0},{40,8},{48,16},{56,24},{6... | collective-permute-start | bytes 983048 | tf_op jit(solution)/shard_map/ppermute | solution.py:425
  33.9 5.4 %collective-permute-done.10.refs_1_ = bf16[10,16,1024]{2,1,0:T(8,128)(2,1)S(1)} collective-permute-done((bf16[10,16,1024]{2,1,0:T(8,128)(2,1)S(1)}, bf16[10,16,1024]{2,1,0:T(8,128)(2,1)S(1)}, u32[]{:S(2)}, u32[]{:S(2)}) %collective-permute-start.10) | collective-permute-done | bytes 327712 | tf_op jit(solution)/shard_map/ppermute | solution.py:425
  39.4 3.2 %collective-permute-start.12 = (bf16[5,16,1024]{2,1,0:T(8,128)(2,1)S(1)}, bf16[5,16,1024]{2,1,0:T(8,128)(2,1)S(1)}, u32[]{:S(2)}, u32[]{:S(2)}) collective-permute-start(bf16[5,16,1024]{2,1,0:T(8,128)(2,1)S(1)} %slice.19), channel_id=1, source_target_pairs={{0,224},{8,232},{16,240},{24,248},{32,0},{40,8},{48,16},{56,24},{6... | collective-permute-start | bytes 491528 | tf_op jit(solution)/shard_map/ppermute | solution.py:425
  48.2 3.7 %collective-permute-start.14 = (bf16[6,16,1024]{2,1,0:T(8,128)(2,1)S(1)}, bf16[6,16,1024]{2,1,0:T(8,128)(2,1)S(1)}, u32[]{:S(2)}, u32[]{:S(2)}) collective-permute-start(bf16[6,16,1024]{2,1,0:T(8,128)(2,1)S(1)} %get-tuple-element.54), channel_id=1, source_target_pairs={{0,16},{8,24},{16,0},{24,8},{32,48},{40,56},{48,32},{56,40},{64,80... | collective-permute-start | bytes 589832 | tf_op jit(solution)/shard_map/ppermute | solution.py:425
  53.8 4.9 %collective-permute-done.8.refs_3_ = bf16[10,16,1024]{2,1,0:T(8,128)(2,1)S(1)} collective-permute-done((bf16[10,16,1024]{2,1,0:T(8,128)(2,1)S(1)}, bf16[10,16,1024]{2,1,0:T(8,128)(2,1)S(1)}, u32[]{:S(2)}, u32[]{:S(2)}) %collective-permute-start.8) | collective-permute-done | bytes 327712 | tf_op jit(solution)/shard_map/ppermute | solution.py:425
  58.7 4.3 %collective-permute-done.15.refs_7_ = bf16[6,16,1024]{2,1,0:T(8,128)(2,1)S(1)} collective-permute-done((bf16[6,16,1024]{2,1,0:T(8,128)(2,1)S(1)}, bf16[6,16,1024]{2,1,0:T(8,128)(2,1)S(1)}, u32[]{:S(2)}, u32[]{:S(2)}) %collective-permute-start.15) | collective-permute-done | bytes 196640 | tf_op jit(solution)/shard_map/ppermute | solution.py:425
  65.3 4.3 %fetch.1 = (bf16[2048,1024]{1,0:T(8,128)(2,1)S(1)}, bf16[2048,1024]{1,0:T(8,128)(2,1)S(1)}, bf16[704,1024]{1,0:T(8,128)(2,1)S(1)}, bf16[704,1024]{1,0:T(8,128)(2,1)S(1)}) custom-call(bf16[2048,1024]{1,0:T(8,128)(2,1)} %refs_0_.3, bf16[2048,1024]{1,0:T(8,128)(2,1)} %refs_1_.1, bf16[704,1024]{1,0:T(8,128)(2,1)} %refs_2_.1, bf16[704,1024]{1,0:T(8,128)(2,1)} %refs_3_.1), custom_call_target="tpu_custom_call" | custom-call | tf_op jit(solution)/shard_map/fetch/pallas_call | solution.py:252
  71.8 7.8 %core_step.1 = (bf16[704,1024]{1,0:T(8,128)(2,1)}, bf16[352,1024]{1,0:T(8,128)(2,1)S(1)}, bf16[352,1024]{1,0:T(8,128)(2,1)S(1)}, bf16[352,1024]{1,0:T(8,128)(2,1)S(1)}) custom-call(s32[3]{0:T(128)S(1)} %pad_add_fusion.2.p_ref, f32[352,1024]{1,0:T(8,128)S(1)} %get-tuple-element.58.ka_ref, f32[352,1024]{1,0:T(8,128)S(1)} %get-tuple-element.59.va_ref, ...), custom_call_target="tpu_custom_call" | custom-call | tf_op jit(solution)/shard_map/core_step/pallas_call | solution.py:373
  83.1 2.6 %collective-permute-start.27 = (bf16[2,16,1024]{2,1,0:T(8,128)(2,1)S(1)}, bf16[2,16,1024]{2,1,0:T(8,128)(2,1)S(1)}, u32[]{:S(2)}, u32[]{:S(2)}) collective-permute-start(bf16[2,16,1024]{2,1,0:T(8,128)(2,1)S(1)} %get-tuple-element.79), channel_id=1, source_target_pairs={{0,24},{8,0},{16,8},{24,16},{32,56},{40,32},{48,40},{56,48},{64,88... | collective-permute-start | bytes 196616 | tf_op jit(solution)/shard_map/ppermute | solution.py:425
  88.7 3.0 %collective-permute-done.28.refs_2_ = bf16[2,16,1024]{2,1,0:T(8,128)(2,1)S(1)} collective-permute-done((bf16[2,16,1024]{2,1,0:T(8,128)(2,1)S(1)}, bf16[2,16,1024]{2,1,0:T(8,128)(2,1)S(1)}, u32[]{:S(2)}, u32[]{:S(2)}) %collective-permute-start.28) | collective-permute-done | bytes 65568 | tf_op jit(solution)/shard_map/ppermute | solution.py:425
  93.1 3.2 %collective-permute-start.31 = (bf16[5,16,1024]{2,1,0:T(8,128)(2,1)S(1)}, bf16[5,16,1024]{2,1,0:T(8,128)(2,1)S(1)}, u32[]{:S(2)}, u32[]{:S(2)}) collective-permute-start(bf16[5,16,1024]{2,1,0:T(8,128)(2,1)S(1)} %get-tuple-element.83), channel_id=1, source_target_pairs={{0,224},{8,232},{16,240},{24,248},{32,0},{40,8},{48,16},{56,24},{6... | collective-permute-start | bytes 491528 | tf_op jit(solution)/shard_map/ppermute | solution.py:425
  107.4 3.2 %collective-permute-start.33 = (bf16[10,16,1024]{2,1,0:T(8,128)(2,1)S(1)}, bf16[10,16,1024]{2,1,0:T(8,128)(2,1)S(1)}, u32[]{:S(2)}, u32[]{:S(2)}) collective-permute-start(bf16[10,16,1024]{2,1,0:T(8,128)(2,1)S(1)} %get-tuple-element.85), channel_id=1, source_target_pairs={{0,224},{8,232},{16,240},{24,248},{32,0},{40,8},{48,16},{56,24},{6... | collective-permute-start | bytes 983048 | tf_op jit(solution)/shard_map/ppermute | solution.py:425
  114.0 2.7 %collective-permute-done.21.refs_1_ = bf16[4,16,1024]{2,1,0:T(8,128)(2,1)S(1)} collective-permute-done((bf16[4,16,1024]{2,1,0:T(8,128)(2,1)S(1)}, bf16[4,16,1024]{2,1,0:T(8,128)(2,1)S(1)}, u32[]{:S(2)}, u32[]{:S(2)}) %collective-permute-start.21) | collective-permute-done | bytes 131104 | tf_op jit(solution)/shard_map/ppermute | solution.py:425
  116.7 2.6 %collective-permute-done.22.refs_2_ = bf16[4,16,1024]{2,1,0:T(8,128)(2,1)S(1)} collective-permute-done((bf16[4,16,1024]{2,1,0:T(8,128)(2,1)S(1)}, bf16[4,16,1024]{2,1,0:T(8,128)(2,1)S(1)}, u32[]{:S(2)}, u32[]{:S(2)}) %collective-permute-start.22) | collective-permute-done | bytes 131104 | tf_op jit(solution)/shard_map/ppermute | solution.py:425
  121.7 3.2 %collective-permute-start.35 = (bf16[10,16,1024]{2,1,0:T(8,128)(2,1)S(1)}, bf16[10,16,1024]{2,1,0:T(8,128)(2,1)S(1)}, u32[]{:S(2)}, u32[]{:S(2)}) collective-permute-start(bf16[10,16,1024]{2,1,0:T(8,128)(2,1)S(1)} %get-tuple-element.87), channel_id=1, source_target_pairs={{0,224},{8,232},{16,240},{24,248},{32,0},{40,8},{48,16},{56,24},{6... | collective-permute-start | bytes 983048 | tf_op jit(solution)/shard_map/ppermute | solution.py:425
  128.7 3.3 %collective-permute-done.18.refs_1_ = bf16[6,16,1024]{2,1,0:T(8,128)(2,1)S(1)} collective-permute-done((bf16[6,16,1024]{2,1,0:T(8,128)(2,1)S(1)}, bf16[6,16,1024]{2,1,0:T(8,128)(2,1)S(1)}, u32[]{:S(2)}, u32[]{:S(2)}) %collective-permute-start.18) | collective-permute-done | bytes 196640 | tf_op jit(solution)/shard_map/ppermute | solution.py:425
  137.4 3.2 %collective-permute-start.37 = (bf16[10,16,1024]{2,1,0:T(8,128)(2,1)S(1)}, bf16[10,16,1024]{2,1,0:T(8,128)(2,1)S(1)}, u32[]{:S(2)}, u32[]{:S(2)}) collective-permute-start(bf16[10,16,1024]{2,1,0:T(8,128)(2,1)S(1)} %get-tuple-element.89), channel_id=1, source_target_pairs={{0,224},{8,232},{16,240},{24,248},{32,0},{40,8},{48,16},{56,24},{6... | collective-permute-start | bytes 983048 | tf_op jit(solution)/shard_map/ppermute | solution.py:425
  140.6 5.0 %collective-permute-done.36.refs_4_ = bf16[10,16,1024]{2,1,0:T(8,128)(2,1)S(1)} collective-permute-done((bf16[10,16,1024]{2,1,0:T(8,128)(2,1)S(1)}, bf16[10,16,1024]{2,1,0:T(8,128)(2,1)S(1)}, u32[]{:S(2)}, u32[]{:S(2)}) %collective-permute-start.36) | collective-permute-done | bytes 327712 | tf_op jit(solution)/shard_map/ppermute | solution.py:425
  (91 shorter events, 55.1 us)
Async XLA Ops:
  0.6 17.0 %collective-permute-start.2 = (bf16[10,16,1024]{2,1,0:T(8,128)(2,1)}, bf16[10,16,1024]{2,1,0:T(8,128)(2,1)S(1)}, u32[]{:S(2)}, u32[]{:S(2)}) collective-permute-start(bf16[10,16,1024]{2,1,0:T(8,128)(2,1)} %refs_0_.2), channel_id=1, source_target_pairs={{0,224},{8,232},{16,240},{24,248},{32,0},{40,8},{48,16},{56,24},{6... | collective-permute-start | bytes 983048 | tf_op jit(solution)/shard_map/ppermute | solution.py:425
  6.6 14.4 %collective-permute-start.3 = (bf16[10,16,1024]{2,1,0:T(8,128)(2,1)}, bf16[10,16,1024]{2,1,0:T(8,128)(2,1)S(1)}, u32[]{:S(2)}, u32[]{:S(2)}) collective-permute-start(bf16[10,16,1024]{2,1,0:T(8,128)(2,1)} %refs_0_.2), channel_id=1, source_target_pairs={{0,32},{8,40},{16,48},{24,56},{32,64},{40,72},{48,80},{56,88},{64,... | collective-permute-start | bytes 983048 | tf_op jit(solution)/shard_map/ppermute | solution.py:425
  17.7 7.9 %collective-permute-start.4 = (bf16[10,16,1024]{2,1,0:T(8,128)(2,1)S(1)}, bf16[10,16,1024]{2,1,0:T(8,128)(2,1)S(1)}, u32[]{:S(2)}, u32[]{:S(2)}) collective-permute-start(bf16[10,16,1024]{2,1,0:T(8,128)(2,1)S(1)} %collective-permute-done.2.refs_1_), channel_id=1, source_target_pairs={{0,224},{8,232},{16,240},{24,248},{32,0},{40,8},{48,16},{56,24},{6... | collective-permute-start | bytes 983048 | tf_op jit(solution)/shard_map/ppermute | solution.py:425
  21.0 8.6 %collective-permute-start.5 = (bf16[10,16,1024]{2,1,0:T(8,128)(2,1)S(1)}, bf16[10,16,1024]{2,1,0:T(8,128)(2,1)S(1)}, u32[]{:S(2)}, u32[]{:S(2)}) collective-permute-start(bf16[10,16,1024]{2,1,0:T(8,128)(2,1)S(1)} %collective-permute-done.3.refs_2_), channel_id=1, source_target_pairs={{0,32},{8,40},{16,48},{24,56},{32,64},{40,72},{48,80},{56,88},{64,... | collective-permute-start | bytes 983048 | tf_op jit(solution)/shard_map/ppermute | solution.py:425
  25.6 8.4 %collective-permute-start.9 = (bf16[10,16,1024]{2,1,0:T(8,128)(2,1)S(1)}, bf16[10,16,1024]{2,1,0:T(8,128)(2,1)S(1)}, u32[]{:S(2)}, u32[]{:S(2)}) collective-permute-start(bf16[10,16,1024]{2,1,0:T(8,128)(2,1)S(1)} %collective-permute-done.4.refs_3_), channel_id=1, source_target_pairs={{0,224},{8,232},{16,240},{24,248},{32,0},{40,8},{48,16},{56,24},{6... | collective-permute-start | bytes 983048 | tf_op jit(solution)/shard_map/ppermute | solution.py:425
  29.6 9.7 %collective-permute-start.10 = (bf16[10,16,1024]{2,1,0:T(8,128)(2,1)S(1)}, bf16[10,16,1024]{2,1,0:T(8,128)(2,1)S(1)}, u32[]{:S(2)}, u32[]{:S(2)}) collective-permute-start(bf16[10,16,1024]{2,1,0:T(8,128)(2,1)S(1)} %collective-permute-done.5.refs_4_), channel_id=1, source_target_pairs={{0,32},{8,40},{16,48},{24,56},{32,64},{40,72},{48,80},{56,88},{64,... | collective-permute-start | bytes 983048 | tf_op jit(solution)/shard_map/ppermute | solution.py:425
  31.5 20.4 %collective-permute-start.6 = (bf16[10,16,1024]{2,1,0:T(8,128)(2,1)S(1)}, bf16[10,16,1024]{2,1,0:T(8,128)(2,1)S(1)}, u32[]{:S(2)}, u32[]{:S(2)}) collective-permute-start(bf16[10,16,1024]{2,1,0:T(8,128)(2,1)S(1)} %get-tuple-element.47), channel_id=1, source_target_pairs={{0,8},{8,16},{16,24},{24,0},{32,40},{40,48},{48,56},{56,32},{64,72... | collective-permute-start | bytes 983048 | tf_op jit(solution)/shard_map/ppermute | solution.py:425
  39.3 7.1 %collective-permute-start.11 = (bf16[5,16,1024]{2,1,0:T(8,128)(2,1)S(1)}, bf16[5,16,1024]{2,1,0:T(8,128)(2,1)S(1)}, u32[]{:S(2)}, u32[]{:S(2)}) collective-permute-start(bf16[5,16,1024]{2,1,0:T(8,128)(2,1)S(1)} %slice.20), channel_id=1, source_target_pairs={{0,32},{8,40},{16,48},{24,56},{32,64},{40,72},{48,80},{56,88},{64,... | collective-permute-start | bytes 491528 | tf_op jit(solution)/shard_map/ppermute | solution.py:425
  42.6 11.2 %collective-permute-start.7 = (bf16[10,16,1024]{2,1,0:T(8,128)(2,1)S(1)}, bf16[10,16,1024]{2,1,0:T(8,128)(2,1)S(1)}, u32[]{:S(2)}, u32[]{:S(2)}) collective-permute-start(bf16[10,16,1024]{2,1,0:T(8,128)(2,1)S(1)} %get-tuple-element.48), channel_id=1, source_target_pairs={{0,16},{8,24},{16,0},{24,8},{32,48},{40,56},{48,32},{56,40},{64,80... | collective-permute-start | bytes 983048 | tf_op jit(solution)/shard_map/ppermute | solution.py:425
  44.3 14.4 %collective-permute-start.8 = (bf16[10,16,1024]{2,1,0:T(8,128)(2,1)S(1)}, bf16[10,16,1024]{2,1,0:T(8,128)(2,1)S(1)}, u32[]{:S(2)}, u32[]{:S(2)}) collective-permute-start(bf16[10,16,1024]{2,1,0:T(8,128)(2,1)S(1)} %get-tuple-element.49), channel_id=1, source_target_pairs={{0,24},{8,0},{16,8},{24,16},{32,56},{40,32},{48,40},{56,48},{64,88... | collective-permute-start | bytes 983048 | tf_op jit(solution)/shard_map/ppermute | solution.py:425
  47.3 11.4 %collective-permute-start.13 = (bf16[6,16,1024]{2,1,0:T(8,128)(2,1)S(1)}, bf16[6,16,1024]{2,1,0:T(8,128)(2,1)S(1)}, u32[]{:S(2)}, u32[]{:S(2)}) collective-permute-start(bf16[6,16,1024]{2,1,0:T(8,128)(2,1)S(1)} %get-tuple-element.53), channel_id=1, source_target_pairs={{0,8},{8,16},{16,24},{24,0},{32,40},{40,48},{48,56},{56,32},{64,72... | collective-permute-start | bytes 589832 | tf_op jit(solution)/shard_map/ppermute | solution.py:425
  48.2 10.5 %collective-permute-start.14 = (bf16[6,16,1024]{2,1,0:T(8,128)(2,1)S(1)}, bf16[6,16,1024]{2,1,0:T(8,128)(2,1)S(1)}, u32[]{:S(2)}, u32[]{:S(2)}) collective-permute-start(bf16[6,16,1024]{2,1,0:T(8,128)(2,1)S(1)} %get-tuple-element.54), channel_id=1, source_target_pairs={{0,16},{8,24},{16,0},{24,8},{32,48},{40,56},{48,32},{56,40},{64,80... | collective-permute-start | bytes 589832 | tf_op jit(solution)/shard_map/ppermute | solution.py:425
  51.9 11.1 %collective-permute-start.15 = (bf16[6,16,1024]{2,1,0:T(8,128)(2,1)S(1)}, bf16[6,16,1024]{2,1,0:T(8,128)(2,1)S(1)}, u32[]{:S(2)}, u32[]{:S(2)}) collective-permute-start(bf16[6,16,1024]{2,1,0:T(8,128)(2,1)S(1)} %get-tuple-element.55), channel_id=1, source_target_pairs={{0,24},{8,0},{16,8},{24,16},{32,56},{40,32},{48,40},{56,48},{64,88... | collective-permute-start | bytes 589832 | tf_op jit(solution)/shard_map/ppermute | solution.py:425
  93.0 13.3 %collective-permute-start.30 = (bf16[5,16,1024]{2,1,0:T(8,128)(2,1)S(1)}, bf16[5,16,1024]{2,1,0:T(8,128)(2,1)S(1)}, u32[]{:S(2)}, u32[]{:S(2)}) collective-permute-start(bf16[5,16,1024]{2,1,0:T(8,128)(2,1)S(1)} %get-tuple-element.82), channel_id=1, source_target_pairs={{0,32},{8,40},{16,48},{24,56},{32,64},{40,72},{48,80},{56,88},{64,... | collective-permute-start | bytes 491528 | tf_op jit(solution)/shard_map/ppermute | solution.py:425
  93.1 13.2 %collective-permute-start.31 = (bf16[5,16,1024]{2,1,0:T(8,128)(2,1)S(1)}, bf16[5,16,1024]{2,1,0:T(8,128)(2,1)S(1)}, u32[]{:S(2)}, u32[]{:S(2)}) collective-permute-start(bf16[5,16,1024]{2,1,0:T(8,128)(2,1)S(1)} %get-tuple-element.83), channel_id=1, source_target_pairs={{0,224},{8,232},{16,240},{24,248},{32,0},{40,8},{48,16},{56,24},{6... | collective-permute-start | bytes 491528 | tf_op jit(solution)/shard_map/ppermute | solution.py:425
  99.0 7.2 %collective-permute-start.26 = (bf16[4,16,1024]{2,1,0:T(8,128)(2,1)S(1)}, bf16[4,16,1024]{2,1,0:T(8,128)(2,1)S(1)}, u32[]{:S(2)}, u32[]{:S(2)}) collective-permute-start(bf16[4,16,1024]{2,1,0:T(8,128)(2,1)S(1)} %get-tuple-element.77), channel_id=1, source_target_pairs={{0,8},{8,16},{16,24},{24,0},{32,40},{40,48},{48,56},{56,32},{64,72... | collective-permute-start | bytes 393224 | tf_op jit(solution)/shard_map/ppermute | solution.py:425
  107.3 13.3 %collective-permute-start.32 = (bf16[10,16,1024]{2,1,0:T(8,128)(2,1)S(1)}, bf16[10,16,1024]{2,1,0:T(8,128)(2,1)S(1)}, u32[]{:S(2)}, u32[]{:S(2)}) collective-permute-start(bf16[10,16,1024]{2,1,0:T(8,128)(2,1)S(1)} %get-tuple-element.84), channel_id=1, source_target_pairs={{0,32},{8,40},{16,48},{24,56},{32,64},{40,72},{48,80},{56,88},{64,... | collective-permute-start | bytes 983048 | tf_op jit(solution)/shard_map/ppermute | solution.py:425
  107.4 13.3 %collective-permute-start.33 = (bf16[10,16,1024]{2,1,0:T(8,128)(2,1)S(1)}, bf16[10,16,1024]{2,1,0:T(8,128)(2,1)S(1)}, u32[]{:S(2)}, u32[]{:S(2)}) collective-permute-start(bf16[10,16,1024]{2,1,0:T(8,128)(2,1)S(1)} %get-tuple-element.85), channel_id=1, source_target_pairs={{0,224},{8,232},{16,240},{24,248},{32,0},{40,8},{48,16},{56,24},{6... | collective-permute-start | bytes 983048 | tf_op jit(solution)/shard_map/ppermute | solution.py:425
  121.6 14.7 %collective-permute-start.34 = (bf16[10,16,1024]{2,1,0:T(8,128)(2,1)S(1)}, bf16[10,16,1024]{2,1,0:T(8,128)(2,1)S(1)}, u32[]{:S(2)}, u32[]{:S(2)}) collective-permute-start(bf16[10,16,1024]{2,1,0:T(8,128)(2,1)S(1)} %get-tuple-element.86), channel_id=1, source_target_pairs={{0,32},{8,40},{16,48},{24,56},{32,64},{40,72},{48,80},{56,88},{64,... | collective-permute-start | bytes 983048 | tf_op jit(solution)/shard_map/ppermute | solution.py:425
  121.7 14.6 %collective-permute-start.35 = (bf16[10,16,1024]{2,1,0:T(8,128)(2,1)S(1)}, bf16[10,16,1024]{2,1,0:T(8,128)(2,1)S(1)}, u32[]{:S(2)}, u32[]{:S(2)}) collective-permute-start(bf16[10,16,1024]{2,1,0:T(8,128)(2,1)S(1)} %get-tuple-element.87), channel_id=1, source_target_pairs={{0,224},{8,232},{16,240},{24,248},{32,0},{40,8},{48,16},{56,24},{6... | collective-permute-start | bytes 983048 | tf_op jit(solution)/shard_map/ppermute | solution.py:425
  127.0 7.3 %collective-permute-start.19 = (bf16[6,16,1024]{2,1,0:T(8,128)(2,1)S(1)}, bf16[6,16,1024]{2,1,0:T(8,128)(2,1)S(1)}, u32[]{:S(2)}, u32[]{:S(2)}) collective-permute-start(bf16[6,16,1024]{2,1,0:T(8,128)(2,1)S(1)} %get-tuple-element.68), channel_id=1, source_target_pairs={{0,16},{8,24},{16,0},{24,8},{32,48},{40,56},{48,32},{56,40},{64,80... | collective-permute-start | bytes 589832 | tf_op jit(solution)/shard_map/ppermute | solution.py:425
  127.9 8.4 %collective-permute-start.20 = (bf16[6,16,1024]{2,1,0:T(8,128)(2,1)S(1)}, bf16[6,16,1024]{2,1,0:T(8,128)(2,1)S(1)}, u32[]{:S(2)}, u32[]{:S(2)}) collective-permute-start(bf16[6,16,1024]{2,1,0:T(8,128)(2,1)S(1)} %get-tuple-element.69), channel_id=1, source_target_pairs={{0,8},{8,16},{16,24},{24,0},{32,40},{40,48},{48,56},{56,32},{64,72... | collective-permute-start | bytes 589832 | tf_op jit(solution)/shard_map/ppermute | solution.py:425
  137.3 8.4 %collective-permute-start.36 = (bf16[10,16,1024]{2,1,0:T(8,128)(2,1)S(1)}, bf16[10,16,1024]{2,1,0:T(8,128)(2,1)S(1)}, u32[]{:S(2)}, u32[]{:S(2)}) collective-permute-start(bf16[10,16,1024]{2,1,0:T(8,128)(2,1)S(1)} %get-tuple-element.88), channel_id=1, source_target_pairs={{0,32},{8,40},{16,48},{24,56},{32,64},{40,72},{48,80},{56,88},{64,... | collective-permute-start | bytes 983048 | tf_op jit(solution)/shard_map/ppermute | solution.py:425
  137.4 8.3 %collective-permute-start.37 = (bf16[10,16,1024]{2,1,0:T(8,128)(2,1)S(1)}, bf16[10,16,1024]{2,1,0:T(8,128)(2,1)S(1)}, u32[]{:S(2)}, u32[]{:S(2)}) collective-permute-start(bf16[10,16,1024]{2,1,0:T(8,128)(2,1)S(1)} %get-tuple-element.89), channel_id=1, source_target_pairs={{0,224},{8,232},{16,240},{24,248},{32,0},{40,8},{48,16},{56,24},{6... | collective-permute-start | bytes 983048 | tf_op jit(solution)/shard_map/ppermute | solution.py:425
  (15 other events, 80.7 us)

commit v4 on v3

--- a/solution.py
+++ b/solution.py
@@ -12,6 +12,8 @@
 HEADS = 16
 NY = 4
 CAP = 2
+SPARE = 2
+WIDE = 512
 
 
 SMEM = pl.BlockSpec(memory_space=pltpu.SMEM)
@@ -98,25 +100,21 @@
         ins, out = refs[:-1], refs[-1]
         for n, phase in enumerate(OUT):
             first, stride, count = span_of(phase, nz)
-            for j in range(NY):
-
-                def place_one(k, carry):
-                    plane = (p_ref[0] + nz + first + stride * (k // CAP)) % nz
-                    r = r_ref[j, plane * CAP + k % CAP]
-
-                    @pl.when(r >= 0)
-                    def _():
-                        out[jnp.maximum(r, 0)] = ins[n * NY + j][k]
-
-                    return carry
-
-                lax.fori_loop(0, count * CAP, place_one, 0, unroll=2)
+
+            def place_slots(k, carry):
+                plane = (p_ref[0] + nz + first + stride * (k // CAP)) % nz
+                at = [r_ref[j, plane * CAP + k % CAP] for j in range(NY)]
+                for j in range(NY):
+                    out[jnp.where(at[j] < 0, ref_count, at[j])] = ins[n * NY + j][k]
+                return carry
+
+            lax.fori_loop(0, count * CAP, place_slots, 0)
 
     return pl.pallas_call(
         body,
         in_specs=[SMEM, SMEM] + [VMEM] * len(flat),
         out_specs=VMEM,
-        out_shape=jax.ShapeDtypeStruct((ref_count,) + tail, BF),
+        out_shape=jax.ShapeDtypeStruct((ref_count + SPARE,) + tail, BF),
         name="compact",
         compiler_params=SMALL,
     )(ref_of, place, *flat)
@@ -128,21 +126,15 @@
     first, stride, _ = span_of(phase, nz)
 
     def body(r_ref, p_ref, own_ref, other_ref, *outs):
-        for j in range(NY):
-
-            def place_one(k, carry):
-                plane = (p_ref[0] + nz + first + stride * (k // CAP)) % nz
-                r = r_ref[j, plane * CAP + k % CAP]
-
-                @pl.when(r >= 0)
-                def _():
-                    at = jnp.maximum(r, 0)
-                    total = own_ref[at] + other_ref[at].astype(F32)
-                    outs[j][k] = total.astype(BF)
-
-                return carry
-
-            lax.fori_loop(0, len(slots), place_one, 0, unroll=2)
+        def place_slots(k, carry):
+            plane = (p_ref[0] + nz + first + stride * (k // CAP)) % nz
+            at = [jnp.maximum(r_ref[j, plane * CAP + k % CAP], 0) for j in range(NY)]
+            for j in range(NY):
+                total = own_ref[at[j]] + other_ref[at[j]].astype(F32)
+                outs[j][k] = total.astype(BF)
+            return carry
+
+        lax.fori_loop(0, len(slots), place_slots, 0)
 
     return pl.pallas_call(
         body,
@@ -260,13 +252,19 @@
     )(*arrays)
 
 
-def project_own(place, own, key_weight, value_weight):
-    rows, half = own.shape
+def project_own(place, own, key_weight, value_weight, rows):
+    half = own.shape[1]
 
     def body(p_ref, own_ref, wk_ref, wv_ref, k_ref, v_ref):
         mine = pl.ds(pl.multiple_of(p_ref[2] * half, half), half)
-        for w_ref, out in ((wk_ref, k_ref), (wv_ref, v_ref)):
-            out[...] = jnp.dot(own_ref[...], w_ref[mine, :], preferred_element_type=F32)
+
+        def block(n, carry):
+            c = pl.ds(pl.multiple_of(n * WIDE, WIDE), WIDE)
+            for w_ref, out in ((wk_ref, k_ref), (wv_ref, v_ref)):
+                out[:, c] = jnp.dot(own_ref[:rows], w_ref[mine, c], preferred_element_type=F32)
+            return carry
+
+        lax.fori_loop(0, half // WIDE, block, 0)
 
     return pl.pallas_call(
         body,
@@ -283,10 +281,15 @@
     nt = (((1,), (1,)), ((), ()))
 
     def body(p_ref, dk_ref, dv_ref, wk_ref, wv_ref, out):
-        mine = pl.ds(pl.multiple_of(p_ref[2] * half, half), half)
-        total = lax.dot_general(dk_ref[...], wk_ref[mine, :], nt, preferred_element_type=F32)
-        total += lax.dot_general(dv_ref[...], wv_ref[mine, :], nt, preferred_element_type=F32)
-        out[...] = total
+        def block(n, carry):
+            c = pl.ds(pl.multiple_of(n * WIDE, WIDE), WIDE)
+            at = pl.ds(pl.multiple_of(p_ref[2] * half + n * WIDE, WIDE), WIDE)
+            total = lax.dot_general(dk_ref[...], wk_ref[at, :], nt, preferred_element_type=F32)
+            total += lax.dot_general(dv_ref[...], wv_ref[at, :], nt, preferred_element_type=F32)
+            out[:, c] = total
+            return carry
+
+        lax.fori_loop(0, half // WIDE, block, 0)
 
     return pl.pallas_call(
         body,
@@ -298,10 +301,15 @@
     )(place, key_grad, value_grad, key_weight, value_weight)
 
 
+def into_vmem(*arrays):
+    held = fetch(*(pltpu.with_memory_space_constraint(a, pltpu.HBM) for a in arrays))
+    return [pltpu.with_memory_space_constraint(a, pltpu.VMEM) for a in held]
+
+
 def core_step(
     place, key_part, value_part, other, key_weight, value_weight, queries, out_grad, spans, head_size
 ):
-    rows, half = other.shape
+    rows, half = key_part.shape
     tok = queries.shape[0] // spans
     per = rows // spans
     heads = half // head_size
@@ -315,9 +323,15 @@
         dq_hbm, poth_ref, dk_ref, dv_ref, dq_ref, k_ref, v_ref, sem,
     ):
         theirs = pl.ds(pl.multiple_of((1 - p_ref[2]) * half, half), half)
-        for part, w_ref, out in ((ka_ref, wk_ref, k_ref), (va_ref, wv_ref, v_ref)):
-            total = jnp.dot(oth_ref[...], w_ref[theirs, :], preferred_element_type=F32)
-            out[...] = (part[...] + total).astype(BF)
+
+        def project(n, carry):
+            c = pl.ds(pl.multiple_of(n * WIDE, WIDE), WIDE)
+            for part, w_ref, out in ((ka_ref, wk_ref, k_ref), (va_ref, wv_ref, v_ref)):
+                total = jnp.dot(oth_ref[:rows], w_ref[theirs, c], preferred_element_type=F32)
+                out[:, c] = (part[:, c] + total).astype(BF)
+            return carry
+
+        lax.fori_loop(0, half // WIDE, project, 0)
 
         def at(u):
             return (
@@ -365,9 +379,20 @@
         grads(spans - 1, *lax.fori_loop(0, spans - 1, both, weigh(0)))
         store = pltpu.make_async_copy(dq_ref, dq_hbm, sem.at[0])
         store.start()
-        total = lax.dot_general(dk_ref[...], wk_ref[theirs, :], nt, preferred_element_type=F32)
-        total += lax.dot_general(dv_ref[...], wv_ref[theirs, :], nt, preferred_element_type=F32)
-        poth_ref[...] = total.astype(BF)
+
+        def back(n, carry):
+            c = pl.ds(pl.multiple_of(n * WIDE, WIDE), WIDE)
+            at_rows = pl.ds(pl.multiple_of((1 - p_ref[2]) * half + n * WIDE, WIDE), WIDE)
+            total = lax.dot_general(
+                dk_ref[...], wk_ref[at_rows, :], nt, preferred_element_type=F32
+            )
+            total += lax.dot_general(
+                dv_ref[...], wv_ref[at_rows, :], nt, preferred_element_type=F32
+            )
+            poth_ref[:, c] = total.astype(BF)
+            return carry
+
+        lax.fori_loop(0, half // WIDE, back, 0)
         store.wait()
 
     return pl.pallas_call(
@@ -429,7 +454,7 @@
 
     place = jnp.stack([z0, y0, head]).astype(jnp.int32)
 
-    blocks = {0: [encodings]}
+    blocks = {0: into_vmem(encodings)}
     ahead = behind = encodings
     readers = None
     for step in range(1, far + 1):
@@ -452,21 +477,15 @@
         picked = pick_rows(table, place, need, phase, nz)
         groups.append([picked[0]] + [move(picked[j], 0, j) for j in range(1, NY)])
 
-    key_weight, value_weight, queries, out_grad = (
-        pltpu.with_memory_space_constraint(a, pltpu.VMEM)
-        for a in fetch(
-            *(
-                pltpu.with_memory_space_constraint(a, pltpu.HBM)
-                for a in (key_weight, value_weight, queries, out_grad)
-            )
-        )
+    key_weight, value_weight, queries, out_grad = into_vmem(
+        key_weight, value_weight, queries, out_grad
     )
     flat = (ref_count * length, half)
     own = compact(ref_of, place, groups, nz, ref_count)
     other = swap(own)
-    parts = project_own(place, own.reshape(flat), key_weight, value_weight)
+    parts = project_own(place, own.reshape(-1, half), key_weight, value_weight, flat[0])
     query_grad, partial_other, key_grad, value_grad = core_step(
-        place, *parts, other.reshape(flat), key_weight, value_weight, queries, out_grad,
+        place, *parts, other.reshape(-1, half), key_weight, value_weight, queries, out_grad,
         spans, D // HEADS,
     )
     came = swap(partial_other)

time: 147 us -> 144 us (0.980)
  waiting for transfers between devices: 56.2 us -> 53.7 us
    ppermute x36, waiting for transfers between devices: 56.2 us -> 53.7 us  [move(): return lax.ppermute(x, 'seq', ring(seq, dz, dy))]
    pallas_call x1 -> x2, Pallas kernels: 4.27 us -> 5.26 us  [fetch(): pl.pallas_call(body, in_specs=[pl.BlockSpec(memory_space=pltpu.HBM)] * co...]
  transfers between devices with their start and end apart: 38 -> 38, of which waited for: 22 -> 20; matrix products, arithmetic and copies ran while one was open for 1% -> 1% of each run, Pallas kernels for 9% -> 10%
where the time goes in v4:
time: 144 us; the launch traced here: 143 us
  starting transfers between devices  57.4 us (40%)
  waiting for transfers between devices  53.7 us (37%)
  Pallas kernels  29.3 us (20%)
    ppermute x36, starting transfers between devices, move(): return lax.ppermute(x, 'seq', ring(seq, dz, dy))  56.8 us
    ppermute x36, waiting for transfers between devices, move(): return lax.ppermute(x, 'seq', ring(seq, dz, dy))  53.7 us
    pallas_call x1, Pallas kernels, core_step(): pl.pallas_call(body, in_specs=[SMEM] + [VMEM] * 7, out_specs=[ANY] + [VME...  8.34 us
    pallas_call x5, Pallas kernels, gather_grads(): pl.pallas_call(body, in_specs=[SMEM, SMEM] + [VMEM] * (NY + len(before)),...  5.32 us
    pallas_call x2, Pallas kernels, fetch(): pl.pallas_call(body, in_specs=[pl.BlockSpec(memory_space=pltpu.HBM)] * co...  5.26 us
    pallas_call x4, Pallas kernels, spread(): pl.pallas_call(body, in_specs=[SMEM, SMEM, VMEM, VMEM], out_specs=[VMEM]...  2.96 us
  transfers between devices with their start and end apart: 38, of which 20 were waited for; matrix products, arithmetic and copies ran while one was open for 1% of the time, Pallas kernels for 10%

profile of v4, /device:TPU:2, one launch (start us, length us, event | category | flops | bytes accessed | tf_op | source)
XLA Modules:
  0.0 143.4 jit_solution(6488291632967710119)
XLA Ops:
  2.6 4.0 %collective-permute-start.2 = (bf16[10,16,1024]{2,1,0:T(8,128)(2,1)}, bf16[10,16,1024]{2,1,0:T(8,128)(2,1)S(1)}, u32[]{:S(2)}, u32[]{:S(2)}) collective-permute-start(bf16[10,16,1024]{2,1,0:T(8,128)(2,1)} %refs_0_.2), channel_id=1, source_target_pairs={{0,224},{8,232},{16,240},{24,248},{32,0},{40,8},{48,16},{56,24},{6... | collective-permute-start | bytes 983048 | tf_op jit(solution)/shard_map/ppermute | solution.py:450
  7.5 3.1 %collective-permute-start = (s32[1,22]{1,0:T(1,128)S(1)}, s32[1,22]{1,0:T(1,128)S(1)}, u32[]{:S(2)}, u32[]{:S(2)}) collective-permute-start(s32[1,22]{1,0:T(1,128)S(1)} %reshape.357), channel_id=1, source_target_pairs={{0,24},{8,0},{16,8},{24,16},{32,56},{40,32},{48,40},{56,48},{64,88... | collective-permute-start | bytes 272 | tf_op jit(solution)/shard_map/ppermute | solution.py:450
  11.9 2.5 %collective-permute-start.1 = (s32[2,22]{1,0:T(2,128)S(1)}, s32[2,22]{1,0:T(2,128)S(1)}, u32[]{:S(2)}, u32[]{:S(2)}) collective-permute-start(s32[2,22]{1,0:T(2,128)S(1)} %pad_add_fusion.1), channel_id=1, source_target_pairs={{0,16},{8,24},{16,0},{24,8},{32,48},{40,56},{48,32},{56,40},{64,80... | collective-permute-start | bytes 536 | tf_op jit(solution)/shard_map/ppermute | solution.py:450
  17.8 3.2 %collective-permute-start.4 = (bf16[10,16,1024]{2,1,0:T(8,128)(2,1)S(1)}, bf16[10,16,1024]{2,1,0:T(8,128)(2,1)S(1)}, u32[]{:S(2)}, u32[]{:S(2)}) collective-permute-start(bf16[10,16,1024]{2,1,0:T(8,128)(2,1)S(1)} %collective-permute-done.2.refs_1_), channel_id=1, source_target_pairs={{0,224},{8,232},{16,240},{24,248},{32,0},{40,8},{48,16},{56,24},{6... | collective-permute-start | bytes 983048 | tf_op jit(solution)/shard_map/ppermute | solution.py:450
  21.1 5.1 %collective-permute-done.5.refs_4_ = bf16[10,16,1024]{2,1,0:T(8,128)(2,1)S(1)} collective-permute-done((bf16[10,16,1024]{2,1,0:T(8,128)(2,1)S(1)}, bf16[10,16,1024]{2,1,0:T(8,128)(2,1)S(1)}, u32[]{:S(2)}, u32[]{:S(2)}) %collective-permute-start.5) | collective-permute-done | bytes 327712 | tf_op jit(solution)/shard_map/ppermute | solution.py:450
  26.2 3.2 %collective-permute-start.9 = (bf16[10,16,1024]{2,1,0:T(8,128)(2,1)S(1)}, bf16[10,16,1024]{2,1,0:T(8,128)(2,1)S(1)}, u32[]{:S(2)}, u32[]{:S(2)}) collective-permute-start(bf16[10,16,1024]{2,1,0:T(8,128)(2,1)S(1)} %collective-permute-done.4.refs_3_), channel_id=1, source_target_pairs={{0,224},{8,232},{16,240},{24,248},{32,0},{40,8},{48,16},{56,24},{6... | collective-permute-start | bytes 983048 | tf_op jit(solution)/shard_map/ppermute | solution.py:450
  31.9 3.1 %collective-permute-done.10.refs_1_ = bf16[10,16,1024]{2,1,0:T(8,128)(2,1)S(1)} collective-permute-done((bf16[10,16,1024]{2,1,0:T(8,128)(2,1)S(1)}, bf16[10,16,1024]{2,1,0:T(8,128)(2,1)S(1)}, u32[]{:S(2)}, u32[]{:S(2)}) %collective-permute-start.10) | collective-permute-done | bytes 327712 | tf_op jit(solution)/shard_map/ppermute | solution.py:450
  35.2 3.5 %collective-permute-start.12 = (bf16[5,16,1024]{2,1,0:T(8,128)(2,1)S(1)}, bf16[5,16,1024]{2,1,0:T(8,128)(2,1)S(1)}, u32[]{:S(2)}, u32[]{:S(2)}) collective-permute-start(bf16[5,16,1024]{2,1,0:T(8,128)(2,1)S(1)} %slice.19), channel_id=1, source_target_pairs={{0,224},{8,232},{16,240},{24,248},{32,0},{40,8},{48,16},{56,24},{6... | collective-permute-start | bytes 491528 | tf_op jit(solution)/shard_map/ppermute | solution.py:450
  38.7 2.5 %collective-permute-start.7 = (bf16[10,16,1024]{2,1,0:T(8,128)(2,1)S(1)}, bf16[10,16,1024]{2,1,0:T(8,128)(2,1)S(1)}, u32[]{:S(2)}, u32[]{:S(2)}) collective-permute-start(bf16[10,16,1024]{2,1,0:T(8,128)(2,1)S(1)} %get-tuple-element.48), channel_id=1, source_target_pairs={{0,16},{8,24},{16,0},{24,8},{32,48},{40,56},{48,32},{56,40},{64,80... | collective-permute-start | bytes 983048 | tf_op jit(solution)/shard_map/ppermute | solution.py:450
  44.3 3.5 %collective-permute-start.14 = (bf16[6,16,1024]{2,1,0:T(8,128)(2,1)S(1)}, bf16[6,16,1024]{2,1,0:T(8,128)(2,1)S(1)}, u32[]{:S(2)}, u32[]{:S(2)}) collective-permute-start(bf16[6,16,1024]{2,1,0:T(8,128)(2,1)S(1)} %get-tuple-element.54), channel_id=1, source_target_pairs={{0,16},{8,24},{16,0},{24,8},{32,48},{40,56},{48,32},{56,40},{64,80... | collective-permute-start | bytes 589832 | tf_op jit(solution)/shard_map/ppermute | solution.py:450
  51.0 5.2 %collective-permute-done.8.refs_3_ = bf16[10,16,1024]{2,1,0:T(8,128)(2,1)S(1)} collective-permute-done((bf16[10,16,1024]{2,1,0:T(8,128)(2,1)S(1)}, bf16[10,16,1024]{2,1,0:T(8,128)(2,1)S(1)}, u32[]{:S(2)}, u32[]{:S(2)}) %collective-permute-start.8) | collective-permute-done | bytes 327712 | tf_op jit(solution)/shard_map/ppermute | solution.py:450
  56.2 4.3 %collective-permute-done.15.refs_7_ = bf16[6,16,1024]{2,1,0:T(8,128)(2,1)S(1)} collective-permute-done((bf16[6,16,1024]{2,1,0:T(8,128)(2,1)S(1)}, bf16[6,16,1024]{2,1,0:T(8,128)(2,1)S(1)}, u32[]{:S(2)}, u32[]{:S(2)}) %collective-permute-start.15) | collective-permute-done | bytes 196640 | tf_op jit(solution)/shard_map/ppermute | solution.py:450
  61.6 4.3 %fetch.3 = (bf16[2048,1024]{1,0:T(8,128)(2,1)S(1)}, bf16[2048,1024]{1,0:T(8,128)(2,1)S(1)}, bf16[704,1024]{1,0:T(8,128)(2,1)S(1)}, bf16[704,1024]{1,0:T(8,128)(2,1)S(1)}) custom-call(bf16[2048,1024]{1,0:T(8,128)(2,1)} %refs_0_.3, bf16[2048,1024]{1,0:T(8,128)(2,1)} %refs_1_.1, bf16[704,1024]{1,0:T(8,128)(2,1)} %refs_2_.1, bf16[704,1024]{1,0:T(8,128)(2,1)} %refs_3_.1), custom_call_target="tpu_custom_call" | custom-call | tf_op jit(solution)/shard_map/fetch/pallas_call | solution.py:244
  68.3 8.3 %core_step.1 = (bf16[704,1024]{1,0:T(8,128)(2,1)}, bf16[352,1024]{1,0:T(8,128)(2,1)S(1)}, bf16[352,1024]{1,0:T(8,128)(2,1)S(1)}, bf16[352,1024]{1,0:T(8,128)(2,1)S(1)}) custom-call(s32[3]{0:T(128)S(1)} %pad_add_fusion.2.p_ref, f32[352,1024]{1,0:T(8,128)S(1)} %get-tuple-element.58.ka_ref, f32[352,1024]{1,0:T(8,128)S(1)} %get-tuple-element.59.va_ref, ...), custom_call_target="tpu_custom_call" | custom-call | tf_op jit(solution)/shard_map/core_step/pallas_call | solution.py:398
  80.3 2.6 %collective-permute-start.27 = (bf16[2,16,1024]{2,1,0:T(8,128)(2,1)S(1)}, bf16[2,16,1024]{2,1,0:T(8,128)(2,1)S(1)}, u32[]{:S(2)}, u32[]{:S(2)}) collective-permute-start(bf16[2,16,1024]{2,1,0:T(8,128)(2,1)S(1)} %get-tuple-element.79), channel_id=1, source_target_pairs={{0,24},{8,0},{16,8},{24,16},{32,56},{40,32},{48,40},{56,48},{64,88... | collective-permute-start | bytes 196616 | tf_op jit(solution)/shard_map/ppermute | solution.py:450
  85.9 3.0 %collective-permute-done.28.refs_2_ = bf16[2,16,1024]{2,1,0:T(8,128)(2,1)S(1)} collective-permute-done((bf16[2,16,1024]{2,1,0:T(8,128)(2,1)S(1)}, bf16[2,16,1024]{2,1,0:T(8,128)(2,1)S(1)}, u32[]{:S(2)}, u32[]{:S(2)}) %collective-permute-start.28) | collective-permute-done | bytes 65568 | tf_op jit(solution)/shard_map/ppermute | solution.py:450
  90.4 3.2 %collective-permute-start.31 = (bf16[5,16,1024]{2,1,0:T(8,128)(2,1)S(1)}, bf16[5,16,1024]{2,1,0:T(8,128)(2,1)S(1)}, u32[]{:S(2)}, u32[]{:S(2)}) collective-permute-start(bf16[5,16,1024]{2,1,0:T(8,128)(2,1)S(1)} %get-tuple-element.83), channel_id=1, source_target_pairs={{0,224},{8,232},{16,240},{24,248},{32,0},{40,8},{48,16},{56,24},{6... | collective-permute-start | bytes 491528 | tf_op jit(solution)/shard_map/ppermute | solution.py:450
  104.3 3.2 %collective-permute-start.33 = (bf16[10,16,1024]{2,1,0:T(8,128)(2,1)S(1)}, bf16[10,16,1024]{2,1,0:T(8,128)(2,1)S(1)}, u32[]{:S(2)}, u32[]{:S(2)}) collective-permute-start(bf16[10,16,1024]{2,1,0:T(8,128)(2,1)S(1)} %get-tuple-element.85), channel_id=1, source_target_pairs={{0,224},{8,232},{16,240},{24,248},{32,0},{40,8},{48,16},{56,24},{6... | collective-permute-start | bytes 983048 | tf_op jit(solution)/shard_map/ppermute | solution.py:450
  110.5 2.8 %collective-permute-done.21.refs_1_ = bf16[4,16,1024]{2,1,0:T(8,128)(2,1)S(1)} collective-permute-done((bf16[4,16,1024]{2,1,0:T(8,128)(2,1)S(1)}, bf16[4,16,1024]{2,1,0:T(8,128)(2,1)S(1)}, u32[]{:S(2)}, u32[]{:S(2)}) %collective-permute-start.21) | collective-permute-done | bytes 131104 | tf_op jit(solution)/shard_map/ppermute | solution.py:450
  113.3 2.6 %collective-permute-done.22.refs_2_ = bf16[4,16,1024]{2,1,0:T(8,128)(2,1)S(1)} collective-permute-done((bf16[4,16,1024]{2,1,0:T(8,128)(2,1)S(1)}, bf16[4,16,1024]{2,1,0:T(8,128)(2,1)S(1)}, u32[]{:S(2)}, u32[]{:S(2)}) %collective-permute-start.22) | collective-permute-done | bytes 131104 | tf_op jit(solution)/shard_map/ppermute | solution.py:450
  118.3 3.2 %collective-permute-start.35 = (bf16[10,16,1024]{2,1,0:T(8,128)(2,1)S(1)}, bf16[10,16,1024]{2,1,0:T(8,128)(2,1)S(1)}, u32[]{:S(2)}, u32[]{:S(2)}) collective-permute-start(bf16[10,16,1024]{2,1,0:T(8,128)(2,1)S(1)} %get-tuple-element.87), channel_id=1, source_target_pairs={{0,224},{8,232},{16,240},{24,248},{32,0},{40,8},{48,16},{56,24},{6... | collective-permute-start | bytes 983048 | tf_op jit(solution)/shard_map/ppermute | solution.py:450
  124.8 3.3 %collective-permute-done.18.refs_1_ = bf16[6,16,1024]{2,1,0:T(8,128)(2,1)S(1)} collective-permute-done((bf16[6,16,1024]{2,1,0:T(8,128)(2,1)S(1)}, bf16[6,16,1024]{2,1,0:T(8,128)(2,1)S(1)}, u32[]{:S(2)}, u32[]{:S(2)}) %collective-permute-start.18) | collective-permute-done | bytes 196640 | tf_op jit(solution)/shard_map/ppermute | solution.py:450
  133.6 3.2 %collective-permute-start.37 = (bf16[10,16,1024]{2,1,0:T(8,128)(2,1)S(1)}, bf16[10,16,1024]{2,1,0:T(8,128)(2,1)S(1)}, u32[]{:S(2)}, u32[]{:S(2)}) collective-permute-start(bf16[10,16,1024]{2,1,0:T(8,128)(2,1)S(1)} %get-tuple-element.89), channel_id=1, source_target_pairs={{0,224},{8,232},{16,240},{24,248},{32,0},{40,8},{48,16},{56,24},{6... | collective-permute-start | bytes 983048 | tf_op jit(solution)/shard_map/ppermute | solution.py:450
  136.8 5.0 %collective-permute-done.36.refs_4_ = bf16[10,16,1024]{2,1,0:T(8,128)(2,1)S(1)} collective-permute-done((bf16[10,16,1024]{2,1,0:T(8,128)(2,1)S(1)}, bf16[10,16,1024]{2,1,0:T(8,128)(2,1)S(1)}, u32[]{:S(2)}, u32[]{:S(2)}) %collective-permute-start.36) | collective-permute-done | bytes 327712 | tf_op jit(solution)/shard_map/ppermute | solution.py:450
  (90 shorter events, 54.3 us)
Async XLA Ops:
  0.6 17.1 %collective-permute-start.3 = (bf16[10,16,1024]{2,1,0:T(8,128)(2,1)}, bf16[10,16,1024]{2,1,0:T(8,128)(2,1)S(1)}, u32[]{:S(2)}, u32[]{:S(2)}) collective-permute-start(bf16[10,16,1024]{2,1,0:T(8,128)(2,1)} %refs_0_.2), channel_id=1, source_target_pairs={{0,32},{8,40},{16,48},{24,56},{32,64},{40,72},{48,80},{56,88},{64,... | collective-permute-start | bytes 983048 | tf_op jit(solution)/shard_map/ppermute | solution.py:450
  2.6 15.2 %collective-permute-start.2 = (bf16[10,16,1024]{2,1,0:T(8,128)(2,1)}, bf16[10,16,1024]{2,1,0:T(8,128)(2,1)S(1)}, u32[]{:S(2)}, u32[]{:S(2)}) collective-permute-start(bf16[10,16,1024]{2,1,0:T(8,128)(2,1)} %refs_0_.2), channel_id=1, source_target_pairs={{0,224},{8,232},{16,240},{24,248},{32,0},{40,8},{48,16},{56,24},{6... | collective-permute-start | bytes 983048 | tf_op jit(solution)/shard_map/ppermute | solution.py:450
  17.7 8.5 %collective-permute-start.5 = (bf16[10,16,1024]{2,1,0:T(8,128)(2,1)S(1)}, bf16[10,16,1024]{2,1,0:T(8,128)(2,1)S(1)}, u32[]{:S(2)}, u32[]{:S(2)}) collective-permute-start(bf16[10,16,1024]{2,1,0:T(8,128)(2,1)S(1)} %collective-permute-done.3.refs_2_), channel_id=1, source_target_pairs={{0,32},{8,40},{16,48},{24,56},{32,64},{40,72},{48,80},{56,88},{64,... | collective-permute-start | bytes 983048 | tf_op jit(solution)/shard_map/ppermute | solution.py:450
  17.8 8.4 %collective-permute-start.4 = (bf16[10,16,1024]{2,1,0:T(8,128)(2,1)S(1)}, bf16[10,16,1024]{2,1,0:T(8,128)(2,1)S(1)}, u32[]{:S(2)}, u32[]{:S(2)}) collective-permute-start(bf16[10,16,1024]{2,1,0:T(8,128)(2,1)S(1)} %collective-permute-done.2.refs_1_), channel_id=1, source_target_pairs={{0,224},{8,232},{16,240},{24,248},{32,0},{40,8},{48,16},{56,24},{6... | collective-permute-start | bytes 983048 | tf_op jit(solution)/shard_map/ppermute | solution.py:450
  26.2 8.8 %collective-permute-start.10 = (bf16[10,16,1024]{2,1,0:T(8,128)(2,1)S(1)}, bf16[10,16,1024]{2,1,0:T(8,128)(2,1)S(1)}, u32[]{:S(2)}, u32[]{:S(2)}) collective-permute-start(bf16[10,16,1024]{2,1,0:T(8,128)(2,1)S(1)} %collective-permute-done.5.refs_4_), channel_id=1, source_target_pairs={{0,32},{8,40},{16,48},{24,56},{32,64},{40,72},{48,80},{56,88},{64,... | collective-permute-start | bytes 983048 | tf_op jit(solution)/shard_map/ppermute | solution.py:450
  26.2 8.8 %collective-permute-start.9 = (bf16[10,16,1024]{2,1,0:T(8,128)(2,1)S(1)}, bf16[10,16,1024]{2,1,0:T(8,128)(2,1)S(1)}, u32[]{:S(2)}, u32[]{:S(2)}) collective-permute-start(bf16[10,16,1024]{2,1,0:T(8,128)(2,1)S(1)} %collective-permute-done.4.refs_3_), channel_id=1, source_target_pairs={{0,224},{8,232},{16,240},{24,248},{32,0},{40,8},{48,16},{56,24},{6... | collective-permute-start | bytes 983048 | tf_op jit(solution)/shard_map/ppermute | solution.py:450
  30.3 17.5 %collective-permute-start.6 = (bf16[10,16,1024]{2,1,0:T(8,128)(2,1)S(1)}, bf16[10,16,1024]{2,1,0:T(8,128)(2,1)S(1)}, u32[]{:S(2)}, u32[]{:S(2)}) collective-permute-start(bf16[10,16,1024]{2,1,0:T(8,128)(2,1)S(1)} %get-tuple-element.47), channel_id=1, source_target_pairs={{0,8},{8,16},{16,24},{24,0},{32,40},{40,48},{48,56},{56,32},{64,72... | collective-permute-start | bytes 983048 | tf_op jit(solution)/shard_map/ppermute | solution.py:450
  35.1 7.4 %collective-permute-start.11 = (bf16[5,16,1024]{2,1,0:T(8,128)(2,1)S(1)}, bf16[5,16,1024]{2,1,0:T(8,128)(2,1)S(1)}, u32[]{:S(2)}, u32[]{:S(2)}) collective-permute-start(bf16[5,16,1024]{2,1,0:T(8,128)(2,1)S(1)} %slice.20), channel_id=1, source_target_pairs={{0,32},{8,40},{16,48},{24,56},{32,64},{40,72},{48,80},{56,88},{64,... | collective-permute-start | bytes 491528 | tf_op jit(solution)/shard_map/ppermute | solution.py:450
  35.2 7.3 %collective-permute-start.12 = (bf16[5,16,1024]{2,1,0:T(8,128)(2,1)S(1)}, bf16[5,16,1024]{2,1,0:T(8,128)(2,1)S(1)}, u32[]{:S(2)}, u32[]{:S(2)}) collective-permute-start(bf16[5,16,1024]{2,1,0:T(8,128)(2,1)S(1)} %slice.19), channel_id=1, source_target_pairs={{0,224},{8,232},{16,240},{24,248},{32,0},{40,8},{48,16},{56,24},{6... | collective-permute-start | bytes 491528 | tf_op jit(solution)/shard_map/ppermute | solution.py:450
  38.7 12.3 %collective-permute-start.7 = (bf16[10,16,1024]{2,1,0:T(8,128)(2,1)S(1)}, bf16[10,16,1024]{2,1,0:T(8,128)(2,1)S(1)}, u32[]{:S(2)}, u32[]{:S(2)}) collective-permute-start(bf16[10,16,1024]{2,1,0:T(8,128)(2,1)S(1)} %get-tuple-element.48), channel_id=1, source_target_pairs={{0,16},{8,24},{16,0},{24,8},{32,48},{40,56},{48,32},{56,40},{64,80... | collective-permute-start | bytes 983048 | tf_op jit(solution)/shard_map/ppermute | solution.py:450
  41.2 15.0 %collective-permute-start.8 = (bf16[10,16,1024]{2,1,0:T(8,128)(2,1)S(1)}, bf16[10,16,1024]{2,1,0:T(8,128)(2,1)S(1)}, u32[]{:S(2)}, u32[]{:S(2)}) collective-permute-start(bf16[10,16,1024]{2,1,0:T(8,128)(2,1)S(1)} %get-tuple-element.49), channel_id=1, source_target_pairs={{0,24},{8,0},{16,8},{24,16},{32,56},{40,32},{48,40},{56,48},{64,88... | collective-permute-start | bytes 983048 | tf_op jit(solution)/shard_map/ppermute | solution.py:450
  43.3 12.9 %collective-permute-start.13 = (bf16[6,16,1024]{2,1,0:T(8,128)(2,1)S(1)}, bf16[6,16,1024]{2,1,0:T(8,128)(2,1)S(1)}, u32[]{:S(2)}, u32[]{:S(2)}) collective-permute-start(bf16[6,16,1024]{2,1,0:T(8,128)(2,1)S(1)} %get-tuple-element.53), channel_id=1, source_target_pairs={{0,8},{8,16},{16,24},{24,0},{32,40},{40,48},{48,56},{56,32},{64,72... | collective-permute-start | bytes 589832 | tf_op jit(solution)/shard_map/ppermute | solution.py:450
  44.3 11.9 %collective-permute-start.14 = (bf16[6,16,1024]{2,1,0:T(8,128)(2,1)S(1)}, bf16[6,16,1024]{2,1,0:T(8,128)(2,1)S(1)}, u32[]{:S(2)}, u32[]{:S(2)}) collective-permute-start(bf16[6,16,1024]{2,1,0:T(8,128)(2,1)S(1)} %get-tuple-element.54), channel_id=1, source_target_pairs={{0,16},{8,24},{16,0},{24,8},{32,48},{40,56},{48,32},{56,40},{64,80... | collective-permute-start | bytes 589832 | tf_op jit(solution)/shard_map/ppermute | solution.py:450
  47.8 12.7 %collective-permute-start.15 = (bf16[6,16,1024]{2,1,0:T(8,128)(2,1)S(1)}, bf16[6,16,1024]{2,1,0:T(8,128)(2,1)S(1)}, u32[]{:S(2)}, u32[]{:S(2)}) collective-permute-start(bf16[6,16,1024]{2,1,0:T(8,128)(2,1)S(1)} %get-tuple-element.55), channel_id=1, source_target_pairs={{0,24},{8,0},{16,8},{24,16},{32,56},{40,32},{48,40},{56,48},{64,88... | collective-permute-start | bytes 589832 | tf_op jit(solution)/shard_map/ppermute | solution.py:450
  90.4 12.8 %collective-permute-start.30 = (bf16[5,16,1024]{2,1,0:T(8,128)(2,1)S(1)}, bf16[5,16,1024]{2,1,0:T(8,128)(2,1)S(1)}, u32[]{:S(2)}, u32[]{:S(2)}) collective-permute-start(bf16[5,16,1024]{2,1,0:T(8,128)(2,1)S(1)} %get-tuple-element.82), channel_id=1, source_target_pairs={{0,32},{8,40},{16,48},{24,56},{32,64},{40,72},{48,80},{56,88},{64,... | collective-permute-start | bytes 491528 | tf_op jit(solution)/shard_map/ppermute | solution.py:450
  90.4 12.7 %collective-permute-start.31 = (bf16[5,16,1024]{2,1,0:T(8,128)(2,1)S(1)}, bf16[5,16,1024]{2,1,0:T(8,128)(2,1)S(1)}, u32[]{:S(2)}, u32[]{:S(2)}) collective-permute-start(bf16[5,16,1024]{2,1,0:T(8,128)(2,1)S(1)} %get-tuple-element.83), channel_id=1, source_target_pairs={{0,224},{8,232},{16,240},{24,248},{32,0},{40,8},{48,16},{56,24},{6... | collective-permute-start | bytes 491528 | tf_op jit(solution)/shard_map/ppermute | solution.py:450
  95.8 7.4 %collective-permute-start.26 = (bf16[4,16,1024]{2,1,0:T(8,128)(2,1)S(1)}, bf16[4,16,1024]{2,1,0:T(8,128)(2,1)S(1)}, u32[]{:S(2)}, u32[]{:S(2)}) collective-permute-start(bf16[4,16,1024]{2,1,0:T(8,128)(2,1)S(1)} %get-tuple-element.77), channel_id=1, source_target_pairs={{0,8},{8,16},{16,24},{24,0},{32,40},{40,48},{48,56},{56,32},{64,72... | collective-permute-start | bytes 393224 | tf_op jit(solution)/shard_map/ppermute | solution.py:450
  104.2 13.0 %collective-permute-start.32 = (bf16[10,16,1024]{2,1,0:T(8,128)(2,1)S(1)}, bf16[10,16,1024]{2,1,0:T(8,128)(2,1)S(1)}, u32[]{:S(2)}, u32[]{:S(2)}) collective-permute-start(bf16[10,16,1024]{2,1,0:T(8,128)(2,1)S(1)} %get-tuple-element.84), channel_id=1, source_target_pairs={{0,32},{8,40},{16,48},{24,56},{32,64},{40,72},{48,80},{56,88},{64,... | collective-permute-start | bytes 983048 | tf_op jit(solution)/shard_map/ppermute | solution.py:450
  104.3 12.9 %collective-permute-start.33 = (bf16[10,16,1024]{2,1,0:T(8,128)(2,1)S(1)}, bf16[10,16,1024]{2,1,0:T(8,128)(2,1)S(1)}, u32[]{:S(2)}, u32[]{:S(2)}) collective-permute-start(bf16[10,16,1024]{2,1,0:T(8,128)(2,1)S(1)} %get-tuple-element.85), channel_id=1, source_target_pairs={{0,224},{8,232},{16,240},{24,248},{32,0},{40,8},{48,16},{56,24},{6... | collective-permute-start | bytes 983048 | tf_op jit(solution)/shard_map/ppermute | solution.py:450
  118.2 14.3 %collective-permute-start.34 = (bf16[10,16,1024]{2,1,0:T(8,128)(2,1)S(1)}, bf16[10,16,1024]{2,1,0:T(8,128)(2,1)S(1)}, u32[]{:S(2)}, u32[]{:S(2)}) collective-permute-start(bf16[10,16,1024]{2,1,0:T(8,128)(2,1)S(1)} %get-tuple-element.86), channel_id=1, source_target_pairs={{0,32},{8,40},{16,48},{24,56},{32,64},{40,72},{48,80},{56,88},{64,... | collective-permute-start | bytes 983048 | tf_op jit(solution)/shard_map/ppermute | solution.py:450
  118.3 14.2 %collective-permute-start.35 = (bf16[10,16,1024]{2,1,0:T(8,128)(2,1)S(1)}, bf16[10,16,1024]{2,1,0:T(8,128)(2,1)S(1)}, u32[]{:S(2)}, u32[]{:S(2)}) collective-permute-start(bf16[10,16,1024]{2,1,0:T(8,128)(2,1)S(1)} %get-tuple-element.87), channel_id=1, source_target_pairs={{0,224},{8,232},{16,240},{24,248},{32,0},{40,8},{48,16},{56,24},{6... | collective-permute-start | bytes 983048 | tf_op jit(solution)/shard_map/ppermute | solution.py:450
  124.2 8.4 %collective-permute-start.20 = (bf16[6,16,1024]{2,1,0:T(8,128)(2,1)S(1)}, bf16[6,16,1024]{2,1,0:T(8,128)(2,1)S(1)}, u32[]{:S(2)}, u32[]{:S(2)}) collective-permute-start(bf16[6,16,1024]{2,1,0:T(8,128)(2,1)S(1)} %get-tuple-element.69), channel_id=1, source_target_pairs={{0,8},{8,16},{16,24},{24,0},{32,40},{40,48},{48,56},{56,32},{64,72... | collective-permute-start | bytes 589832 | tf_op jit(solution)/shard_map/ppermute | solution.py:450
  133.5 8.4 %collective-permute-start.36 = (bf16[10,16,1024]{2,1,0:T(8,128)(2,1)S(1)}, bf16[10,16,1024]{2,1,0:T(8,128)(2,1)S(1)}, u32[]{:S(2)}, u32[]{:S(2)}) collective-permute-start(bf16[10,16,1024]{2,1,0:T(8,128)(2,1)S(1)} %get-tuple-element.88), channel_id=1, source_target_pairs={{0,32},{8,40},{16,48},{24,56},{32,64},{40,72},{48,80},{56,88},{64,... | collective-permute-start | bytes 983048 | tf_op jit(solution)/shard_map/ppermute | solution.py:450
  133.6 8.3 %collective-permute-start.37 = (bf16[10,16,1024]{2,1,0:T(8,128)(2,1)S(1)}, bf16[10,16,1024]{2,1,0:T(8,128)(2,1)S(1)}, u32[]{:S(2)}, u32[]{:S(2)}) collective-permute-start(bf16[10,16,1024]{2,1,0:T(8,128)(2,1)S(1)} %get-tuple-element.89), channel_id=1, source_target_pairs={{0,224},{8,232},{16,240},{24,248},{32,0},{40,8},{48,16},{56,24},{6... | collective-permute-start | bytes 983048 | tf_op jit(solution)/shard_map/ppermute | solution.py:450
  (14 other events, 80.3 us)

commit v5 on v4

--- a/solution.py
+++ b/solution.py
@@ -120,30 +120,34 @@
     )(ref_of, place, *flat)
 
 
-def spread(ref_of, place, own, other, phase, nz):
+def spread(ref_of, place, own, other, phases, nz):
     tail = own.shape[1:]
-    slots = slots_of(phase, nz)
-    first, stride, _ = span_of(phase, nz)
+    spans = [span_of(phase, nz) for phase in phases]
 
     def body(r_ref, p_ref, own_ref, other_ref, *outs):
-        def place_slots(k, carry):
-            plane = (p_ref[0] + nz + first + stride * (k // CAP)) % nz
-            at = [jnp.maximum(r_ref[j, plane * CAP + k % CAP], 0) for j in range(NY)]
-            for j in range(NY):
-                total = own_ref[at[j]] + other_ref[at[j]].astype(F32)
-                outs[j][k] = total.astype(BF)
-            return carry
-
-        lax.fori_loop(0, len(slots), place_slots, 0)
-
-    return pl.pallas_call(
+        for n, (first, stride, count) in enumerate(spans):
+
+            def place_slots(k, carry):
+                plane = (p_ref[0] + nz + first + stride * (k // CAP)) % nz
+                at = [jnp.maximum(r_ref[j, plane * CAP + k % CAP], 0) for j in range(NY)]
+                for j in range(NY):
+                    total = own_ref[at[j]] + other_ref[at[j]].astype(F32)
+                    outs[n * NY + j][k] = total.astype(BF)
+                return carry
+
+            lax.fori_loop(0, count * CAP, place_slots, 0)
+
+    flat = pl.pallas_call(
         body,
         in_specs=[SMEM, SMEM, VMEM, VMEM],
-        out_specs=[VMEM] * NY,
-        out_shape=[jax.ShapeDtypeStruct((len(slots),) + tail, BF)] * NY,
+        out_specs=[VMEM] * (NY * len(phases)),
+        out_shape=[
+            jax.ShapeDtypeStruct((count * CAP,) + tail, BF) for *_, count in spans for _ in range(NY)
+        ],
         compiler_params=SMALL,
         name="spread",
     )(ref_of, place, own, other)
+    return [flat[n * NY : (n + 1) * NY] for n in range(len(phases))]
 
 
 def gather_grads(table, place, parts, phase, before, step, nz, rows_here):
@@ -182,7 +186,7 @@
             acc[1, r + cut] = prev[1][r].astype(F32)
             return carry
 
-        lax.fori_loop(0, rows_here, fill, 0)
+        lax.fori_loop(0, rows_here, fill, 0, unroll=2)
         if halves:
             lax.fori_loop(0, cut, low, 0)
             lax.fori_loop(0, rows_here - cut, high, 0)
@@ -215,7 +219,7 @@
             lax.fori_loop(0, cut, drain_low, 0)
             lax.fori_loop(0, rows_here - cut, drain_high, 0)
         else:
-            lax.fori_loop(0, rows_here, drain, 0)
+            lax.fori_loop(0, rows_here, drain, 0, unroll=2)
 
     return pl.pallas_call(
         body,
@@ -325,13 +329,13 @@
         theirs = pl.ds(pl.multiple_of((1 - p_ref[2]) * half, half), half)
 
         def project(n, carry):
-            c = pl.ds(pl.multiple_of(n * WIDE, WIDE), WIDE)
+            c = pl.ds(pl.multiple_of(n * half, half), half)
             for part, w_ref, out in ((ka_ref, wk_ref, k_ref), (va_ref, wv_ref, v_ref)):
                 total = jnp.dot(oth_ref[:rows], w_ref[theirs, c], preferred_element_type=F32)
                 out[:, c] = (part[:, c] + total).astype(BF)
             return carry
 
-        lax.fori_loop(0, half // WIDE, project, 0)
+        lax.fori_loop(0, half // half, project, 0)
 
         def at(u):
             return (
@@ -381,8 +385,8 @@
         store.start()
 
         def back(n, carry):
-            c = pl.ds(pl.multiple_of(n * WIDE, WIDE), WIDE)
-            at_rows = pl.ds(pl.multiple_of((1 - p_ref[2]) * half + n * WIDE, WIDE), WIDE)
+            c = pl.ds(pl.multiple_of(n * half, half), half)
+            at_rows = pl.ds(pl.multiple_of((1 - p_ref[2]) * half + n * half, half), half)
             total = lax.dot_general(
                 dk_ref[...], wk_ref[at_rows, :], nt, preferred_element_type=F32
             )
@@ -392,7 +396,7 @@
             poth_ref[:, c] = total.astype(BF)
             return carry
 
-        lax.fori_loop(0, half // WIDE, back, 0)
+        lax.fori_loop(0, half // half, back, 0)
         store.wait()
 
     return pl.pallas_call(
@@ -494,8 +498,11 @@
     partial_own, came = partial_own.reshape(shape), came.reshape(shape)
 
     before = ()
-    for phase in BACK:
-        parts = spread(ref_of, place, partial_own, came, phase, nz)
+    for n, phase in enumerate(BACK):
+        if n in (0, len(BACK) - 1):
+            ahead = BACK[n:] if n else BACK[:-1]
+            sends = dict(enumerate(spread(ref_of, place, partial_own, came, ahead, nz), n))
+        parts = sends[n]
         parts = [parts[0]] + [move(parts[j], 0, -j) for j in range(1, NY)]
         for step in phase:
             total = gather_grads(table, place, parts, phase, before, step, nz, rows_here)

time: 144 us -> 142 us (0.986)
  Pallas kernels: 29.3 us -> 27.6 us
    pallas_call x4 -> x2, Pallas kernels: 2.96 us -> 1.83 us  [spread(): pl.pallas_call(body, in_specs=[SMEM, SMEM, VMEM, VMEM], out_specs=[VMEM]...]
  transfers between devices with their start and end apart: 38 -> 38, of which waited for: 20 -> 20; matrix products, arithmetic and copies ran while one was open for 1% -> 1% of each run, Pallas kernels for 10% -> 9%
where the time goes in v5:
time: 142 us
  starting transfers between devices  57.2 us (40%)
  waiting for transfers between devices  53.8 us (38%)
  Pallas kernels  27.6 us (19%)
    ppermute x36, starting transfers between devices, move(): return lax.ppermute(x, 'seq', ring(seq, dz, dy))  56.5 us
    ppermute x36, waiting for transfers between devices, move(): return lax.ppermute(x, 'seq', ring(seq, dz, dy))  53.8 us
    pallas_call x1, Pallas kernels, core_step(): pl.pallas_call(body, in_specs=[SMEM] + [VMEM] * 7, out_specs=[ANY] + [VME...  7.75 us
    pallas_call x5, Pallas kernels, gather_grads(): pl.pallas_call(body, in_specs=[SMEM, SMEM] + [VMEM] * (NY + len(before)),...  5.39 us
    pallas_call x2, Pallas kernels, fetch(): pl.pallas_call(body, in_specs=[pl.BlockSpec(memory_space=pltpu.HBM)] * co...  5.26 us
  transfers between devices with their start and end apart: 38, of which 20 were waited for; matrix products, arithmetic and copies ran while one was open for 1% of the time, Pallas kernels for 9%

profile of v5, /device:TPU:2, one launch (start us, length us, event | category | flops | bytes accessed | tf_op | source)
XLA Modules:
  0.0 141.6 jit_solution(918757204013130284)
XLA Ops:
  2.6 4.0 %collective-permute-start.2 = (bf16[10,16,1024]{2,1,0:T(8,128)(2,1)}, bf16[10,16,1024]{2,1,0:T(8,128)(2,1)S(1)}, u32[]{:S(2)}, u32[]{:S(2)}) collective-permute-start(bf16[10,16,1024]{2,1,0:T(8,128)(2,1)} %refs_0_.2), channel_id=1, source_target_pairs={{0,224},{8,232},{16,240},{24,248},{32,0},{40,8},{48,16},{56,24},{6... | collective-permute-start | bytes 983048 | tf_op jit(solution)/shard_map/ppermute | solution.py:454
  7.5 3.1 %collective-permute-start = (s32[1,22]{1,0:T(1,128)S(1)}, s32[1,22]{1,0:T(1,128)S(1)}, u32[]{:S(2)}, u32[]{:S(2)}) collective-permute-start(s32[1,22]{1,0:T(1,128)S(1)} %reshape.357), channel_id=1, source_target_pairs={{0,24},{8,0},{16,8},{24,16},{32,56},{40,32},{48,40},{56,48},{64,88... | collective-permute-start | bytes 272 | tf_op jit(solution)/shard_map/ppermute | solution.py:454
  11.9 2.5 %collective-permute-start.1 = (s32[2,22]{1,0:T(2,128)S(1)}, s32[2,22]{1,0:T(2,128)S(1)}, u32[]{:S(2)}, u32[]{:S(2)}) collective-permute-start(s32[2,22]{1,0:T(2,128)S(1)} %pad_add_fusion.1), channel_id=1, source_target_pairs={{0,16},{8,24},{16,0},{24,8},{32,48},{40,56},{48,32},{56,40},{64,80... | collective-permute-start | bytes 536 | tf_op jit(solution)/shard_map/ppermute | solution.py:454
  17.8 3.2 %collective-permute-start.4 = (bf16[10,16,1024]{2,1,0:T(8,128)(2,1)S(1)}, bf16[10,16,1024]{2,1,0:T(8,128)(2,1)S(1)}, u32[]{:S(2)}, u32[]{:S(2)}) collective-permute-start(bf16[10,16,1024]{2,1,0:T(8,128)(2,1)S(1)} %collective-permute-done.2.refs_1_), channel_id=1, source_target_pairs={{0,224},{8,232},{16,240},{24,248},{32,0},{40,8},{48,16},{56,24},{6... | collective-permute-start | bytes 983048 | tf_op jit(solution)/shard_map/ppermute | solution.py:454
  21.1 5.1 %collective-permute-done.5.refs_4_ = bf16[10,16,1024]{2,1,0:T(8,128)(2,1)S(1)} collective-permute-done((bf16[10,16,1024]{2,1,0:T(8,128)(2,1)S(1)}, bf16[10,16,1024]{2,1,0:T(8,128)(2,1)S(1)}, u32[]{:S(2)}, u32[]{:S(2)}) %collective-permute-start.5) | collective-permute-done | bytes 327712 | tf_op jit(solution)/shard_map/ppermute | solution.py:454
  26.2 3.2 %collective-permute-start.9 = (bf16[10,16,1024]{2,1,0:T(8,128)(2,1)S(1)}, bf16[10,16,1024]{2,1,0:T(8,128)(2,1)S(1)}, u32[]{:S(2)}, u32[]{:S(2)}) collective-permute-start(bf16[10,16,1024]{2,1,0:T(8,128)(2,1)S(1)} %collective-permute-done.4.refs_3_), channel_id=1, source_target_pairs={{0,224},{8,232},{16,240},{24,248},{32,0},{40,8},{48,16},{56,24},{6... | collective-permute-start | bytes 983048 | tf_op jit(solution)/shard_map/ppermute | solution.py:454
  31.9 3.1 %collective-permute-done.10.refs_1_ = bf16[10,16,1024]{2,1,0:T(8,128)(2,1)S(1)} collective-permute-done((bf16[10,16,1024]{2,1,0:T(8,128)(2,1)S(1)}, bf16[10,16,1024]{2,1,0:T(8,128)(2,1)S(1)}, u32[]{:S(2)}, u32[]{:S(2)}) %collective-permute-start.10) | collective-permute-done | bytes 327712 | tf_op jit(solution)/shard_map/ppermute | solution.py:454
  35.2 3.5 %collective-permute-start.12 = (bf16[5,16,1024]{2,1,0:T(8,128)(2,1)S(1)}, bf16[5,16,1024]{2,1,0:T(8,128)(2,1)S(1)}, u32[]{:S(2)}, u32[]{:S(2)}) collective-permute-start(bf16[5,16,1024]{2,1,0:T(8,128)(2,1)S(1)} %slice.19), channel_id=1, source_target_pairs={{0,224},{8,232},{16,240},{24,248},{32,0},{40,8},{48,16},{56,24},{6... | collective-permute-start | bytes 491528 | tf_op jit(solution)/shard_map/ppermute | solution.py:454
  38.7 2.5 %collective-permute-start.7 = (bf16[10,16,1024]{2,1,0:T(8,128)(2,1)S(1)}, bf16[10,16,1024]{2,1,0:T(8,128)(2,1)S(1)}, u32[]{:S(2)}, u32[]{:S(2)}) collective-permute-start(bf16[10,16,1024]{2,1,0:T(8,128)(2,1)S(1)} %get-tuple-element.48), channel_id=1, source_target_pairs={{0,16},{8,24},{16,0},{24,8},{32,48},{40,56},{48,32},{56,40},{64,80... | collective-permute-start | bytes 983048 | tf_op jit(solution)/shard_map/ppermute | solution.py:454
  44.3 3.5 %collective-permute-start.14 = (bf16[6,16,1024]{2,1,0:T(8,128)(2,1)S(1)}, bf16[6,16,1024]{2,1,0:T(8,128)(2,1)S(1)}, u32[]{:S(2)}, u32[]{:S(2)}) collective-permute-start(bf16[6,16,1024]{2,1,0:T(8,128)(2,1)S(1)} %get-tuple-element.54), channel_id=1, source_target_pairs={{0,16},{8,24},{16,0},{24,8},{32,48},{40,56},{48,32},{56,40},{64,80... | collective-permute-start | bytes 589832 | tf_op jit(solution)/shard_map/ppermute | solution.py:454
  51.0 5.2 %collective-permute-done.8.refs_3_ = bf16[10,16,1024]{2,1,0:T(8,128)(2,1)S(1)} collective-permute-done((bf16[10,16,1024]{2,1,0:T(8,128)(2,1)S(1)}, bf16[10,16,1024]{2,1,0:T(8,128)(2,1)S(1)}, u32[]{:S(2)}, u32[]{:S(2)}) %collective-permute-start.8) | collective-permute-done | bytes 327712 | tf_op jit(solution)/shard_map/ppermute | solution.py:454
  56.2 4.3 %collective-permute-done.15.refs_7_ = bf16[6,16,1024]{2,1,0:T(8,128)(2,1)S(1)} collective-permute-done((bf16[6,16,1024]{2,1,0:T(8,128)(2,1)S(1)}, bf16[6,16,1024]{2,1,0:T(8,128)(2,1)S(1)}, u32[]{:S(2)}, u32[]{:S(2)}) %collective-permute-start.15) | collective-permute-done | bytes 196640 | tf_op jit(solution)/shard_map/ppermute | solution.py:454
  61.6 4.3 %fetch.3 = (bf16[2048,1024]{1,0:T(8,128)(2,1)S(1)}, bf16[2048,1024]{1,0:T(8,128)(2,1)S(1)}, bf16[704,1024]{1,0:T(8,128)(2,1)S(1)}, bf16[704,1024]{1,0:T(8,128)(2,1)S(1)}) custom-call(bf16[2048,1024]{1,0:T(8,128)(2,1)} %refs_0_.3, bf16[2048,1024]{1,0:T(8,128)(2,1)} %refs_1_.1, bf16[704,1024]{1,0:T(8,128)(2,1)} %refs_2_.1, bf16[704,1024]{1,0:T(8,128)(2,1)} %refs_3_.1), custom_call_target="tpu_custom_call" | custom-call | tf_op jit(solution)/shard_map/fetch/pallas_call | solution.py:248
  68.3 7.8 %core_step.1 = (bf16[704,1024]{1,0:T(8,128)(2,1)}, bf16[352,1024]{1,0:T(8,128)(2,1)S(1)}, bf16[352,1024]{1,0:T(8,128)(2,1)S(1)}, bf16[352,1024]{1,0:T(8,128)(2,1)S(1)}) custom-call(s32[3]{0:T(128)S(1)} %pad_add_fusion.2.p_ref, f32[352,1024]{1,0:T(8,128)S(1)} %get-tuple-element.58.ka_ref, f32[352,1024]{1,0:T(8,128)S(1)} %get-tuple-element.59.va_ref, ...), custom_call_target="tpu_custom_call" | custom-call | tf_op jit(solution)/shard_map/core_step/pallas_call | solution.py:402
  80.1 2.6 %collective-permute-start.27 = (bf16[2,16,1024]{2,1,0:T(8,128)(2,1)S(1)}, bf16[2,16,1024]{2,1,0:T(8,128)(2,1)S(1)}, u32[]{:S(2)}, u32[]{:S(2)}) collective-permute-start(bf16[2,16,1024]{2,1,0:T(8,128)(2,1)S(1)} %get-tuple-element.79), channel_id=1, source_target_pairs={{0,24},{8,0},{16,8},{24,16},{32,56},{40,32},{48,40},{56,48},{64,88... | collective-permute-start | bytes 196616 | tf_op jit(solution)/shard_map/ppermute | solution.py:454
  85.7 3.0 %collective-permute-done.28.refs_2_ = bf16[2,16,1024]{2,1,0:T(8,128)(2,1)S(1)} collective-permute-done((bf16[2,16,1024]{2,1,0:T(8,128)(2,1)S(1)}, bf16[2,16,1024]{2,1,0:T(8,128)(2,1)S(1)}, u32[]{:S(2)}, u32[]{:S(2)}) %collective-permute-start.28) | collective-permute-done | bytes 65568 | tf_op jit(solution)/shard_map/ppermute | solution.py:454
  90.2 3.2 %collective-permute-start.31 = (bf16[5,16,1024]{2,1,0:T(8,128)(2,1)S(1)}, bf16[5,16,1024]{2,1,0:T(8,128)(2,1)S(1)}, u32[]{:S(2)}, u32[]{:S(2)}) collective-permute-start(bf16[5,16,1024]{2,1,0:T(8,128)(2,1)S(1)} %get-tuple-element.83), channel_id=1, source_target_pairs={{0,224},{8,232},{16,240},{24,248},{32,0},{40,8},{48,16},{56,24},{6... | collective-permute-start | bytes 491528 | tf_op jit(solution)/shard_map/ppermute | solution.py:454
  103.4 3.2 %collective-permute-start.33 = (bf16[10,16,1024]{2,1,0:T(8,128)(2,1)S(1)}, bf16[10,16,1024]{2,1,0:T(8,128)(2,1)S(1)}, u32[]{:S(2)}, u32[]{:S(2)}) collective-permute-start(bf16[10,16,1024]{2,1,0:T(8,128)(2,1)S(1)} %get-tuple-element.85), channel_id=1, source_target_pairs={{0,224},{8,232},{16,240},{24,248},{32,0},{40,8},{48,16},{56,24},{6... | collective-permute-start | bytes 983048 | tf_op jit(solution)/shard_map/ppermute | solution.py:454
  108.7 2.9 %collective-permute-done.21.refs_1_ = bf16[4,16,1024]{2,1,0:T(8,128)(2,1)S(1)} collective-permute-done((bf16[4,16,1024]{2,1,0:T(8,128)(2,1)S(1)}, bf16[4,16,1024]{2,1,0:T(8,128)(2,1)S(1)}, u32[]{:S(2)}, u32[]{:S(2)}) %collective-permute-start.21) | collective-permute-done | bytes 131104 | tf_op jit(solution)/shard_map/ppermute | solution.py:454
  111.6 2.6 %collective-permute-done.22.refs_2_ = bf16[4,16,1024]{2,1,0:T(8,128)(2,1)S(1)} collective-permute-done((bf16[4,16,1024]{2,1,0:T(8,128)(2,1)S(1)}, bf16[4,16,1024]{2,1,0:T(8,128)(2,1)S(1)}, u32[]{:S(2)}, u32[]{:S(2)}) %collective-permute-start.22) | collective-permute-done | bytes 131104 | tf_op jit(solution)/shard_map/ppermute | solution.py:454
  116.6 3.2 %collective-permute-start.35 = (bf16[10,16,1024]{2,1,0:T(8,128)(2,1)S(1)}, bf16[10,16,1024]{2,1,0:T(8,128)(2,1)S(1)}, u32[]{:S(2)}, u32[]{:S(2)}) collective-permute-start(bf16[10,16,1024]{2,1,0:T(8,128)(2,1)S(1)} %get-tuple-element.87), channel_id=1, source_target_pairs={{0,224},{8,232},{16,240},{24,248},{32,0},{40,8},{48,16},{56,24},{6... | collective-permute-start | bytes 983048 | tf_op jit(solution)/shard_map/ppermute | solution.py:454
  123.1 3.3 %collective-permute-done.18.refs_1_ = bf16[6,16,1024]{2,1,0:T(8,128)(2,1)S(1)} collective-permute-done((bf16[6,16,1024]{2,1,0:T(8,128)(2,1)S(1)}, bf16[6,16,1024]{2,1,0:T(8,128)(2,1)S(1)}, u32[]{:S(2)}, u32[]{:S(2)}) %collective-permute-start.18) | collective-permute-done | bytes 196640 | tf_op jit(solution)/shard_map/ppermute | solution.py:454
  131.8 3.2 %collective-permute-start.37 = (bf16[10,16,1024]{2,1,0:T(8,128)(2,1)S(1)}, bf16[10,16,1024]{2,1,0:T(8,128)(2,1)S(1)}, u32[]{:S(2)}, u32[]{:S(2)}) collective-permute-start(bf16[10,16,1024]{2,1,0:T(8,128)(2,1)S(1)} %get-tuple-element.89), channel_id=1, source_target_pairs={{0,224},{8,232},{16,240},{24,248},{32,0},{40,8},{48,16},{56,24},{6... | collective-permute-start | bytes 983048 | tf_op jit(solution)/shard_map/ppermute | solution.py:454
  135.0 5.0 %collective-permute-done.36.refs_4_ = bf16[10,16,1024]{2,1,0:T(8,128)(2,1)S(1)} collective-permute-done((bf16[10,16,1024]{2,1,0:T(8,128)(2,1)S(1)}, bf16[10,16,1024]{2,1,0:T(8,128)(2,1)S(1)}, u32[]{:S(2)}, u32[]{:S(2)}) %collective-permute-start.36) | collective-permute-done | bytes 327712 | tf_op jit(solution)/shard_map/ppermute | solution.py:454
  (88 shorter events, 53.0 us)
Async XLA Ops:
  0.6 17.1 %collective-permute-start.3 = (bf16[10,16,1024]{2,1,0:T(8,128)(2,1)}, bf16[10,16,1024]{2,1,0:T(8,128)(2,1)S(1)}, u32[]{:S(2)}, u32[]{:S(2)}) collective-permute-start(bf16[10,16,1024]{2,1,0:T(8,128)(2,1)} %refs_0_.2), channel_id=1, source_target_pairs={{0,32},{8,40},{16,48},{24,56},{32,64},{40,72},{48,80},{56,88},{64,... | collective-permute-start | bytes 983048 | tf_op jit(solution)/shard_map/ppermute | solution.py:454
  2.6 15.2 %collective-permute-start.2 = (bf16[10,16,1024]{2,1,0:T(8,128)(2,1)}, bf16[10,16,1024]{2,1,0:T(8,128)(2,1)S(1)}, u32[]{:S(2)}, u32[]{:S(2)}) collective-permute-start(bf16[10,16,1024]{2,1,0:T(8,128)(2,1)} %refs_0_.2), channel_id=1, source_target_pairs={{0,224},{8,232},{16,240},{24,248},{32,0},{40,8},{48,16},{56,24},{6... | collective-permute-start | bytes 983048 | tf_op jit(solution)/shard_map/ppermute | solution.py:454
  17.7 8.5 %collective-permute-start.5 = (bf16[10,16,1024]{2,1,0:T(8,128)(2,1)S(1)}, bf16[10,16,1024]{2,1,0:T(8,128)(2,1)S(1)}, u32[]{:S(2)}, u32[]{:S(2)}) collective-permute-start(bf16[10,16,1024]{2,1,0:T(8,128)(2,1)S(1)} %collective-permute-done.3.refs_2_), channel_id=1, source_target_pairs={{0,32},{8,40},{16,48},{24,56},{32,64},{40,72},{48,80},{56,88},{64,... | collective-permute-start | bytes 983048 | tf_op jit(solution)/shard_map/ppermute | solution.py:454
  17.8 8.4 %collective-permute-start.4 = (bf16[10,16,1024]{2,1,0:T(8,128)(2,1)S(1)}, bf16[10,16,1024]{2,1,0:T(8,128)(2,1)S(1)}, u32[]{:S(2)}, u32[]{:S(2)}) collective-permute-start(bf16[10,16,1024]{2,1,0:T(8,128)(2,1)S(1)} %collective-permute-done.2.refs_1_), channel_id=1, source_target_pairs={{0,224},{8,232},{16,240},{24,248},{32,0},{40,8},{48,16},{56,24},{6... | collective-permute-start | bytes 983048 | tf_op jit(solution)/shard_map/ppermute | solution.py:454
  26.2 8.8 %collective-permute-start.10 = (bf16[10,16,1024]{2,1,0:T(8,128)(2,1)S(1)}, bf16[10,16,1024]{2,1,0:T(8,128)(2,1)S(1)}, u32[]{:S(2)}, u32[]{:S(2)}) collective-permute-start(bf16[10,16,1024]{2,1,0:T(8,128)(2,1)S(1)} %collective-permute-done.5.refs_4_), channel_id=1, source_target_pairs={{0,32},{8,40},{16,48},{24,56},{32,64},{40,72},{48,80},{56,88},{64,... | collective-permute-start | bytes 983048 | tf_op jit(solution)/shard_map/ppermute | solution.py:454
  26.2 8.8 %collective-permute-start.9 = (bf16[10,16,1024]{2,1,0:T(8,128)(2,1)S(1)}, bf16[10,16,1024]{2,1,0:T(8,128)(2,1)S(1)}, u32[]{:S(2)}, u32[]{:S(2)}) collective-permute-start(bf16[10,16,1024]{2,1,0:T(8,128)(2,1)S(1)} %collective-permute-done.4.refs_3_), channel_id=1, source_target_pairs={{0,224},{8,232},{16,240},{24,248},{32,0},{40,8},{48,16},{56,24},{6... | collective-permute-start | bytes 983048 | tf_op jit(solution)/shard_map/ppermute | solution.py:454
  30.3 17.5 %collective-permute-start.6 = (bf16[10,16,1024]{2,1,0:T(8,128)(2,1)S(1)}, bf16[10,16,1024]{2,1,0:T(8,128)(2,1)S(1)}, u32[]{:S(2)}, u32[]{:S(2)}) collective-permute-start(bf16[10,16,1024]{2,1,0:T(8,128)(2,1)S(1)} %get-tuple-element.47), channel_id=1, source_target_pairs={{0,8},{8,16},{16,24},{24,0},{32,40},{40,48},{48,56},{56,32},{64,72... | collective-permute-start | bytes 983048 | tf_op jit(solution)/shard_map/ppermute | solution.py:454
  35.1 7.4 %collective-permute-start.11 = (bf16[5,16,1024]{2,1,0:T(8,128)(2,1)S(1)}, bf16[5,16,1024]{2,1,0:T(8,128)(2,1)S(1)}, u32[]{:S(2)}, u32[]{:S(2)}) collective-permute-start(bf16[5,16,1024]{2,1,0:T(8,128)(2,1)S(1)} %slice.20), channel_id=1, source_target_pairs={{0,32},{8,40},{16,48},{24,56},{32,64},{40,72},{48,80},{56,88},{64,... | collective-permute-start | bytes 491528 | tf_op jit(solution)/shard_map/ppermute | solution.py:454
  35.2 7.3 %collective-permute-start.12 = (bf16[5,16,1024]{2,1,0:T(8,128)(2,1)S(1)}, bf16[5,16,1024]{2,1,0:T(8,128)(2,1)S(1)}, u32[]{:S(2)}, u32[]{:S(2)}) collective-permute-start(bf16[5,16,1024]{2,1,0:T(8,128)(2,1)S(1)} %slice.19), channel_id=1, source_target_pairs={{0,224},{8,232},{16,240},{24,248},{32,0},{40,8},{48,16},{56,24},{6... | collective-permute-start | bytes 491528 | tf_op jit(solution)/shard_map/ppermute | solution.py:454
  38.7 12.3 %collective-permute-start.7 = (bf16[10,16,1024]{2,1,0:T(8,128)(2,1)S(1)}, bf16[10,16,1024]{2,1,0:T(8,128)(2,1)S(1)}, u32[]{:S(2)}, u32[]{:S(2)}) collective-permute-start(bf16[10,16,1024]{2,1,0:T(8,128)(2,1)S(1)} %get-tuple-element.48), channel_id=1, source_target_pairs={{0,16},{8,24},{16,0},{24,8},{32,48},{40,56},{48,32},{56,40},{64,80... | collective-permute-start | bytes 983048 | tf_op jit(solution)/shard_map/ppermute | solution.py:454
  41.2 15.0 %collective-permute-start.8 = (bf16[10,16,1024]{2,1,0:T(8,128)(2,1)S(1)}, bf16[10,16,1024]{2,1,0:T(8,128)(2,1)S(1)}, u32[]{:S(2)}, u32[]{:S(2)}) collective-permute-start(bf16[10,16,1024]{2,1,0:T(8,128)(2,1)S(1)} %get-tuple-element.49), channel_id=1, source_target_pairs={{0,24},{8,0},{16,8},{24,16},{32,56},{40,32},{48,40},{56,48},{64,88... | collective-permute-start | bytes 983048 | tf_op jit(solution)/shard_map/ppermute | solution.py:454
  43.3 12.9 %collective-permute-start.13 = (bf16[6,16,1024]{2,1,0:T(8,128)(2,1)S(1)}, bf16[6,16,1024]{2,1,0:T(8,128)(2,1)S(1)}, u32[]{:S(2)}, u32[]{:S(2)}) collective-permute-start(bf16[6,16,1024]{2,1,0:T(8,128)(2,1)S(1)} %get-tuple-element.53), channel_id=1, source_target_pairs={{0,8},{8,16},{16,24},{24,0},{32,40},{40,48},{48,56},{56,32},{64,72... | collective-permute-start | bytes 589832 | tf_op jit(solution)/shard_map/ppermute | solution.py:454
  44.3 11.9 %collective-permute-start.14 = (bf16[6,16,1024]{2,1,0:T(8,128)(2,1)S(1)}, bf16[6,16,1024]{2,1,0:T(8,128)(2,1)S(1)}, u32[]{:S(2)}, u32[]{:S(2)}) collective-permute-start(bf16[6,16,1024]{2,1,0:T(8,128)(2,1)S(1)} %get-tuple-element.54), channel_id=1, source_target_pairs={{0,16},{8,24},{16,0},{24,8},{32,48},{40,56},{48,32},{56,40},{64,80... | collective-permute-start | bytes 589832 | tf_op jit(solution)/shard_map/ppermute | solution.py:454
  47.8 12.7 %collective-permute-start.15 = (bf16[6,16,1024]{2,1,0:T(8,128)(2,1)S(1)}, bf16[6,16,1024]{2,1,0:T(8,128)(2,1)S(1)}, u32[]{:S(2)}, u32[]{:S(2)}) collective-permute-start(bf16[6,16,1024]{2,1,0:T(8,128)(2,1)S(1)} %get-tuple-element.55), channel_id=1, source_target_pairs={{0,24},{8,0},{16,8},{24,16},{32,56},{40,32},{48,40},{56,48},{64,88... | collective-permute-start | bytes 589832 | tf_op jit(solution)/shard_map/ppermute | solution.py:454
  90.1 12.0 %collective-permute-start.30 = (bf16[5,16,1024]{2,1,0:T(8,128)(2,1)S(1)}, bf16[5,16,1024]{2,1,0:T(8,128)(2,1)S(1)}, u32[]{:S(2)}, u32[]{:S(2)}) collective-permute-start(bf16[5,16,1024]{2,1,0:T(8,128)(2,1)S(1)} %get-tuple-element.82), channel_id=1, source_target_pairs={{0,32},{8,40},{16,48},{24,56},{32,64},{40,72},{48,80},{56,88},{64,... | collective-permute-start | bytes 491528 | tf_op jit(solution)/shard_map/ppermute | solution.py:454
  90.2 11.9 %collective-permute-start.31 = (bf16[5,16,1024]{2,1,0:T(8,128)(2,1)S(1)}, bf16[5,16,1024]{2,1,0:T(8,128)(2,1)S(1)}, u32[]{:S(2)}, u32[]{:S(2)}) collective-permute-start(bf16[5,16,1024]{2,1,0:T(8,128)(2,1)S(1)} %get-tuple-element.83), channel_id=1, source_target_pairs={{0,224},{8,232},{16,240},{24,248},{32,0},{40,8},{48,16},{56,24},{6... | collective-permute-start | bytes 491528 | tf_op jit(solution)/shard_map/ppermute | solution.py:454
  94.6 7.5 %collective-permute-start.26 = (bf16[4,16,1024]{2,1,0:T(8,128)(2,1)S(1)}, bf16[4,16,1024]{2,1,0:T(8,128)(2,1)S(1)}, u32[]{:S(2)}, u32[]{:S(2)}) collective-permute-start(bf16[4,16,1024]{2,1,0:T(8,128)(2,1)S(1)} %get-tuple-element.77), channel_id=1, source_target_pairs={{0,8},{8,16},{16,24},{24,0},{32,40},{40,48},{48,56},{56,32},{64,72... | collective-permute-start | bytes 393224 | tf_op jit(solution)/shard_map/ppermute | solution.py:454
  103.3 12.2 %collective-permute-start.32 = (bf16[10,16,1024]{2,1,0:T(8,128)(2,1)S(1)}, bf16[10,16,1024]{2,1,0:T(8,128)(2,1)S(1)}, u32[]{:S(2)}, u32[]{:S(2)}) collective-permute-start(bf16[10,16,1024]{2,1,0:T(8,128)(2,1)S(1)} %get-tuple-element.84), channel_id=1, source_target_pairs={{0,32},{8,40},{16,48},{24,56},{32,64},{40,72},{48,80},{56,88},{64,... | collective-permute-start | bytes 983048 | tf_op jit(solution)/shard_map/ppermute | solution.py:454
  103.4 12.1 %collective-permute-start.33 = (bf16[10,16,1024]{2,1,0:T(8,128)(2,1)S(1)}, bf16[10,16,1024]{2,1,0:T(8,128)(2,1)S(1)}, u32[]{:S(2)}, u32[]{:S(2)}) collective-permute-start(bf16[10,16,1024]{2,1,0:T(8,128)(2,1)S(1)} %get-tuple-element.85), channel_id=1, source_target_pairs={{0,224},{8,232},{16,240},{24,248},{32,0},{40,8},{48,16},{56,24},{6... | collective-permute-start | bytes 983048 | tf_op jit(solution)/shard_map/ppermute | solution.py:454
  116.5 14.3 %collective-permute-start.34 = (bf16[10,16,1024]{2,1,0:T(8,128)(2,1)S(1)}, bf16[10,16,1024]{2,1,0:T(8,128)(2,1)S(1)}, u32[]{:S(2)}, u32[]{:S(2)}) collective-permute-start(bf16[10,16,1024]{2,1,0:T(8,128)(2,1)S(1)} %get-tuple-element.86), channel_id=1, source_target_pairs={{0,32},{8,40},{16,48},{24,56},{32,64},{40,72},{48,80},{56,88},{64,... | collective-permute-start | bytes 983048 | tf_op jit(solution)/shard_map/ppermute | solution.py:454
  116.6 14.2 %collective-permute-start.35 = (bf16[10,16,1024]{2,1,0:T(8,128)(2,1)S(1)}, bf16[10,16,1024]{2,1,0:T(8,128)(2,1)S(1)}, u32[]{:S(2)}, u32[]{:S(2)}) collective-permute-start(bf16[10,16,1024]{2,1,0:T(8,128)(2,1)S(1)} %get-tuple-element.87), channel_id=1, source_target_pairs={{0,224},{8,232},{16,240},{24,248},{32,0},{40,8},{48,16},{56,24},{6... | collective-permute-start | bytes 983048 | tf_op jit(solution)/shard_map/ppermute | solution.py:454
  122.4 8.4 %collective-permute-start.20 = (bf16[6,16,1024]{2,1,0:T(8,128)(2,1)S(1)}, bf16[6,16,1024]{2,1,0:T(8,128)(2,1)S(1)}, u32[]{:S(2)}, u32[]{:S(2)}) collective-permute-start(bf16[6,16,1024]{2,1,0:T(8,128)(2,1)S(1)} %get-tuple-element.69), channel_id=1, source_target_pairs={{0,8},{8,16},{16,24},{24,0},{32,40},{40,48},{48,56},{56,32},{64,72... | collective-permute-start | bytes 589832 | tf_op jit(solution)/shard_map/ppermute | solution.py:454
  131.7 8.4 %collective-permute-start.36 = (bf16[10,16,1024]{2,1,0:T(8,128)(2,1)S(1)}, bf16[10,16,1024]{2,1,0:T(8,128)(2,1)S(1)}, u32[]{:S(2)}, u32[]{:S(2)}) collective-permute-start(bf16[10,16,1024]{2,1,0:T(8,128)(2,1)S(1)} %get-tuple-element.88), channel_id=1, source_target_pairs={{0,32},{8,40},{16,48},{24,56},{32,64},{40,72},{48,80},{56,88},{64,... | collective-permute-start | bytes 983048 | tf_op jit(solution)/shard_map/ppermute | solution.py:454
  131.8 8.3 %collective-permute-start.37 = (bf16[10,16,1024]{2,1,0:T(8,128)(2,1)S(1)}, bf16[10,16,1024]{2,1,0:T(8,128)(2,1)S(1)}, u32[]{:S(2)}, u32[]{:S(2)}) collective-permute-start(bf16[10,16,1024]{2,1,0:T(8,128)(2,1)S(1)} %get-tuple-element.89), channel_id=1, source_target_pairs={{0,224},{8,232},{16,240},{24,248},{32,0},{40,8},{48,16},{56,24},{6... | collective-permute-start | bytes 983048 | tf_op jit(solution)/shard_map/ppermute | solution.py:454
  (14 other events, 80.2 us)

commit v6 on v5

--- a/solution.py
+++ b/solution.py
@@ -13,8 +13,9 @@
 NY = 4
 CAP = 2
 SPARE = 2
-WIDE = 512
-
+
+
+SPREADS = {0: 1, 1: 3, 3: 4}
 
 SMEM = pl.BlockSpec(memory_space=pltpu.SMEM)
 VMEM = pl.BlockSpec(memory_space=pltpu.VMEM)
@@ -263,12 +264,12 @@
         mine = pl.ds(pl.multiple_of(p_ref[2] * half, half), half)
 
         def block(n, carry):
-            c = pl.ds(pl.multiple_of(n * WIDE, WIDE), WIDE)
+            c = pl.ds(pl.multiple_of(n * half, half), half)
             for w_ref, out in ((wk_ref, k_ref), (wv_ref, v_ref)):
                 out[:, c] = jnp.dot(own_ref[:rows], w_ref[mine, c], preferred_element_type=F32)
             return carry
 
-        lax.fori_loop(0, half // WIDE, block, 0)
+        lax.fori_loop(0, 1, block, 0)
 
     return pl.pallas_call(
         body,
@@ -286,14 +287,14 @@
 
     def body(p_ref, dk_ref, dv_ref, wk_ref, wv_ref, out):
         def block(n, carry):
-            c = pl.ds(pl.multiple_of(n * WIDE, WIDE), WIDE)
-            at = pl.ds(pl.multiple_of(p_ref[2] * half + n * WIDE, WIDE), WIDE)
+            c = pl.ds(pl.multiple_of(n * half, half), half)
+            at = pl.ds(pl.multiple_of(p_ref[2] * half + n * half, half), half)
             total = lax.dot_general(dk_ref[...], wk_ref[at, :], nt, preferred_element_type=F32)
             total += lax.dot_general(dv_ref[...], wv_ref[at, :], nt, preferred_element_type=F32)
             out[:, c] = total
             return carry
 
-        lax.fori_loop(0, half // WIDE, block, 0)
+        lax.fori_loop(0, 1, block, 0)
 
     return pl.pallas_call(
         body,
@@ -499,9 +500,9 @@
 
     before = ()
     for n, phase in enumerate(BACK):
-        if n in (0, len(BACK) - 1):
-            ahead = BACK[n:] if n else BACK[:-1]
-            sends = dict(enumerate(spread(ref_of, place, partial_own, came, ahead, nz), n))
+        if n in SPREADS:
+            some = BACK[n : SPREADS[n]]
+            sends = dict(enumerate(spread(ref_of, place, partial_own, came, some, nz), n))
         parts = sends[n]
         parts = [parts[0]] + [move(parts[j], 0, -j) for j in range(1, NY)]
         for step in phase:

time: 142 us -> 142 us (level)
  no operation moved by 1% of the time
where the time goes in v6:
time: 142 us
  starting transfers between devices  57.5 us (40%)
  waiting for transfers between devices  53.6 us (38%)
  Pallas kernels  27.6 us (19%)
    ppermute x36, starting transfers between devices, move(): return lax.ppermute(x, 'seq', ring(seq, dz, dy))  56.9 us
    ppermute x36, waiting for transfers between devices, move(): return lax.ppermute(x, 'seq', ring(seq, dz, dy))  53.5 us
    pallas_call x1, Pallas kernels, core_step(): pl.pallas_call(body, in_specs=[SMEM] + [VMEM] * 7, out_specs=[ANY] + [VME...  7.75 us
    pallas_call x2, Pallas kernels, fetch(): pl.pallas_call(body, in_specs=[pl.BlockSpec(memory_space=pltpu.HBM)] * co...  5.26 us
    pallas_call x5, Pallas kernels, gather_grads(): pl.pallas_call(body, in_specs=[SMEM, SMEM] + [VMEM] * (NY + len(before)),...  5.17 us
  transfers between devices with their start and end apart: 38, of which 20 were waited for; matrix products, arithmetic and copies ran while one was open for 1% of the time, Pallas kernels for 9%

profile of v6, /device:TPU:2, one launch (start us, length us, event | category | flops | bytes accessed | tf_op | source)
XLA Modules:
  0.0 141.7 jit_solution(11112202285303468363)
XLA Ops:
  2.6 4.0 %collective-permute-start.2 = (bf16[10,16,1024]{2,1,0:T(8,128)(2,1)}, bf16[10,16,1024]{2,1,0:T(8,128)(2,1)S(1)}, u32[]{:S(2)}, u32[]{:S(2)}) collective-permute-start(bf16[10,16,1024]{2,1,0:T(8,128)(2,1)} %refs_0_.2), channel_id=1, source_target_pairs={{0,224},{8,232},{16,240},{24,248},{32,0},{40,8},{48,16},{56,24},{6... | collective-permute-start | bytes 983048 | tf_op jit(solution)/shard_map/ppermute | solution.py:455
  7.5 3.1 %collective-permute-start = (s32[1,22]{1,0:T(1,128)S(1)}, s32[1,22]{1,0:T(1,128)S(1)}, u32[]{:S(2)}, u32[]{:S(2)}) collective-permute-start(s32[1,22]{1,0:T(1,128)S(1)} %reshape.357), channel_id=1, source_target_pairs={{0,24},{8,0},{16,8},{24,16},{32,56},{40,32},{48,40},{56,48},{64,88... | collective-permute-start | bytes 272 | tf_op jit(solution)/shard_map/ppermute | solution.py:455
  11.9 2.5 %collective-permute-start.1 = (s32[2,22]{1,0:T(2,128)S(1)}, s32[2,22]{1,0:T(2,128)S(1)}, u32[]{:S(2)}, u32[]{:S(2)}) collective-permute-start(s32[2,22]{1,0:T(2,128)S(1)} %pad_add_fusion.1), channel_id=1, source_target_pairs={{0,16},{8,24},{16,0},{24,8},{32,48},{40,56},{48,32},{56,40},{64,80... | collective-permute-start | bytes 536 | tf_op jit(solution)/shard_map/ppermute | solution.py:455
  17.8 3.2 %collective-permute-start.4 = (bf16[10,16,1024]{2,1,0:T(8,128)(2,1)S(1)}, bf16[10,16,1024]{2,1,0:T(8,128)(2,1)S(1)}, u32[]{:S(2)}, u32[]{:S(2)}) collective-permute-start(bf16[10,16,1024]{2,1,0:T(8,128)(2,1)S(1)} %collective-permute-done.2.refs_1_), channel_id=1, source_target_pairs={{0,224},{8,232},{16,240},{24,248},{32,0},{40,8},{48,16},{56,24},{6... | collective-permute-start | bytes 983048 | tf_op jit(solution)/shard_map/ppermute | solution.py:455
  21.1 5.1 %collective-permute-done.5.refs_4_ = bf16[10,16,1024]{2,1,0:T(8,128)(2,1)S(1)} collective-permute-done((bf16[10,16,1024]{2,1,0:T(8,128)(2,1)S(1)}, bf16[10,16,1024]{2,1,0:T(8,128)(2,1)S(1)}, u32[]{:S(2)}, u32[]{:S(2)}) %collective-permute-start.5) | collective-permute-done | bytes 327712 | tf_op jit(solution)/shard_map/ppermute | solution.py:455
  26.2 3.2 %collective-permute-start.9 = (bf16[10,16,1024]{2,1,0:T(8,128)(2,1)S(1)}, bf16[10,16,1024]{2,1,0:T(8,128)(2,1)S(1)}, u32[]{:S(2)}, u32[]{:S(2)}) collective-permute-start(bf16[10,16,1024]{2,1,0:T(8,128)(2,1)S(1)} %collective-permute-done.4.refs_3_), channel_id=1, source_target_pairs={{0,224},{8,232},{16,240},{24,248},{32,0},{40,8},{48,16},{56,24},{6... | collective-permute-start | bytes 983048 | tf_op jit(solution)/shard_map/ppermute | solution.py:455
  31.9 3.1 %collective-permute-done.10.refs_1_ = bf16[10,16,1024]{2,1,0:T(8,128)(2,1)S(1)} collective-permute-done((bf16[10,16,1024]{2,1,0:T(8,128)(2,1)S(1)}, bf16[10,16,1024]{2,1,0:T(8,128)(2,1)S(1)}, u32[]{:S(2)}, u32[]{:S(2)}) %collective-permute-start.10) | collective-permute-done | bytes 327712 | tf_op jit(solution)/shard_map/ppermute | solution.py:455
  35.2 3.5 %collective-permute-start.12 = (bf16[5,16,1024]{2,1,0:T(8,128)(2,1)S(1)}, bf16[5,16,1024]{2,1,0:T(8,128)(2,1)S(1)}, u32[]{:S(2)}, u32[]{:S(2)}) collective-permute-start(bf16[5,16,1024]{2,1,0:T(8,128)(2,1)S(1)} %slice.19), channel_id=1, source_target_pairs={{0,224},{8,232},{16,240},{24,248},{32,0},{40,8},{48,16},{56,24},{6... | collective-permute-start | bytes 491528 | tf_op jit(solution)/shard_map/ppermute | solution.py:455
  38.7 2.5 %collective-permute-start.7 = (bf16[10,16,1024]{2,1,0:T(8,128)(2,1)S(1)}, bf16[10,16,1024]{2,1,0:T(8,128)(2,1)S(1)}, u32[]{:S(2)}, u32[]{:S(2)}) collective-permute-start(bf16[10,16,1024]{2,1,0:T(8,128)(2,1)S(1)} %get-tuple-element.48), channel_id=1, source_target_pairs={{0,16},{8,24},{16,0},{24,8},{32,48},{40,56},{48,32},{56,40},{64,80... | collective-permute-start | bytes 983048 | tf_op jit(solution)/shard_map/ppermute | solution.py:455
  44.3 3.5 %collective-permute-start.14 = (bf16[6,16,1024]{2,1,0:T(8,128)(2,1)S(1)}, bf16[6,16,1024]{2,1,0:T(8,128)(2,1)S(1)}, u32[]{:S(2)}, u32[]{:S(2)}) collective-permute-start(bf16[6,16,1024]{2,1,0:T(8,128)(2,1)S(1)} %get-tuple-element.54), channel_id=1, source_target_pairs={{0,16},{8,24},{16,0},{24,8},{32,48},{40,56},{48,32},{56,40},{64,80... | collective-permute-start | bytes 589832 | tf_op jit(solution)/shard_map/ppermute | solution.py:455
  51.0 5.2 %collective-permute-done.8.refs_3_ = bf16[10,16,1024]{2,1,0:T(8,128)(2,1)S(1)} collective-permute-done((bf16[10,16,1024]{2,1,0:T(8,128)(2,1)S(1)}, bf16[10,16,1024]{2,1,0:T(8,128)(2,1)S(1)}, u32[]{:S(2)}, u32[]{:S(2)}) %collective-permute-start.8) | collective-permute-done | bytes 327712 | tf_op jit(solution)/shard_map/ppermute | solution.py:455
  56.2 4.3 %collective-permute-done.15.refs_7_ = bf16[6,16,1024]{2,1,0:T(8,128)(2,1)S(1)} collective-permute-done((bf16[6,16,1024]{2,1,0:T(8,128)(2,1)S(1)}, bf16[6,16,1024]{2,1,0:T(8,128)(2,1)S(1)}, u32[]{:S(2)}, u32[]{:S(2)}) %collective-permute-start.15) | collective-permute-done | bytes 196640 | tf_op jit(solution)/shard_map/ppermute | solution.py:455
  61.6 4.3 %fetch.3 = (bf16[2048,1024]{1,0:T(8,128)(2,1)S(1)}, bf16[2048,1024]{1,0:T(8,128)(2,1)S(1)}, bf16[704,1024]{1,0:T(8,128)(2,1)S(1)}, bf16[704,1024]{1,0:T(8,128)(2,1)S(1)}) custom-call(bf16[2048,1024]{1,0:T(8,128)(2,1)} %refs_0_.3, bf16[2048,1024]{1,0:T(8,128)(2,1)} %refs_1_.1, bf16[704,1024]{1,0:T(8,128)(2,1)} %refs_2_.1, bf16[704,1024]{1,0:T(8,128)(2,1)} %refs_3_.1), custom_call_target="tpu_custom_call" | custom-call | tf_op jit(solution)/shard_map/fetch/pallas_call | solution.py:249
  68.1 7.8 %core_step.1 = (bf16[704,1024]{1,0:T(8,128)(2,1)}, bf16[352,1024]{1,0:T(8,128)(2,1)S(1)}, bf16[352,1024]{1,0:T(8,128)(2,1)S(1)}, bf16[352,1024]{1,0:T(8,128)(2,1)S(1)}) custom-call(s32[3]{0:T(128)S(1)} %pad_add_fusion.2.p_ref, f32[352,1024]{1,0:T(8,128)S(1)} %get-tuple-element.58.ka_ref, f32[352,1024]{1,0:T(8,128)S(1)} %get-tuple-element.59.va_ref, ...), custom_call_target="tpu_custom_call" | custom-call | tf_op jit(solution)/shard_map/core_step/pallas_call | solution.py:403
  79.4 2.6 %collective-permute-start.27 = (bf16[2,16,1024]{2,1,0:T(8,128)(2,1)S(1)}, bf16[2,16,1024]{2,1,0:T(8,128)(2,1)S(1)}, u32[]{:S(2)}, u32[]{:S(2)}) collective-permute-start(bf16[2,16,1024]{2,1,0:T(8,128)(2,1)S(1)} %get-tuple-element.79), channel_id=1, source_target_pairs={{0,24},{8,0},{16,8},{24,16},{32,56},{40,32},{48,40},{56,48},{64,88... | collective-permute-start | bytes 196616 | tf_op jit(solution)/shard_map/ppermute | solution.py:455
  85.0 3.0 %collective-permute-done.28.refs_2_ = bf16[2,16,1024]{2,1,0:T(8,128)(2,1)S(1)} collective-permute-done((bf16[2,16,1024]{2,1,0:T(8,128)(2,1)S(1)}, bf16[2,16,1024]{2,1,0:T(8,128)(2,1)S(1)}, u32[]{:S(2)}, u32[]{:S(2)}) %collective-permute-start.28) | collective-permute-done | bytes 65568 | tf_op jit(solution)/shard_map/ppermute | solution.py:455
  89.5 3.2 %collective-permute-start.31 = (bf16[5,16,1024]{2,1,0:T(8,128)(2,1)S(1)}, bf16[5,16,1024]{2,1,0:T(8,128)(2,1)S(1)}, u32[]{:S(2)}, u32[]{:S(2)}) collective-permute-start(bf16[5,16,1024]{2,1,0:T(8,128)(2,1)S(1)} %get-tuple-element.83), channel_id=1, source_target_pairs={{0,224},{8,232},{16,240},{24,248},{32,0},{40,8},{48,16},{56,24},{6... | collective-permute-start | bytes 491528 | tf_op jit(solution)/shard_map/ppermute | solution.py:455
  103.5 3.2 %collective-permute-start.33 = (bf16[10,16,1024]{2,1,0:T(8,128)(2,1)S(1)}, bf16[10,16,1024]{2,1,0:T(8,128)(2,1)S(1)}, u32[]{:S(2)}, u32[]{:S(2)}) collective-permute-start(bf16[10,16,1024]{2,1,0:T(8,128)(2,1)S(1)} %get-tuple-element.85), channel_id=1, source_target_pairs={{0,224},{8,232},{16,240},{24,248},{32,0},{40,8},{48,16},{56,24},{6... | collective-permute-start | bytes 983048 | tf_op jit(solution)/shard_map/ppermute | solution.py:455
  109.1 2.6 %collective-permute-done.21.refs_1_ = bf16[4,16,1024]{2,1,0:T(8,128)(2,1)S(1)} collective-permute-done((bf16[4,16,1024]{2,1,0:T(8,128)(2,1)S(1)}, bf16[4,16,1024]{2,1,0:T(8,128)(2,1)S(1)}, u32[]{:S(2)}, u32[]{:S(2)}) %collective-permute-start.21) | collective-permute-done | bytes 131104 | tf_op jit(solution)/shard_map/ppermute | solution.py:455
  111.7 2.6 %collective-permute-done.22.refs_2_ = bf16[4,16,1024]{2,1,0:T(8,128)(2,1)S(1)} collective-permute-done((bf16[4,16,1024]{2,1,0:T(8,128)(2,1)S(1)}, bf16[4,16,1024]{2,1,0:T(8,128)(2,1)S(1)}, u32[]{:S(2)}, u32[]{:S(2)}) %collective-permute-start.22) | collective-permute-done | bytes 131104 | tf_op jit(solution)/shard_map/ppermute | solution.py:455
  116.6 3.2 %collective-permute-start.35 = (bf16[10,16,1024]{2,1,0:T(8,128)(2,1)S(1)}, bf16[10,16,1024]{2,1,0:T(8,128)(2,1)S(1)}, u32[]{:S(2)}, u32[]{:S(2)}) collective-permute-start(bf16[10,16,1024]{2,1,0:T(8,128)(2,1)S(1)} %get-tuple-element.87), channel_id=1, source_target_pairs={{0,224},{8,232},{16,240},{24,248},{32,0},{40,8},{48,16},{56,24},{6... | collective-permute-start | bytes 983048 | tf_op jit(solution)/shard_map/ppermute | solution.py:455
  123.1 3.3 %collective-permute-done.18.refs_1_ = bf16[6,16,1024]{2,1,0:T(8,128)(2,1)S(1)} collective-permute-done((bf16[6,16,1024]{2,1,0:T(8,128)(2,1)S(1)}, bf16[6,16,1024]{2,1,0:T(8,128)(2,1)S(1)}, u32[]{:S(2)}, u32[]{:S(2)}) %collective-permute-start.18) | collective-permute-done | bytes 196640 | tf_op jit(solution)/shard_map/ppermute | solution.py:455
  131.9 3.2 %collective-permute-start.37 = (bf16[10,16,1024]{2,1,0:T(8,128)(2,1)S(1)}, bf16[10,16,1024]{2,1,0:T(8,128)(2,1)S(1)}, u32[]{:S(2)}, u32[]{:S(2)}) collective-permute-start(bf16[10,16,1024]{2,1,0:T(8,128)(2,1)S(1)} %get-tuple-element.89), channel_id=1, source_target_pairs={{0,224},{8,232},{16,240},{24,248},{32,0},{40,8},{48,16},{56,24},{6... | collective-permute-start | bytes 983048 | tf_op jit(solution)/shard_map/ppermute | solution.py:455
  135.1 5.0 %collective-permute-done.36.refs_4_ = bf16[10,16,1024]{2,1,0:T(8,128)(2,1)S(1)} collective-permute-done((bf16[10,16,1024]{2,1,0:T(8,128)(2,1)S(1)}, bf16[10,16,1024]{2,1,0:T(8,128)(2,1)S(1)}, u32[]{:S(2)}, u32[]{:S(2)}) %collective-permute-start.36) | collective-permute-done | bytes 327712 | tf_op jit(solution)/shard_map/ppermute | solution.py:455
  (89 shorter events, 53.4 us)
Async XLA Ops:
  0.6 17.1 %collective-permute-start.3 = (bf16[10,16,1024]{2,1,0:T(8,128)(2,1)}, bf16[10,16,1024]{2,1,0:T(8,128)(2,1)S(1)}, u32[]{:S(2)}, u32[]{:S(2)}) collective-permute-start(bf16[10,16,1024]{2,1,0:T(8,128)(2,1)} %refs_0_.2), channel_id=1, source_target_pairs={{0,32},{8,40},{16,48},{24,56},{32,64},{40,72},{48,80},{56,88},{64,... | collective-permute-start | bytes 983048 | tf_op jit(solution)/shard_map/ppermute | solution.py:455
  2.6 15.2 %collective-permute-start.2 = (bf16[10,16,1024]{2,1,0:T(8,128)(2,1)}, bf16[10,16,1024]{2,1,0:T(8,128)(2,1)S(1)}, u32[]{:S(2)}, u32[]{:S(2)}) collective-permute-start(bf16[10,16,1024]{2,1,0:T(8,128)(2,1)} %refs_0_.2), channel_id=1, source_target_pairs={{0,224},{8,232},{16,240},{24,248},{32,0},{40,8},{48,16},{56,24},{6... | collective-permute-start | bytes 983048 | tf_op jit(solution)/shard_map/ppermute | solution.py:455
  17.7 8.5 %collective-permute-start.5 = (bf16[10,16,1024]{2,1,0:T(8,128)(2,1)S(1)}, bf16[10,16,1024]{2,1,0:T(8,128)(2,1)S(1)}, u32[]{:S(2)}, u32[]{:S(2)}) collective-permute-start(bf16[10,16,1024]{2,1,0:T(8,128)(2,1)S(1)} %collective-permute-done.3.refs_2_), channel_id=1, source_target_pairs={{0,32},{8,40},{16,48},{24,56},{32,64},{40,72},{48,80},{56,88},{64,... | collective-permute-start | bytes 983048 | tf_op jit(solution)/shard_map/ppermute | solution.py:455
  17.8 8.4 %collective-permute-start.4 = (bf16[10,16,1024]{2,1,0:T(8,128)(2,1)S(1)}, bf16[10,16,1024]{2,1,0:T(8,128)(2,1)S(1)}, u32[]{:S(2)}, u32[]{:S(2)}) collective-permute-start(bf16[10,16,1024]{2,1,0:T(8,128)(2,1)S(1)} %collective-permute-done.2.refs_1_), channel_id=1, source_target_pairs={{0,224},{8,232},{16,240},{24,248},{32,0},{40,8},{48,16},{56,24},{6... | collective-permute-start | bytes 983048 | tf_op jit(solution)/shard_map/ppermute | solution.py:455
  26.2 8.8 %collective-permute-start.10 = (bf16[10,16,1024]{2,1,0:T(8,128)(2,1)S(1)}, bf16[10,16,1024]{2,1,0:T(8,128)(2,1)S(1)}, u32[]{:S(2)}, u32[]{:S(2)}) collective-permute-start(bf16[10,16,1024]{2,1,0:T(8,128)(2,1)S(1)} %collective-permute-done.5.refs_4_), channel_id=1, source_target_pairs={{0,32},{8,40},{16,48},{24,56},{32,64},{40,72},{48,80},{56,88},{64,... | collective-permute-start | bytes 983048 | tf_op jit(solution)/shard_map/ppermute | solution.py:455
  26.2 8.8 %collective-permute-start.9 = (bf16[10,16,1024]{2,1,0:T(8,128)(2,1)S(1)}, bf16[10,16,1024]{2,1,0:T(8,128)(2,1)S(1)}, u32[]{:S(2)}, u32[]{:S(2)}) collective-permute-start(bf16[10,16,1024]{2,1,0:T(8,128)(2,1)S(1)} %collective-permute-done.4.refs_3_), channel_id=1, source_target_pairs={{0,224},{8,232},{16,240},{24,248},{32,0},{40,8},{48,16},{56,24},{6... | collective-permute-start | bytes 983048 | tf_op jit(solution)/shard_map/ppermute | solution.py:455
  30.3 17.5 %collective-permute-start.6 = (bf16[10,16,1024]{2,1,0:T(8,128)(2,1)S(1)}, bf16[10,16,1024]{2,1,0:T(8,128)(2,1)S(1)}, u32[]{:S(2)}, u32[]{:S(2)}) collective-permute-start(bf16[10,16,1024]{2,1,0:T(8,128)(2,1)S(1)} %get-tuple-element.47), channel_id=1, source_target_pairs={{0,8},{8,16},{16,24},{24,0},{32,40},{40,48},{48,56},{56,32},{64,72... | collective-permute-start | bytes 983048 | tf_op jit(solution)/shard_map/ppermute | solution.py:455
  35.1 7.4 %collective-permute-start.11 = (bf16[5,16,1024]{2,1,0:T(8,128)(2,1)S(1)}, bf16[5,16,1024]{2,1,0:T(8,128)(2,1)S(1)}, u32[]{:S(2)}, u32[]{:S(2)}) collective-permute-start(bf16[5,16,1024]{2,1,0:T(8,128)(2,1)S(1)} %slice.20), channel_id=1, source_target_pairs={{0,32},{8,40},{16,48},{24,56},{32,64},{40,72},{48,80},{56,88},{64,... | collective-permute-start | bytes 491528 | tf_op jit(solution)/shard_map/ppermute | solution.py:455
  35.2 7.3 %collective-permute-start.12 = (bf16[5,16,1024]{2,1,0:T(8,128)(2,1)S(1)}, bf16[5,16,1024]{2,1,0:T(8,128)(2,1)S(1)}, u32[]{:S(2)}, u32[]{:S(2)}) collective-permute-start(bf16[5,16,1024]{2,1,0:T(8,128)(2,1)S(1)} %slice.19), channel_id=1, source_target_pairs={{0,224},{8,232},{16,240},{24,248},{32,0},{40,8},{48,16},{56,24},{6... | collective-permute-start | bytes 491528 | tf_op jit(solution)/shard_map/ppermute | solution.py:455
  38.7 12.3 %collective-permute-start.7 = (bf16[10,16,1024]{2,1,0:T(8,128)(2,1)S(1)}, bf16[10,16,1024]{2,1,0:T(8,128)(2,1)S(1)}, u32[]{:S(2)}, u32[]{:S(2)}) collective-permute-start(bf16[10,16,1024]{2,1,0:T(8,128)(2,1)S(1)} %get-tuple-element.48), channel_id=1, source_target_pairs={{0,16},{8,24},{16,0},{24,8},{32,48},{40,56},{48,32},{56,40},{64,80... | collective-permute-start | bytes 983048 | tf_op jit(solution)/shard_map/ppermute | solution.py:455
  41.2 15.0 %collective-permute-start.8 = (bf16[10,16,1024]{2,1,0:T(8,128)(2,1)S(1)}, bf16[10,16,1024]{2,1,0:T(8,128)(2,1)S(1)}, u32[]{:S(2)}, u32[]{:S(2)}) collective-permute-start(bf16[10,16,1024]{2,1,0:T(8,128)(2,1)S(1)} %get-tuple-element.49), channel_id=1, source_target_pairs={{0,24},{8,0},{16,8},{24,16},{32,56},{40,32},{48,40},{56,48},{64,88... | collective-permute-start | bytes 983048 | tf_op jit(solution)/shard_map/ppermute | solution.py:455
  43.3 12.9 %collective-permute-start.13 = (bf16[6,16,1024]{2,1,0:T(8,128)(2,1)S(1)}, bf16[6,16,1024]{2,1,0:T(8,128)(2,1)S(1)}, u32[]{:S(2)}, u32[]{:S(2)}) collective-permute-start(bf16[6,16,1024]{2,1,0:T(8,128)(2,1)S(1)} %get-tuple-element.53), channel_id=1, source_target_pairs={{0,8},{8,16},{16,24},{24,0},{32,40},{40,48},{48,56},{56,32},{64,72... | collective-permute-start | bytes 589832 | tf_op jit(solution)/shard_map/ppermute | solution.py:455
  44.3 11.9 %collective-permute-start.14 = (bf16[6,16,1024]{2,1,0:T(8,128)(2,1)S(1)}, bf16[6,16,1024]{2,1,0:T(8,128)(2,1)S(1)}, u32[]{:S(2)}, u32[]{:S(2)}) collective-permute-start(bf16[6,16,1024]{2,1,0:T(8,128)(2,1)S(1)} %get-tuple-element.54), channel_id=1, source_target_pairs={{0,16},{8,24},{16,0},{24,8},{32,48},{40,56},{48,32},{56,40},{64,80... | collective-permute-start | bytes 589832 | tf_op jit(solution)/shard_map/ppermute | solution.py:455
  47.8 12.7 %collective-permute-start.15 = (bf16[6,16,1024]{2,1,0:T(8,128)(2,1)S(1)}, bf16[6,16,1024]{2,1,0:T(8,128)(2,1)S(1)}, u32[]{:S(2)}, u32[]{:S(2)}) collective-permute-start(bf16[6,16,1024]{2,1,0:T(8,128)(2,1)S(1)} %get-tuple-element.55), channel_id=1, source_target_pairs={{0,24},{8,0},{16,8},{24,16},{32,56},{40,32},{48,40},{56,48},{64,88... | collective-permute-start | bytes 589832 | tf_op jit(solution)/shard_map/ppermute | solution.py:455
  89.4 13.0 %collective-permute-start.30 = (bf16[5,16,1024]{2,1,0:T(8,128)(2,1)S(1)}, bf16[5,16,1024]{2,1,0:T(8,128)(2,1)S(1)}, u32[]{:S(2)}, u32[]{:S(2)}) collective-permute-start(bf16[5,16,1024]{2,1,0:T(8,128)(2,1)S(1)} %get-tuple-element.82), channel_id=1, source_target_pairs={{0,32},{8,40},{16,48},{24,56},{32,64},{40,72},{48,80},{56,88},{64,... | collective-permute-start | bytes 491528 | tf_op jit(solution)/shard_map/ppermute | solution.py:455
  89.5 12.9 %collective-permute-start.31 = (bf16[5,16,1024]{2,1,0:T(8,128)(2,1)S(1)}, bf16[5,16,1024]{2,1,0:T(8,128)(2,1)S(1)}, u32[]{:S(2)}, u32[]{:S(2)}) collective-permute-start(bf16[5,16,1024]{2,1,0:T(8,128)(2,1)S(1)} %get-tuple-element.83), channel_id=1, source_target_pairs={{0,224},{8,232},{16,240},{24,248},{32,0},{40,8},{48,16},{56,24},{6... | collective-permute-start | bytes 491528 | tf_op jit(solution)/shard_map/ppermute | solution.py:455
  103.4 12.2 %collective-permute-start.32 = (bf16[10,16,1024]{2,1,0:T(8,128)(2,1)S(1)}, bf16[10,16,1024]{2,1,0:T(8,128)(2,1)S(1)}, u32[]{:S(2)}, u32[]{:S(2)}) collective-permute-start(bf16[10,16,1024]{2,1,0:T(8,128)(2,1)S(1)} %get-tuple-element.84), channel_id=1, source_target_pairs={{0,32},{8,40},{16,48},{24,56},{32,64},{40,72},{48,80},{56,88},{64,... | collective-permute-start | bytes 983048 | tf_op jit(solution)/shard_map/ppermute | solution.py:455
  103.5 12.1 %collective-permute-start.33 = (bf16[10,16,1024]{2,1,0:T(8,128)(2,1)S(1)}, bf16[10,16,1024]{2,1,0:T(8,128)(2,1)S(1)}, u32[]{:S(2)}, u32[]{:S(2)}) collective-permute-start(bf16[10,16,1024]{2,1,0:T(8,128)(2,1)S(1)} %get-tuple-element.85), channel_id=1, source_target_pairs={{0,224},{8,232},{16,240},{24,248},{32,0},{40,8},{48,16},{56,24},{6... | collective-permute-start | bytes 983048 | tf_op jit(solution)/shard_map/ppermute | solution.py:455
  116.5 14.3 %collective-permute-start.34 = (bf16[10,16,1024]{2,1,0:T(8,128)(2,1)S(1)}, bf16[10,16,1024]{2,1,0:T(8,128)(2,1)S(1)}, u32[]{:S(2)}, u32[]{:S(2)}) collective-permute-start(bf16[10,16,1024]{2,1,0:T(8,128)(2,1)S(1)} %get-tuple-element.86), channel_id=1, source_target_pairs={{0,32},{8,40},{16,48},{24,56},{32,64},{40,72},{48,80},{56,88},{64,... | collective-permute-start | bytes 983048 | tf_op jit(solution)/shard_map/ppermute | solution.py:455
  116.6 14.2 %collective-permute-start.35 = (bf16[10,16,1024]{2,1,0:T(8,128)(2,1)S(1)}, bf16[10,16,1024]{2,1,0:T(8,128)(2,1)S(1)}, u32[]{:S(2)}, u32[]{:S(2)}) collective-permute-start(bf16[10,16,1024]{2,1,0:T(8,128)(2,1)S(1)} %get-tuple-element.87), channel_id=1, source_target_pairs={{0,224},{8,232},{16,240},{24,248},{32,0},{40,8},{48,16},{56,24},{6... | collective-permute-start | bytes 983048 | tf_op jit(solution)/shard_map/ppermute | solution.py:455
  121.6 7.3 %collective-permute-start.19 = (bf16[6,16,1024]{2,1,0:T(8,128)(2,1)S(1)}, bf16[6,16,1024]{2,1,0:T(8,128)(2,1)S(1)}, u32[]{:S(2)}, u32[]{:S(2)}) collective-permute-start(bf16[6,16,1024]{2,1,0:T(8,128)(2,1)S(1)} %get-tuple-element.68), channel_id=1, source_target_pairs={{0,16},{8,24},{16,0},{24,8},{32,48},{40,56},{48,32},{56,40},{64,80... | collective-permute-start | bytes 589832 | tf_op jit(solution)/shard_map/ppermute | solution.py:455
  122.5 8.4 %collective-permute-start.20 = (bf16[6,16,1024]{2,1,0:T(8,128)(2,1)S(1)}, bf16[6,16,1024]{2,1,0:T(8,128)(2,1)S(1)}, u32[]{:S(2)}, u32[]{:S(2)}) collective-permute-start(bf16[6,16,1024]{2,1,0:T(8,128)(2,1)S(1)} %get-tuple-element.69), channel_id=1, source_target_pairs={{0,8},{8,16},{16,24},{24,0},{32,40},{40,48},{48,56},{56,32},{64,72... | collective-permute-start | bytes 589832 | tf_op jit(solution)/shard_map/ppermute | solution.py:455
  131.8 8.4 %collective-permute-start.36 = (bf16[10,16,1024]{2,1,0:T(8,128)(2,1)S(1)}, bf16[10,16,1024]{2,1,0:T(8,128)(2,1)S(1)}, u32[]{:S(2)}, u32[]{:S(2)}) collective-permute-start(bf16[10,16,1024]{2,1,0:T(8,128)(2,1)S(1)} %get-tuple-element.88), channel_id=1, source_target_pairs={{0,32},{8,40},{16,48},{24,56},{32,64},{40,72},{48,80},{56,88},{64,... | collective-permute-start | bytes 983048 | tf_op jit(solution)/shard_map/ppermute | solution.py:455
  131.9 8.3 %collective-permute-start.37 = (bf16[10,16,1024]{2,1,0:T(8,128)(2,1)S(1)}, bf16[10,16,1024]{2,1,0:T(8,128)(2,1)S(1)}, u32[]{:S(2)}, u32[]{:S(2)}) collective-permute-start(bf16[10,16,1024]{2,1,0:T(8,128)(2,1)S(1)} %get-tuple-element.89), channel_id=1, source_target_pairs={{0,224},{8,232},{16,240},{24,248},{32,0},{40,8},{48,16},{56,24},{6... | collective-permute-start | bytes 983048 | tf_op jit(solution)/shard_map/ppermute | solution.py:455
  (14 other events, 79.8 us)

commit v7 on v6

--- a/solution.py
+++ b/solution.py
@@ -109,7 +109,7 @@
                     out[jnp.where(at[j] < 0, ref_count, at[j])] = ins[n * NY + j][k]
                 return carry
 
-            lax.fori_loop(0, count * CAP, place_slots, 0)
+            lax.fori_loop(0, count * CAP, place_slots, 0, unroll=2)
 
     return pl.pallas_call(
         body,
@@ -136,7 +136,7 @@
                     outs[n * NY + j][k] = total.astype(BF)
                 return carry
 
-            lax.fori_loop(0, count * CAP, place_slots, 0)
+            lax.fori_loop(0, count * CAP, place_slots, 0, unroll=2)
 
     flat = pl.pallas_call(
         body,
@@ -166,8 +166,8 @@
     def body(t_ref, p_ref, *refs):
         ins = refs[:NY]
         prev = refs[NY : NY + len(before)]
-        outs = refs[NY + len(before) : -1]
-        acc = refs[-1]
+        outs = refs[NY + len(before) : NY + len(before) + len(shapes)]
+        acc = refs[NY + len(before) + len(shapes)]
 
         def fill(r, carry):
             for p in range(len(planes)):
@@ -219,15 +219,33 @@
         if far:
             lax.fori_loop(0, cut, drain_low, 0)
             lax.fori_loop(0, rows_here - cut, drain_high, 0)
+        elif step == 0:
+            done, sem = refs[-2:]
+            stores = []
+            for n, (start, stop) in enumerate(((0, cut), (cut, rows_here))):
+
+                def finish(r, carry):
+                    done[r] = acc[0, r].astype(BF)
+                    return carry
+
+                lax.fori_loop(start, stop, finish, 0)
+                rows = slice(start, stop)
+                stores.append(
+                    pltpu.make_async_copy(done.at[rows], outs[0].at[rows], sem.at[n])
+                )
+                stores[-1].start()
+            for store in stores:
+                store.wait()
         else:
             lax.fori_loop(0, rows_here, drain, 0, unroll=2)
 
     return pl.pallas_call(
         body,
         in_specs=[SMEM, SMEM] + [VMEM] * (NY + len(before)),
-        out_specs=[VMEM] * len(shapes),
+        out_specs=[ANY if step == 0 else VMEM] * len(shapes),
         out_shape=[jax.ShapeDtypeStruct(s, BF) for s in shapes],
-        scratch_shapes=[pltpu.VMEM((len(planes), rows_here) + tail, F32)],
+        scratch_shapes=[pltpu.VMEM((len(planes), rows_here) + tail, F32)]
+        + ([pltpu.VMEM(shapes[0], BF), pltpu.SemaphoreType.DMA((2,))] if step == 0 else []),
         compiler_params=SMALL,
         name="gather",
     )(table, place, *parts, *before)
@@ -381,7 +399,7 @@
             grads(u, *carry)
             return after
 
-        grads(spans - 1, *lax.fori_loop(0, spans - 1, both, weigh(0)))
+        grads(spans - 1, *lax.fori_loop(0, spans - 1, both, weigh(0), unroll=2))
         store = pltpu.make_async_copy(dq_ref, dq_hbm, sem.at[0])
         store.start()
 

time: 142 us -> 141 us (level)
  no operation moved by 1% of the time
where the time goes in v7:
time: 141 us
  starting transfers between devices  57.6 us (41%)
  waiting for transfers between devices  53.4 us (38%)
  Pallas kernels  26.7 us (19%)
    ppermute x36, starting transfers between devices, move(): return lax.ppermute(x, 'seq', ring(seq, dz, dy))  56.9 us
    ppermute x36, waiting for transfers between devices, move(): return lax.ppermute(x, 'seq', ring(seq, dz, dy))  53.4 us
    pallas_call x1, Pallas kernels, core_step(): pl.pallas_call(body, in_specs=[SMEM] + [VMEM] * 7, out_specs=[ANY] + [VME...  7.13 us
    pallas_call x2, Pallas kernels, fetch(): pl.pallas_call(body, in_specs=[pl.BlockSpec(memory_space=pltpu.HBM)] * co...  5.26 us
    pallas_call x5, Pallas kernels, gather_grads(): pl.pallas_call(body, in_specs=[SMEM, SMEM] + [VMEM] * (NY + len(before)),...  5.16 us
  transfers between devices with their start and end apart: 38, of which 20 were waited for; matrix products, arithmetic and copies ran while one was open for 1% of the time, Pallas kernels for 9%

profile of v7, /device:TPU:2, one launch (start us, length us, event | category | flops | bytes accessed | tf_op | source)
XLA Modules:
  0.0 140.9 jit_solution(11183839409126792150)
XLA Ops:
  2.6 4.0 %collective-permute-start.2 = (bf16[10,16,1024]{2,1,0:T(8,128)(2,1)}, bf16[10,16,1024]{2,1,0:T(8,128)(2,1)S(1)}, u32[]{:S(2)}, u32[]{:S(2)}) collective-permute-start(bf16[10,16,1024]{2,1,0:T(8,128)(2,1)} %refs_0_.2), channel_id=1, source_target_pairs={{0,224},{8,232},{16,240},{24,248},{32,0},{40,8},{48,16},{56,24},{6... | collective-permute-start | bytes 983048 | tf_op jit(solution)/shard_map/ppermute | solution.py:473
  7.5 3.1 %collective-permute-start = (s32[1,22]{1,0:T(1,128)S(1)}, s32[1,22]{1,0:T(1,128)S(1)}, u32[]{:S(2)}, u32[]{:S(2)}) collective-permute-start(s32[1,22]{1,0:T(1,128)S(1)} %reshape.357), channel_id=1, source_target_pairs={{0,24},{8,0},{16,8},{24,16},{32,56},{40,32},{48,40},{56,48},{64,88... | collective-permute-start | bytes 272 | tf_op jit(solution)/shard_map/ppermute | solution.py:473
  11.9 2.5 %collective-permute-start.1 = (s32[2,22]{1,0:T(2,128)S(1)}, s32[2,22]{1,0:T(2,128)S(1)}, u32[]{:S(2)}, u32[]{:S(2)}) collective-permute-start(s32[2,22]{1,0:T(2,128)S(1)} %pad_add_fusion.1), channel_id=1, source_target_pairs={{0,16},{8,24},{16,0},{24,8},{32,48},{40,56},{48,32},{56,40},{64,80... | collective-permute-start | bytes 536 | tf_op jit(solution)/shard_map/ppermute | solution.py:473
  17.8 3.2 %collective-permute-start.4 = (bf16[10,16,1024]{2,1,0:T(8,128)(2,1)S(1)}, bf16[10,16,1024]{2,1,0:T(8,128)(2,1)S(1)}, u32[]{:S(2)}, u32[]{:S(2)}) collective-permute-start(bf16[10,16,1024]{2,1,0:T(8,128)(2,1)S(1)} %collective-permute-done.2.refs_1_), channel_id=1, source_target_pairs={{0,224},{8,232},{16,240},{24,248},{32,0},{40,8},{48,16},{56,24},{6... | collective-permute-start | bytes 983048 | tf_op jit(solution)/shard_map/ppermute | solution.py:473
  21.1 5.1 %collective-permute-done.5.refs_4_ = bf16[10,16,1024]{2,1,0:T(8,128)(2,1)S(1)} collective-permute-done((bf16[10,16,1024]{2,1,0:T(8,128)(2,1)S(1)}, bf16[10,16,1024]{2,1,0:T(8,128)(2,1)S(1)}, u32[]{:S(2)}, u32[]{:S(2)}) %collective-permute-start.5) | collective-permute-done | bytes 327712 | tf_op jit(solution)/shard_map/ppermute | solution.py:473
  26.2 3.2 %collective-permute-start.9 = (bf16[10,16,1024]{2,1,0:T(8,128)(2,1)S(1)}, bf16[10,16,1024]{2,1,0:T(8,128)(2,1)S(1)}, u32[]{:S(2)}, u32[]{:S(2)}) collective-permute-start(bf16[10,16,1024]{2,1,0:T(8,128)(2,1)S(1)} %collective-permute-done.4.refs_3_), channel_id=1, source_target_pairs={{0,224},{8,232},{16,240},{24,248},{32,0},{40,8},{48,16},{56,24},{6... | collective-permute-start | bytes 983048 | tf_op jit(solution)/shard_map/ppermute | solution.py:473
  31.9 3.1 %collective-permute-done.10.refs_1_ = bf16[10,16,1024]{2,1,0:T(8,128)(2,1)S(1)} collective-permute-done((bf16[10,16,1024]{2,1,0:T(8,128)(2,1)S(1)}, bf16[10,16,1024]{2,1,0:T(8,128)(2,1)S(1)}, u32[]{:S(2)}, u32[]{:S(2)}) %collective-permute-start.10) | collective-permute-done | bytes 327712 | tf_op jit(solution)/shard_map/ppermute | solution.py:473
  35.2 3.5 %collective-permute-start.12 = (bf16[5,16,1024]{2,1,0:T(8,128)(2,1)S(1)}, bf16[5,16,1024]{2,1,0:T(8,128)(2,1)S(1)}, u32[]{:S(2)}, u32[]{:S(2)}) collective-permute-start(bf16[5,16,1024]{2,1,0:T(8,128)(2,1)S(1)} %slice.19), channel_id=1, source_target_pairs={{0,224},{8,232},{16,240},{24,248},{32,0},{40,8},{48,16},{56,24},{6... | collective-permute-start | bytes 491528 | tf_op jit(solution)/shard_map/ppermute | solution.py:473
  38.7 2.5 %collective-permute-start.7 = (bf16[10,16,1024]{2,1,0:T(8,128)(2,1)S(1)}, bf16[10,16,1024]{2,1,0:T(8,128)(2,1)S(1)}, u32[]{:S(2)}, u32[]{:S(2)}) collective-permute-start(bf16[10,16,1024]{2,1,0:T(8,128)(2,1)S(1)} %get-tuple-element.48), channel_id=1, source_target_pairs={{0,16},{8,24},{16,0},{24,8},{32,48},{40,56},{48,32},{56,40},{64,80... | collective-permute-start | bytes 983048 | tf_op jit(solution)/shard_map/ppermute | solution.py:473
  44.3 3.5 %collective-permute-start.14 = (bf16[6,16,1024]{2,1,0:T(8,128)(2,1)S(1)}, bf16[6,16,1024]{2,1,0:T(8,128)(2,1)S(1)}, u32[]{:S(2)}, u32[]{:S(2)}) collective-permute-start(bf16[6,16,1024]{2,1,0:T(8,128)(2,1)S(1)} %get-tuple-element.54), channel_id=1, source_target_pairs={{0,16},{8,24},{16,0},{24,8},{32,48},{40,56},{48,32},{56,40},{64,80... | collective-permute-start | bytes 589832 | tf_op jit(solution)/shard_map/ppermute | solution.py:473
  51.0 5.2 %collective-permute-done.8.refs_3_ = bf16[10,16,1024]{2,1,0:T(8,128)(2,1)S(1)} collective-permute-done((bf16[10,16,1024]{2,1,0:T(8,128)(2,1)S(1)}, bf16[10,16,1024]{2,1,0:T(8,128)(2,1)S(1)}, u32[]{:S(2)}, u32[]{:S(2)}) %collective-permute-start.8) | collective-permute-done | bytes 327712 | tf_op jit(solution)/shard_map/ppermute | solution.py:473
  56.2 4.3 %collective-permute-done.15.refs_7_ = bf16[6,16,1024]{2,1,0:T(8,128)(2,1)S(1)} collective-permute-done((bf16[6,16,1024]{2,1,0:T(8,128)(2,1)S(1)}, bf16[6,16,1024]{2,1,0:T(8,128)(2,1)S(1)}, u32[]{:S(2)}, u32[]{:S(2)}) %collective-permute-start.15) | collective-permute-done | bytes 196640 | tf_op jit(solution)/shard_map/ppermute | solution.py:473
  61.5 4.3 %fetch.3 = (bf16[2048,1024]{1,0:T(8,128)(2,1)S(1)}, bf16[2048,1024]{1,0:T(8,128)(2,1)S(1)}, bf16[704,1024]{1,0:T(8,128)(2,1)S(1)}, bf16[704,1024]{1,0:T(8,128)(2,1)S(1)}) custom-call(bf16[2048,1024]{1,0:T(8,128)(2,1)} %refs_0_.3, bf16[2048,1024]{1,0:T(8,128)(2,1)} %refs_1_.1, bf16[704,1024]{1,0:T(8,128)(2,1)} %refs_2_.1, bf16[704,1024]{1,0:T(8,128)(2,1)} %refs_3_.1), custom_call_target="tpu_custom_call" | custom-call | tf_op jit(solution)/shard_map/fetch/pallas_call | solution.py:267
  68.0 7.1 %core_step.1 = (bf16[704,1024]{1,0:T(8,128)(2,1)}, bf16[352,1024]{1,0:T(8,128)(2,1)S(1)}, bf16[352,1024]{1,0:T(8,128)(2,1)S(1)}, bf16[352,1024]{1,0:T(8,128)(2,1)S(1)}) custom-call(s32[3]{0:T(128)S(1)} %pad_add_fusion.2.p_ref, f32[352,1024]{1,0:T(8,128)S(1)} %get-tuple-element.58.ka_ref, f32[352,1024]{1,0:T(8,128)S(1)} %get-tuple-element.59.va_ref, ...), custom_call_target="tpu_custom_call" | custom-call | tf_op jit(solution)/shard_map/core_step/pallas_call | solution.py:421
  78.6 2.6 %collective-permute-start.27 = (bf16[2,16,1024]{2,1,0:T(8,128)(2,1)S(1)}, bf16[2,16,1024]{2,1,0:T(8,128)(2,1)S(1)}, u32[]{:S(2)}, u32[]{:S(2)}) collective-permute-start(bf16[2,16,1024]{2,1,0:T(8,128)(2,1)S(1)} %get-tuple-element.79), channel_id=1, source_target_pairs={{0,24},{8,0},{16,8},{24,16},{32,56},{40,32},{48,40},{56,48},{64,88... | collective-permute-start | bytes 196616 | tf_op jit(solution)/shard_map/ppermute | solution.py:473
  84.2 3.0 %collective-permute-done.28.refs_2_ = bf16[2,16,1024]{2,1,0:T(8,128)(2,1)S(1)} collective-permute-done((bf16[2,16,1024]{2,1,0:T(8,128)(2,1)S(1)}, bf16[2,16,1024]{2,1,0:T(8,128)(2,1)S(1)}, u32[]{:S(2)}, u32[]{:S(2)}) %collective-permute-start.28) | collective-permute-done | bytes 65568 | tf_op jit(solution)/shard_map/ppermute | solution.py:473
  88.7 3.2 %collective-permute-start.31 = (bf16[5,16,1024]{2,1,0:T(8,128)(2,1)S(1)}, bf16[5,16,1024]{2,1,0:T(8,128)(2,1)S(1)}, u32[]{:S(2)}, u32[]{:S(2)}) collective-permute-start(bf16[5,16,1024]{2,1,0:T(8,128)(2,1)S(1)} %get-tuple-element.83), channel_id=1, source_target_pairs={{0,224},{8,232},{16,240},{24,248},{32,0},{40,8},{48,16},{56,24},{6... | collective-permute-start | bytes 491528 | tf_op jit(solution)/shard_map/ppermute | solution.py:473
  102.6 3.2 %collective-permute-start.33 = (bf16[10,16,1024]{2,1,0:T(8,128)(2,1)S(1)}, bf16[10,16,1024]{2,1,0:T(8,128)(2,1)S(1)}, u32[]{:S(2)}, u32[]{:S(2)}) collective-permute-start(bf16[10,16,1024]{2,1,0:T(8,128)(2,1)S(1)} %get-tuple-element.85), channel_id=1, source_target_pairs={{0,224},{8,232},{16,240},{24,248},{32,0},{40,8},{48,16},{56,24},{6... | collective-permute-start | bytes 983048 | tf_op jit(solution)/shard_map/ppermute | solution.py:473
  108.3 2.5 %collective-permute-done.21.refs_1_ = bf16[4,16,1024]{2,1,0:T(8,128)(2,1)S(1)} collective-permute-done((bf16[4,16,1024]{2,1,0:T(8,128)(2,1)S(1)}, bf16[4,16,1024]{2,1,0:T(8,128)(2,1)S(1)}, u32[]{:S(2)}, u32[]{:S(2)}) %collective-permute-start.21) | collective-permute-done | bytes 131104 | tf_op jit(solution)/shard_map/ppermute | solution.py:473
  110.8 2.6 %collective-permute-done.22.refs_2_ = bf16[4,16,1024]{2,1,0:T(8,128)(2,1)S(1)} collective-permute-done((bf16[4,16,1024]{2,1,0:T(8,128)(2,1)S(1)}, bf16[4,16,1024]{2,1,0:T(8,128)(2,1)S(1)}, u32[]{:S(2)}, u32[]{:S(2)}) %collective-permute-start.22) | collective-permute-done | bytes 131104 | tf_op jit(solution)/shard_map/ppermute | solution.py:473
  115.8 3.2 %collective-permute-start.35 = (bf16[10,16,1024]{2,1,0:T(8,128)(2,1)S(1)}, bf16[10,16,1024]{2,1,0:T(8,128)(2,1)S(1)}, u32[]{:S(2)}, u32[]{:S(2)}) collective-permute-start(bf16[10,16,1024]{2,1,0:T(8,128)(2,1)S(1)} %get-tuple-element.87), channel_id=1, source_target_pairs={{0,224},{8,232},{16,240},{24,248},{32,0},{40,8},{48,16},{56,24},{6... | collective-permute-start | bytes 983048 | tf_op jit(solution)/shard_map/ppermute | solution.py:473
  122.2 3.3 %collective-permute-done.18.refs_1_ = bf16[6,16,1024]{2,1,0:T(8,128)(2,1)S(1)} collective-permute-done((bf16[6,16,1024]{2,1,0:T(8,128)(2,1)S(1)}, bf16[6,16,1024]{2,1,0:T(8,128)(2,1)S(1)}, u32[]{:S(2)}, u32[]{:S(2)}) %collective-permute-start.18) | collective-permute-done | bytes 196640 | tf_op jit(solution)/shard_map/ppermute | solution.py:473
  130.9 3.2 %collective-permute-start.37 = (bf16[10,16,1024]{2,1,0:T(8,128)(2,1)S(1)}, bf16[10,16,1024]{2,1,0:T(8,128)(2,1)S(1)}, u32[]{:S(2)}, u32[]{:S(2)}) collective-permute-start(bf16[10,16,1024]{2,1,0:T(8,128)(2,1)S(1)} %get-tuple-element.89), channel_id=1, source_target_pairs={{0,224},{8,232},{16,240},{24,248},{32,0},{40,8},{48,16},{56,24},{6... | collective-permute-start | bytes 983048 | tf_op jit(solution)/shard_map/ppermute | solution.py:473
  134.2 5.0 %collective-permute-done.36.refs_4_ = bf16[10,16,1024]{2,1,0:T(8,128)(2,1)S(1)} collective-permute-done((bf16[10,16,1024]{2,1,0:T(8,128)(2,1)S(1)}, bf16[10,16,1024]{2,1,0:T(8,128)(2,1)S(1)}, u32[]{:S(2)}, u32[]{:S(2)}) %collective-permute-start.36) | collective-permute-done | bytes 327712 | tf_op jit(solution)/shard_map/ppermute | solution.py:473
  (89 shorter events, 53.0 us)
Async XLA Ops:
  0.6 17.1 %collective-permute-start.3 = (bf16[10,16,1024]{2,1,0:T(8,128)(2,1)}, bf16[10,16,1024]{2,1,0:T(8,128)(2,1)S(1)}, u32[]{:S(2)}, u32[]{:S(2)}) collective-permute-start(bf16[10,16,1024]{2,1,0:T(8,128)(2,1)} %refs_0_.2), channel_id=1, source_target_pairs={{0,32},{8,40},{16,48},{24,56},{32,64},{40,72},{48,80},{56,88},{64,... | collective-permute-start | bytes 983048 | tf_op jit(solution)/shard_map/ppermute | solution.py:473
  2.6 15.2 %collective-permute-start.2 = (bf16[10,16,1024]{2,1,0:T(8,128)(2,1)}, bf16[10,16,1024]{2,1,0:T(8,128)(2,1)S(1)}, u32[]{:S(2)}, u32[]{:S(2)}) collective-permute-start(bf16[10,16,1024]{2,1,0:T(8,128)(2,1)} %refs_0_.2), channel_id=1, source_target_pairs={{0,224},{8,232},{16,240},{24,248},{32,0},{40,8},{48,16},{56,24},{6... | collective-permute-start | bytes 983048 | tf_op jit(solution)/shard_map/ppermute | solution.py:473
  17.7 8.5 %collective-permute-start.5 = (bf16[10,16,1024]{2,1,0:T(8,128)(2,1)S(1)}, bf16[10,16,1024]{2,1,0:T(8,128)(2,1)S(1)}, u32[]{:S(2)}, u32[]{:S(2)}) collective-permute-start(bf16[10,16,1024]{2,1,0:T(8,128)(2,1)S(1)} %collective-permute-done.3.refs_2_), channel_id=1, source_target_pairs={{0,32},{8,40},{16,48},{24,56},{32,64},{40,72},{48,80},{56,88},{64,... | collective-permute-start | bytes 983048 | tf_op jit(solution)/shard_map/ppermute | solution.py:473
  17.8 8.4 %collective-permute-start.4 = (bf16[10,16,1024]{2,1,0:T(8,128)(2,1)S(1)}, bf16[10,16,1024]{2,1,0:T(8,128)(2,1)S(1)}, u32[]{:S(2)}, u32[]{:S(2)}) collective-permute-start(bf16[10,16,1024]{2,1,0:T(8,128)(2,1)S(1)} %collective-permute-done.2.refs_1_), channel_id=1, source_target_pairs={{0,224},{8,232},{16,240},{24,248},{32,0},{40,8},{48,16},{56,24},{6... | collective-permute-start | bytes 983048 | tf_op jit(solution)/shard_map/ppermute | solution.py:473
  26.2 8.8 %collective-permute-start.10 = (bf16[10,16,1024]{2,1,0:T(8,128)(2,1)S(1)}, bf16[10,16,1024]{2,1,0:T(8,128)(2,1)S(1)}, u32[]{:S(2)}, u32[]{:S(2)}) collective-permute-start(bf16[10,16,1024]{2,1,0:T(8,128)(2,1)S(1)} %collective-permute-done.5.refs_4_), channel_id=1, source_target_pairs={{0,32},{8,40},{16,48},{24,56},{32,64},{40,72},{48,80},{56,88},{64,... | collective-permute-start | bytes 983048 | tf_op jit(solution)/shard_map/ppermute | solution.py:473
  26.2 8.8 %collective-permute-start.9 = (bf16[10,16,1024]{2,1,0:T(8,128)(2,1)S(1)}, bf16[10,16,1024]{2,1,0:T(8,128)(2,1)S(1)}, u32[]{:S(2)}, u32[]{:S(2)}) collective-permute-start(bf16[10,16,1024]{2,1,0:T(8,128)(2,1)S(1)} %collective-permute-done.4.refs_3_), channel_id=1, source_target_pairs={{0,224},{8,232},{16,240},{24,248},{32,0},{40,8},{48,16},{56,24},{6... | collective-permute-start | bytes 983048 | tf_op jit(solution)/shard_map/ppermute | solution.py:473
  30.3 17.5 %collective-permute-start.6 = (bf16[10,16,1024]{2,1,0:T(8,128)(2,1)S(1)}, bf16[10,16,1024]{2,1,0:T(8,128)(2,1)S(1)}, u32[]{:S(2)}, u32[]{:S(2)}) collective-permute-start(bf16[10,16,1024]{2,1,0:T(8,128)(2,1)S(1)} %get-tuple-element.47), channel_id=1, source_target_pairs={{0,8},{8,16},{16,24},{24,0},{32,40},{40,48},{48,56},{56,32},{64,72... | collective-permute-start | bytes 983048 | tf_op jit(solution)/shard_map/ppermute | solution.py:473
  35.1 7.4 %collective-permute-start.11 = (bf16[5,16,1024]{2,1,0:T(8,128)(2,1)S(1)}, bf16[5,16,1024]{2,1,0:T(8,128)(2,1)S(1)}, u32[]{:S(2)}, u32[]{:S(2)}) collective-permute-start(bf16[5,16,1024]{2,1,0:T(8,128)(2,1)S(1)} %slice.20), channel_id=1, source_target_pairs={{0,32},{8,40},{16,48},{24,56},{32,64},{40,72},{48,80},{56,88},{64,... | collective-permute-start | bytes 491528 | tf_op jit(solution)/shard_map/ppermute | solution.py:473
  35.2 7.3 %collective-permute-start.12 = (bf16[5,16,1024]{2,1,0:T(8,128)(2,1)S(1)}, bf16[5,16,1024]{2,1,0:T(8,128)(2,1)S(1)}, u32[]{:S(2)}, u32[]{:S(2)}) collective-permute-start(bf16[5,16,1024]{2,1,0:T(8,128)(2,1)S(1)} %slice.19), channel_id=1, source_target_pairs={{0,224},{8,232},{16,240},{24,248},{32,0},{40,8},{48,16},{56,24},{6... | collective-permute-start | bytes 491528 | tf_op jit(solution)/shard_map/ppermute | solution.py:473
  38.7 12.3 %collective-permute-start.7 = (bf16[10,16,1024]{2,1,0:T(8,128)(2,1)S(1)}, bf16[10,16,1024]{2,1,0:T(8,128)(2,1)S(1)}, u32[]{:S(2)}, u32[]{:S(2)}) collective-permute-start(bf16[10,16,1024]{2,1,0:T(8,128)(2,1)S(1)} %get-tuple-element.48), channel_id=1, source_target_pairs={{0,16},{8,24},{16,0},{24,8},{32,48},{40,56},{48,32},{56,40},{64,80... | collective-permute-start | bytes 983048 | tf_op jit(solution)/shard_map/ppermute | solution.py:473
  41.2 15.0 %collective-permute-start.8 = (bf16[10,16,1024]{2,1,0:T(8,128)(2,1)S(1)}, bf16[10,16,1024]{2,1,0:T(8,128)(2,1)S(1)}, u32[]{:S(2)}, u32[]{:S(2)}) collective-permute-start(bf16[10,16,1024]{2,1,0:T(8,128)(2,1)S(1)} %get-tuple-element.49), channel_id=1, source_target_pairs={{0,24},{8,0},{16,8},{24,16},{32,56},{40,32},{48,40},{56,48},{64,88... | collective-permute-start | bytes 983048 | tf_op jit(solution)/shard_map/ppermute | solution.py:473
  43.3 12.9 %collective-permute-start.13 = (bf16[6,16,1024]{2,1,0:T(8,128)(2,1)S(1)}, bf16[6,16,1024]{2,1,0:T(8,128)(2,1)S(1)}, u32[]{:S(2)}, u32[]{:S(2)}) collective-permute-start(bf16[6,16,1024]{2,1,0:T(8,128)(2,1)S(1)} %get-tuple-element.53), channel_id=1, source_target_pairs={{0,8},{8,16},{16,24},{24,0},{32,40},{40,48},{48,56},{56,32},{64,72... | collective-permute-start | bytes 589832 | tf_op jit(solution)/shard_map/ppermute | solution.py:473
  44.3 11.9 %collective-permute-start.14 = (bf16[6,16,1024]{2,1,0:T(8,128)(2,1)S(1)}, bf16[6,16,1024]{2,1,0:T(8,128)(2,1)S(1)}, u32[]{:S(2)}, u32[]{:S(2)}) collective-permute-start(bf16[6,16,1024]{2,1,0:T(8,128)(2,1)S(1)} %get-tuple-element.54), channel_id=1, source_target_pairs={{0,16},{8,24},{16,0},{24,8},{32,48},{40,56},{48,32},{56,40},{64,80... | collective-permute-start | bytes 589832 | tf_op jit(solution)/shard_map/ppermute | solution.py:473
  47.8 12.7 %collective-permute-start.15 = (bf16[6,16,1024]{2,1,0:T(8,128)(2,1)S(1)}, bf16[6,16,1024]{2,1,0:T(8,128)(2,1)S(1)}, u32[]{:S(2)}, u32[]{:S(2)}) collective-permute-start(bf16[6,16,1024]{2,1,0:T(8,128)(2,1)S(1)} %get-tuple-element.55), channel_id=1, source_target_pairs={{0,24},{8,0},{16,8},{24,16},{32,56},{40,32},{48,40},{56,48},{64,88... | collective-permute-start | bytes 589832 | tf_op jit(solution)/shard_map/ppermute | solution.py:473
  88.6 12.9 %collective-permute-start.30 = (bf16[5,16,1024]{2,1,0:T(8,128)(2,1)S(1)}, bf16[5,16,1024]{2,1,0:T(8,128)(2,1)S(1)}, u32[]{:S(2)}, u32[]{:S(2)}) collective-permute-start(bf16[5,16,1024]{2,1,0:T(8,128)(2,1)S(1)} %get-tuple-element.82), channel_id=1, source_target_pairs={{0,32},{8,40},{16,48},{24,56},{32,64},{40,72},{48,80},{56,88},{64,... | collective-permute-start | bytes 491528 | tf_op jit(solution)/shard_map/ppermute | solution.py:473
  88.7 12.8 %collective-permute-start.31 = (bf16[5,16,1024]{2,1,0:T(8,128)(2,1)S(1)}, bf16[5,16,1024]{2,1,0:T(8,128)(2,1)S(1)}, u32[]{:S(2)}, u32[]{:S(2)}) collective-permute-start(bf16[5,16,1024]{2,1,0:T(8,128)(2,1)S(1)} %get-tuple-element.83), channel_id=1, source_target_pairs={{0,224},{8,232},{16,240},{24,248},{32,0},{40,8},{48,16},{56,24},{6... | collective-permute-start | bytes 491528 | tf_op jit(solution)/shard_map/ppermute | solution.py:473
  102.5 12.2 %collective-permute-start.32 = (bf16[10,16,1024]{2,1,0:T(8,128)(2,1)S(1)}, bf16[10,16,1024]{2,1,0:T(8,128)(2,1)S(1)}, u32[]{:S(2)}, u32[]{:S(2)}) collective-permute-start(bf16[10,16,1024]{2,1,0:T(8,128)(2,1)S(1)} %get-tuple-element.84), channel_id=1, source_target_pairs={{0,32},{8,40},{16,48},{24,56},{32,64},{40,72},{48,80},{56,88},{64,... | collective-permute-start | bytes 983048 | tf_op jit(solution)/shard_map/ppermute | solution.py:473
  102.6 12.1 %collective-permute-start.33 = (bf16[10,16,1024]{2,1,0:T(8,128)(2,1)S(1)}, bf16[10,16,1024]{2,1,0:T(8,128)(2,1)S(1)}, u32[]{:S(2)}, u32[]{:S(2)}) collective-permute-start(bf16[10,16,1024]{2,1,0:T(8,128)(2,1)S(1)} %get-tuple-element.85), channel_id=1, source_target_pairs={{0,224},{8,232},{16,240},{24,248},{32,0},{40,8},{48,16},{56,24},{6... | collective-permute-start | bytes 983048 | tf_op jit(solution)/shard_map/ppermute | solution.py:473
  115.7 14.2 %collective-permute-start.34 = (bf16[10,16,1024]{2,1,0:T(8,128)(2,1)S(1)}, bf16[10,16,1024]{2,1,0:T(8,128)(2,1)S(1)}, u32[]{:S(2)}, u32[]{:S(2)}) collective-permute-start(bf16[10,16,1024]{2,1,0:T(8,128)(2,1)S(1)} %get-tuple-element.86), channel_id=1, source_target_pairs={{0,32},{8,40},{16,48},{24,56},{32,64},{40,72},{48,80},{56,88},{64,... | collective-permute-start | bytes 983048 | tf_op jit(solution)/shard_map/ppermute | solution.py:473
  115.8 14.1 %collective-permute-start.35 = (bf16[10,16,1024]{2,1,0:T(8,128)(2,1)S(1)}, bf16[10,16,1024]{2,1,0:T(8,128)(2,1)S(1)}, u32[]{:S(2)}, u32[]{:S(2)}) collective-permute-start(bf16[10,16,1024]{2,1,0:T(8,128)(2,1)S(1)} %get-tuple-element.87), channel_id=1, source_target_pairs={{0,224},{8,232},{16,240},{24,248},{32,0},{40,8},{48,16},{56,24},{6... | collective-permute-start | bytes 983048 | tf_op jit(solution)/shard_map/ppermute | solution.py:473
  120.6 7.3 %collective-permute-start.19 = (bf16[6,16,1024]{2,1,0:T(8,128)(2,1)S(1)}, bf16[6,16,1024]{2,1,0:T(8,128)(2,1)S(1)}, u32[]{:S(2)}, u32[]{:S(2)}) collective-permute-start(bf16[6,16,1024]{2,1,0:T(8,128)(2,1)S(1)} %get-tuple-element.68), channel_id=1, source_target_pairs={{0,16},{8,24},{16,0},{24,8},{32,48},{40,56},{48,32},{56,40},{64,80... | collective-permute-start | bytes 589832 | tf_op jit(solution)/shard_map/ppermute | solution.py:473
  121.5 8.4 %collective-permute-start.20 = (bf16[6,16,1024]{2,1,0:T(8,128)(2,1)S(1)}, bf16[6,16,1024]{2,1,0:T(8,128)(2,1)S(1)}, u32[]{:S(2)}, u32[]{:S(2)}) collective-permute-start(bf16[6,16,1024]{2,1,0:T(8,128)(2,1)S(1)} %get-tuple-element.69), channel_id=1, source_target_pairs={{0,8},{8,16},{16,24},{24,0},{32,40},{40,48},{48,56},{56,32},{64,72... | collective-permute-start | bytes 589832 | tf_op jit(solution)/shard_map/ppermute | solution.py:473
  130.8 8.4 %collective-permute-start.36 = (bf16[10,16,1024]{2,1,0:T(8,128)(2,1)S(1)}, bf16[10,16,1024]{2,1,0:T(8,128)(2,1)S(1)}, u32[]{:S(2)}, u32[]{:S(2)}) collective-permute-start(bf16[10,16,1024]{2,1,0:T(8,128)(2,1)S(1)} %get-tuple-element.88), channel_id=1, source_target_pairs={{0,32},{8,40},{16,48},{24,56},{32,64},{40,72},{48,80},{56,88},{64,... | collective-permute-start | bytes 983048 | tf_op jit(solution)/shard_map/ppermute | solution.py:473
  130.9 8.3 %collective-permute-start.37 = (bf16[10,16,1024]{2,1,0:T(8,128)(2,1)S(1)}, bf16[10,16,1024]{2,1,0:T(8,128)(2,1)S(1)}, u32[]{:S(2)}, u32[]{:S(2)}) collective-permute-start(bf16[10,16,1024]{2,1,0:T(8,128)(2,1)S(1)} %get-tuple-element.89), channel_id=1, source_target_pairs={{0,224},{8,232},{16,240},{24,248},{32,0},{40,8},{48,16},{56,24},{6... | collective-permute-start | bytes 983048 | tf_op jit(solution)/shard_map/ppermute | solution.py:473
  (14 other events, 79.7 us)
